TPU v7x, 32 devices: a whole 2x2x4 slice. The times are simulated.
32 devices in a mesh: groups: 2 (over y), ep: 16 (over z, x, core).
Axes of the slice: x: 2, y: 2, z: 4, core: 2. Of those that a mesh axis runs over, the one named last changes fastest.
Arguments:
- queries: bfloat16 [32, 64, 512], P(('groups', 'ep')), parts along dimension 0, may hold values from -8 to 8
- key_cache: bfloat16 [32, 2, 512, 128], P(('groups', 'ep')), parts along dimension 0, may hold values from -6 to 6
- value_cache: bfloat16 [32, 2, 512, 128], P(('groups', 'ep')), parts along dimension 0, may hold values from -6 to 6
- key_block: bfloat16 [32, 64, 128], P(('groups', 'ep')), parts along dimension 0, may hold values from -8 to 8
- value_block: bfloat16 [32, 64, 128], P(('groups', 'ep')), parts along dimension 0, may hold values from -6 to 6
- cache_length_list: int32 [16], P('groups'), parts along dimension 0, may hold values from 0 to 512, as said below
- residual: bfloat16 [512, 2048], P(('groups', 'ep')), parts along dimension 0, may hold values from -6 to 6
- output_weight: bfloat16 [16, 512, 2048], P('ep'), may hold values from -3 to 3, as said below
- norm_gain: float32 [2048], replicated, may hold values from 0.1 to 1.9
- routes: int32 [512, 8], P(('groups', 'ep')), parts along dimension 0, may hold values from 0 to 15, all different within a row; in each aligned block of 16 rows (0 to 15, 16 to 31, ...) at most 16 rows name the same one
- route_logits: float32 [512, 8], P(('groups', 'ep')), parts along dimension 0, may hold values from -8 to 8
- w_gate: bfloat16 [16, 2048, 768], P('ep'), may hold values from -0.125 to 0.125
- w_up: bfloat16 [16, 2048, 768], P('ep'), may hold values from -0.125 to 0.125
- w_down: bfloat16 [16, 768, 2048], P('ep'), may hold values from -0.21875 to 0.21875
Outputs:
- attended: bfloat16 [512, 2048], P(('groups', 'ep')), parts along dimension 0
- expert_out: bfloat16 [512, 2048], P(('groups', 'ep')), parts along dimension 0
There are 2 independent parts, one for each index of `groups`. A program takes and returns all parts, laid end to end along the dimension named above; an argument that names none is the same for every part. Nothing has to cross between parts.
Inputs may be any that keep to these rules, and one draw needn't show every extreme that they name: `cache_length_list`: multiples of 32; some sequence has exactly 512 in every draw. `output_weight`: entries p and q along the first dimension are equal where p - q is a multiple of 4. `routes`: each row names 8 different experts; at most 16 rows of one device name one expert, a bound that some block reaches.
All inputs are finite; a program needn't handle non-finite values.
Results may differ from a plain program's by a relative error of at most 0.0079.
Values may be sent and summed in bfloat16 or wider, within the bound.
No kernel may reach another device: no remote copies, remote signals or barrier semaphores. Data moves between devices by JAX's collectives and lax.ppermute only.
A program may use at most 64 MiB of HBM per device.

v0:
```python
import functools
import math

import jax
import jax.numpy as jnp
from jax import lax
from jax.experimental import pallas as pl
from jax.experimental.pallas import tpu as pltpu
from jax.sharding import PartitionSpec as P


MODEL_WIDTH = 2048
QUERY_HEADS = 16
KEY_VALUE_HEADS = 4
HEAD_SIZE = 128


ROUTE_SCALE = 2.5
EPSILON = 1e-06
LANES = 128
WIDE = MODEL_WIDTH + LANES
CHUNK = 256


def exchanged(block, mask):
    count = lax.axis_size("ep")
    return lax.ppermute(block, "ep", [(index, index ^ mask) for index in range(count)])


def attend_kernel(
    lens_hbm, q_hbm, kc_hbm, vc_hbm, kb_hbm, vb_hbm, res_hbm, routes_hbm, logits_hbm, w_hbm,
    sent, kept,
    lens, q, kc, vc, kb, vb, res, routes, logits, w, attn, sems,
):
    pairs = (
        (lens_hbm, lens), (q_hbm, q), (kb_hbm, kb), (kc_hbm, kc), (vb_hbm, vb), (vc_hbm, vc),
        (routes_hbm, routes), (logits_hbm, logits), (res_hbm, res), (w_hbm, w),
    )
    copies = [pltpu.make_async_copy(a, b, sems.at[i]) for i, (a, b) in enumerate(pairs)]
    for copy in copies:
        copy.start()
    worker = lax.axis_index("ep")
    shard = lax.rem(worker, KEY_VALUE_HEADS)
    group = lax.div(worker, KEY_VALUE_HEADS)
    seqs = kc.shape[1]
    block = q.shape[1] // seqs
    heads = q.shape[2] // HEAD_SIZE
    rows = res.shape[0]
    scale = 1.0 / math.sqrt(HEAD_SIZE)
    nt = (((1,), (1,)), ((), ()))
    for copy in copies[:6]:
        copy.wait()
    for t in range(seqs):
        live = lens[group * seqs + t]
        part = slice(t * block, (t + 1) * block)
        queries = jnp.concatenate(
            [q[0, part, g * HEAD_SIZE : (g + 1) * HEAD_SIZE] for g in range(heads)], 0
        )
        cache = lax.dot_general(queries, kc[0, t], nt, preferred_element_type=jnp.float32) * scale
        fresh = lax.dot_general(queries, kb[0, part], nt, preferred_element_type=jnp.float32) * scale
        position = lax.broadcasted_iota(jnp.int32, cache.shape, 1)
        cache = jnp.where(position < live, cache, -1e30)
        largest = jnp.maximum(
            jnp.max(cache, -1, keepdims=True), jnp.max(fresh, -1, keepdims=True)
        )
        cache = jnp.exp(cache - largest)
        fresh = jnp.exp(fresh - largest)
        total = jnp.sum(cache, -1, keepdims=True) + jnp.sum(fresh, -1, keepdims=True)
        share = 1.0 / total
        mixed = jnp.dot(
            (cache * share).astype(jnp.bfloat16), vc[0, t], preferred_element_type=jnp.float32
        ) + jnp.dot(
            (fresh * share).astype(jnp.bfloat16), vb[0, part], preferred_element_type=jnp.float32
        )
        for g in range(heads):
            attn[part, g * HEAD_SIZE : (g + 1) * HEAD_SIZE] = mixed[
                g * block : (g + 1) * block
            ].astype(jnp.bfloat16)
    for copy in copies[6:9]:
        copy.wait()
    experts = lax.axis_size("ep")
    sig = 1.0 / (1.0 + jnp.exp(-logits[...]))
    weights = ROUTE_SCALE * sig / jnp.sum(sig, 0, keepdims=True)
    line = lax.broadcasted_iota(jnp.int32, (LANES, rows), 0)
    name = jnp.where(line < experts, line, line - experts)
    table = jnp.zeros((LANES, rows), jnp.float32)
    for k in range(routes.shape[0]):
        table = table + jnp.where(routes[k : k + 1, :] == name, weights[k : k + 1, :], 0.0)
    high = table.astype(jnp.bfloat16).astype(jnp.float32)
    table = jnp.where(line < experts, high, table - high).astype(jnp.bfloat16)
    row = lax.broadcasted_iota(jnp.int32, (rows, rows), 0)
    unit = jnp.where(row == lax.broadcasted_iota(jnp.int32, (rows, rows), 1), 1.0, 0.0)
    kept[:rows, MODEL_WIDTH:] = lax.dot_general(
        unit.astype(jnp.bfloat16), table, nt, preferred_element_type=jnp.float32
    )
    kept[rows:, MODEL_WIDTH:] = jnp.zeros((rows, LANES), jnp.float32)
    sent[:, MODEL_WIDTH:] = jnp.zeros((2 * rows, LANES), jnp.bfloat16)
    copies[9].wait()
    picked = [
        attn[pl.ds(pl.multiple_of((shard ^ mask) * rows, rows), rows), :] for mask in (1, 3, 0, 2)
    ]
    picked = jnp.concatenate(picked, 0)
    for n in range(0, MODEL_WIDTH, 2 * CHUNK):
        cols = slice(n, n + 2 * CHUNK)
        out = jnp.dot(picked, w[0, :, cols], preferred_element_type=jnp.float32)
        sent[:, cols] = out[: 2 * rows].astype(jnp.bfloat16)
        kept[:rows, cols] = out[2 * rows : 3 * rows] + res[:, cols].astype(jnp.float32)
        kept[rows:, cols] = out[3 * rows :]


def norm_kernel(block, kept, core, chip, gain, *outs):
    packet = outs[-1]
    rows = packet.shape[0]
    here = slice(block * rows, (block + 1) * rows)
    hidden = kept[here, :] + core[here, :].astype(jnp.float32) + chip[...].astype(jnp.float32)
    table = hidden[:, MODEL_WIDTH:]
    hidden = hidden[:, :MODEL_WIDTH]
    if block == 0:
        outs[0][...] = hidden.astype(jnp.bfloat16)
    mean = jnp.sum(hidden * hidden, -1, keepdims=True) * (1.0 / MODEL_WIDTH)
    packet[:, :MODEL_WIDTH] = (hidden * lax.rsqrt(mean + EPSILON) * gain[...]).astype(jnp.bfloat16)
    packet[:, MODEL_WIDTH:] = table.astype(jnp.bfloat16)


def expert_kernel(mine, other, w_gate, w_up, w_down, keep, send, x, act):
    half = mine.shape[0]
    experts = lax.axis_size("ep")
    own = lax.axis_index("ep")
    x[:half, :] = mine[...]
    x[half:, :] = other[...]
    lane = lax.broadcasted_iota(jnp.int32, (2 * half, LANES), 1)
    codes = x[:, MODEL_WIDTH:].astype(jnp.float32)
    chosen = (lane == own) | (lane == own + experts)
    weight = jnp.sum(jnp.where(chosen, codes, 0.0), 1, keepdims=True)
    rows = x[:, :MODEL_WIDTH]
    hidden_units = w_gate.shape[2]
    for n in range(0, hidden_units, CHUNK):
        cols = slice(n, n + CHUNK)
        gate = jnp.dot(rows, w_gate[0, :, cols], preferred_element_type=jnp.float32)
        up = jnp.dot(rows, w_up[0, :, cols], preferred_element_type=jnp.float32)
        act[:, cols] = (gate / (1.0 + jnp.exp(-gate)) * up).astype(jnp.bfloat16)
    for n in range(0, MODEL_WIDTH, CHUNK):
        cols = slice(n, n + CHUNK)
        out = jnp.dot(act[...], w_down[0, :, cols], preferred_element_type=jnp.float32) * weight
        keep[:, cols] = out[:half]
        send[:, cols] = out[half:].astype(jnp.bfloat16)


def every_row(
    queries, key_cache, value_cache, key_block, value_block, cache_length_list, residual,
    output_weight, norm_gain, routes, route_logits, w_gate, w_up, w_down,
):
    rows = residual.shape[0]
    owners = lax.axis_size("ep")
    anywhere = pl.BlockSpec(memory_space=pl.ANY)
    whole = pl.BlockSpec(memory_space=pltpu.VMEM)
    operands = (
        cache_length_list, queries, key_cache, value_cache, key_block, value_block, residual,
        routes.T, route_logits.T, output_weight,
    )
    operands = tuple(pltpu.with_memory_space_constraint(a, pltpu.HBM) for a in operands)
    scratch = [pltpu.SMEM(cache_length_list.shape, jnp.int32)]
    scratch += [pltpu.VMEM(a.shape, a.dtype) for a in operands[1:]]
    scratch += [
        pltpu.VMEM((queries.shape[1], queries.shape[2]), jnp.bfloat16),
        pltpu.SemaphoreType.DMA((len(operands),)),
    ]
    sent, kept = pl.pallas_call(
        attend_kernel,
        out_shape=(
            jax.ShapeDtypeStruct((2 * rows, WIDE), jnp.bfloat16),
            jax.ShapeDtypeStruct((2 * rows, WIDE), jnp.float32),
        ),
        in_specs=[anywhere] * len(operands),
        out_specs=(whole, whole),
        scratch_shapes=scratch,
        compiler_params=pltpu.CompilerParams(vmem_limit_bytes=12 << 20),
        cost_estimate=pl.CostEstimate(flops=1 << 30, bytes_accessed=1 << 23, transcendentals=1 << 18),
        name="attend",
    )(*operands)
    sent, w_gate, w_up, w_down = lax.optimization_barrier((sent, w_gate, w_up, w_down))
    core = exchanged(sent, 1)
    sums = (kept + core.astype(jnp.float32)).astype(jnp.bfloat16)
    chip_own = exchanged(sums[rows:], 2)
    chip_pair = exchanged(sums[:rows], 2)

    def normed(block, chip):
        outs = (jax.ShapeDtypeStruct((rows, MODEL_WIDTH), jnp.bfloat16),) * (block == 0)
        outs += (jax.ShapeDtypeStruct((rows, WIDE), jnp.bfloat16),)
        return pl.pallas_call(
            functools.partial(norm_kernel, block),
            out_shape=outs,
            in_specs=[whole] * 4,
            out_specs=(whole,) * len(outs),
            compiler_params=pltpu.CompilerParams(vmem_limit_bytes=6 << 20),
            cost_estimate=pl.CostEstimate(
                flops=1 << 34, bytes_accessed=1 << 20, transcendentals=1 << 10
            ),
            name="norm",
        )(kept, core, chip, norm_gain[None])

    attended, own = normed(0, chip_own)
    far = exchanged(own, 8)
    (pair,) = normed(1, chip_pair)
    packet = jnp.concatenate([own, pair], 0)
    across = exchanged(packet, 12)
    near = exchanged(packet, 4)
    passed = exchanged(far, 2)
    mine = jnp.concatenate([packet, near, far, passed, across], 0)
    other = exchanged(mine, 1)
    half = mine.shape[0]
    keep, send = pl.pallas_call(
        expert_kernel,
        out_shape=(
            jax.ShapeDtypeStruct((half, MODEL_WIDTH), jnp.float32),
            jax.ShapeDtypeStruct((half, MODEL_WIDTH), jnp.bfloat16),
        ),
        in_specs=[whole] * 5,
        out_specs=(whole, whole),
        scratch_shapes=[
            pltpu.VMEM((2 * half, WIDE), jnp.bfloat16),
            pltpu.VMEM((2 * half, w_gate.shape[2]), jnp.bfloat16),
        ],
        compiler_params=pltpu.CompilerParams(vmem_limit_bytes=12 << 20),
        cost_estimate=pl.CostEstimate(flops=1 << 31, bytes_accessed=1 << 23, transcendentals=1 << 18),
        name="expert",
    )(mine, other, w_gate, w_up, w_down)
    total = keep + exchanged(send, 1).astype(jnp.float32)
    total = total.reshape(owners // 4, 2, rows, MODEL_WIDTH)
    to_chip = total[:, 1].astype(jnp.bfloat16)
    got_far = exchanged(to_chip[2:], 2)
    got_near = exchanged(to_chip[:2], 2)
    far_sums = (total[2:, 0] + got_far.astype(jnp.float32)).astype(jnp.bfloat16)
    across = exchanged(far_sums[1], 12)
    far = exchanged(far_sums[0], 8)
    near_sum = (total[1, 0] + got_near[1].astype(jnp.float32)).astype(jnp.bfloat16)
    near = exchanged(near_sum, 4)
    summed = total[0, 0] + got_near[0].astype(jnp.float32) + near.astype(jnp.float32)
    summed = summed + far.astype(jnp.float32) + across.astype(jnp.float32)
    return (attended, summed.astype(jnp.bfloat16))


def swapped(block, axis, distance):
    count = lax.axis_size(axis)
    route = []
    for low in range(count):
        high = low | 1 << distance
        if high != low and high < count:
            route += [(low, high), (high, low)]
    return lax.ppermute(block, axis, route)


def routed_rows(
    queries,
    key_cache,
    value_cache,
    key_block,
    value_block,
    cache_length_list,
    residual,
    output_weight,
    norm_gain,
    routes,
    route_logits,
    w_gate,
    w_up,
    w_down,
):
    group_results = QUERY_HEADS // KEY_VALUE_HEADS
    shard_worker = lax.axis_index("ep")
    sequence_group_index = shard_worker // KEY_VALUE_HEADS
    head_shard_index = shard_worker % KEY_VALUE_HEADS
    seq_grp = key_cache.shape[1]
    cache_len = key_cache.shape[2]
    rows_per_group = queries.shape[1]
    block_len = rows_per_group // seq_grp
    live_lens = lax.dynamic_slice_in_dim(cache_length_list, sequence_group_index * seq_grp, seq_grp)
    heads_of_query = queries[0].reshape(seq_grp, block_len, group_results, HEAD_SIZE)
    keys_of_block = key_block[0].reshape(seq_grp, block_len, HEAD_SIZE)
    values_of_block = value_block[0].reshape(seq_grp, block_len, HEAD_SIZE)
    score_cache = jnp.einsum(
        "srgd,spd->sgrp", heads_of_query, key_cache[0], preferred_element_type=jnp.float32
    ) / math.sqrt(HEAD_SIZE)
    score_block = jnp.einsum(
        "srgd,spd->sgrp", heads_of_query, keys_of_block, preferred_element_type=jnp.float32
    ) / math.sqrt(HEAD_SIZE)
    position = jnp.arange(cache_len, dtype=jnp.int32)
    live_slots = position[None, :] < live_lens[:, None]
    score_cache = jnp.where(live_slots[:, None, None, :], score_cache, -1e30)
    largest = jnp.maximum(
        jnp.max(score_cache, -1, keepdims=True), jnp.max(score_block, -1, keepdims=True)
    )
    exp_cache = jnp.exp(score_cache - largest)
    exp_block = jnp.exp(score_block - largest)
    denominator = jnp.sum(exp_cache, -1, keepdims=True) + jnp.sum(exp_block, -1, keepdims=True)
    prob_cache = (exp_cache / denominator).astype(jnp.bfloat16)
    prob_block = (exp_block / denominator).astype(jnp.bfloat16)
    mixed_heads = jnp.einsum(
        "sgrp,spd->srgd", prob_cache, value_cache[0], preferred_element_type=jnp.float32
    )
    mixed_heads = mixed_heads + jnp.einsum(
        "sgrp,spd->srgd", prob_block, values_of_block, preferred_element_type=jnp.float32
    )
    attn_rows = mixed_heads.reshape(rows_per_group, group_results * HEAD_SIZE).astype(jnp.bfloat16)
    partial_value = jnp.dot(attn_rows, output_weight[0], preferred_element_type=jnp.float32)
    tree_levels = KEY_VALUE_HEADS.bit_length() - 1
    projected = partial_value
    for bit_pos in reversed(range(tree_levels)):
        half_rows = projected.shape[0] // 2
        low_half = projected[:half_rows]
        high_half = projected[half_rows:]
        upper_side = head_shard_index >> bit_pos & 1 == 1
        kept_rows = jnp.where(upper_side, high_half, low_half)
        sent_rows = jnp.where(upper_side, low_half, high_half)
        projected = kept_rows + swapped(sent_rows, "ep", bit_pos)
    hidden = residual.astype(jnp.float32) + projected
    attended = hidden.astype(jnp.bfloat16)
    normed = (
        hidden * lax.rsqrt(jnp.mean(hidden * hidden, -1, keepdims=True) + EPSILON) * norm_gain
    ).astype(jnp.bfloat16)
    sig_values = jax.nn.sigmoid(route_logits)
    route_weights = ROUTE_SCALE * sig_values / jnp.sum(sig_values, -1, keepdims=True)
    owners = lax.axis_size("ep")
    exp_dev = w_gate.shape[0]
    experts = owners * exp_dev
    row_count = residual.shape[0]
    top_k = routes.shape[1]
    capacity = max(2, 2 * row_count * top_k // experts)
    flat_ids = routes.reshape(-1)
    onehot = (flat_ids[:, None] == jnp.arange(experts, dtype=jnp.int32)[None, :]).astype(jnp.int32)
    slot_rank = jnp.sum(jnp.cumsum(onehot, 0) * onehot, 1) - 1
    target = flat_ids * capacity + slot_rank
    source_rows = jnp.repeat(normed, top_k, axis=0)
    outgoing = (
        jnp.zeros((experts * capacity, MODEL_WIDTH), jnp.bfloat16).at[target].set(source_rows)
    )
    outgoing = outgoing.reshape(owners, exp_dev, capacity, MODEL_WIDTH)
    arrived = lax.all_to_all(outgoing, "ep", split_axis=0, concat_axis=0, tiled=True)
    gate_part = jnp.einsum("nesd,edh->nesh", arrived, w_gate, preferred_element_type=jnp.float32)
    up_part = jnp.einsum("nesd,edh->nesh", arrived, w_up, preferred_element_type=jnp.float32)
    active = (jax.nn.silu(gate_part) * up_part).astype(jnp.bfloat16)
    result = jnp.einsum(
        "nesh,ehd->nesd", active, w_down, preferred_element_type=jnp.float32
    ).astype(jnp.bfloat16)
    returned = lax.all_to_all(result, "ep", split_axis=0, concat_axis=0, tiled=True)
    fetched = returned.reshape(experts * capacity, MODEL_WIDTH)[target].reshape(
        row_count, top_k, MODEL_WIDTH
    )
    weighted = jnp.sum(route_weights[:, :, None] * fetched.astype(jnp.float32), 1)
    expert_out = weighted.astype(jnp.bfloat16)
    return (attended, expert_out)


def on_device(*inputs):
    row_count, top_k = inputs[9].shape
    owners = lax.axis_size("ep")
    experts = owners * inputs[11].shape[0]
    capacity = max(2, 2 * row_count * top_k // experts)
    all_rows = row_count <= capacity and experts == owners == 4 * KEY_VALUE_HEADS
    if not all_rows:
        return routed_rows(*inputs)
    return every_row(*inputs)


def solution(mesh):
    return jax.shard_map(
        on_device,
        mesh=mesh,
        in_specs=(
            P(("groups", "ep"), None, None),
            P(("groups", "ep"), None, None, None),
            P(("groups", "ep"), None, None, None),
            P(("groups", "ep"), None, None),
            P(("groups", "ep"), None, None),
            P("groups"),
            P(("groups", "ep"), None),
            P("ep", None, None),
            P(),
            P(("groups", "ep"), None),
            P(("groups", "ep"), None),
            P("ep", None, None),
            P("ep", None, None),
            P("ep", None, None),
        ),
        out_specs=(P(("groups", "ep"), None), P(("groups", "ep"), None)),
        check_vma=False,
    )
```

profile of v0, /device:TPU:0, one launch (start us, length us, event | category | flops | bytes accessed | tf_op | source)
XLA Modules:
  0.0 50.1 jit_solution(1953555877275497901)
XLA Ops:
  0.6 2.9 %attend.1 = (bf16[32,2176]{1,0:T(8,128)(2,1)S(1)}, f32[32,2176]{1,0:T(8,128)S(1)}) custom-call(s32[8]{0:T(128)} %lens_hbm.1, bf16[1,64,512]{2,1,0:T(8,128)(2,1)} %q_hbm.1, bf16[1,2,512,128]{3,2,1,0:T(8,128)(2,1)} %kc_hbm.1, bf16[1,2,512,128]{3,2,1,0:T(8,128)(2,1)} %vc_hbm.1, bf16[1,64,128]{2,1,0:T(8,128)(2,1)} %kb_hbm.1, bf16[1,64,128]{2,1,0:T(8,128)(2,1)} %vb_hbm.1, ...), custom_call_target="tpu_custom_call" | custom-call | flops 1073741824 | bytes 8388608 | tf_op jit(solution)/shard_map/attend/pallas_call | solution.py:168
  3.5 0.6 %collective-permute-start = (bf16[32,2176]{1,0:T(8,128)(2,1)S(1)}, bf16[32,2176]{1,0:T(8,128)(2,1)S(1)}, u32[]{:S(2)}, u32[]{:S(2)}) collective-permute-start(bf16[32,2176]{1,0:T(8,128)(2,1)S(1)} %get-tuple-element.14), channel_id=1, source_target_pairs={{0,1},{1,0},{2,3},{3,2},{4,5},{5,4},{6,7},{7,6},{8,9},{9,8},{10,11... | collective-permute-start | bytes 417800 | tf_op jit(solution)/shard_map/ppermute | solution.py:27
  4.1 1.0 %collective-permute-done.core = bf16[32,2176]{1,0:T(8,128)(2,1)S(1)} collective-permute-done((bf16[32,2176]{1,0:T(8,128)(2,1)S(1)}, bf16[32,2176]{1,0:T(8,128)(2,1)S(1)}, u32[]{:S(2)}, u32[]{:S(2)}) %collective-permute-start) | collective-permute-done | bytes 139296 | tf_op jit(solution)/shard_map/ppermute | solution.py:27
  5.1 2.9 %collective-permute-start.1 = (bf16[16,2176]{1,0:T(8,128)(2,1)S(1)}, bf16[16,2176]{1,0:T(8,128)(2,1)S(1)}, u32[]{:S(2)}, u32[]{:S(2)}) collective-permute-start(bf16[16,2176]{1,0:T(8,128)(2,1)S(1)} %get-tuple-element.25), channel_id=1, source_target_pairs={{0,2},{1,3},{2,0},{3,1},{4,6},{5,7},{6,4},{7,5},{8,10},{9,11},{10,... | collective-permute-start | bytes 208904 | tf_op jit(solution)/shard_map/ppermute | solution.py:27
  8.0 0.1 collective-permute-start.2
  8.1 2.4 %collective-permute-done.1.chip = bf16[16,2176]{1,0:T(8,128)(2,1)S(1)} collective-permute-done((bf16[16,2176]{1,0:T(8,128)(2,1)S(1)}, bf16[16,2176]{1,0:T(8,128)(2,1)S(1)}, u32[]{:S(2)}, u32[]{:S(2)}) %collective-permute-start.1) | collective-permute-done | bytes 69664 | tf_op jit(solution)/shard_map/ppermute | solution.py:27
  10.5 0.7 %norm.2 = (bf16[16,2048]{1,0:T(8,128)(2,1)}, bf16[16,2176]{1,0:T(8,128)(2,1)S(1)}) custom-call(f32[32,2176]{1,0:T(8,128)S(1)} %get-tuple-element.12.kept, bf16[32,2176]{1,0:T(8,128)(2,1)S(1)} %collective-permute-done.core, bf16[16,2176]{1,0:T(8,128)(2,1)S(1)} %collective-permute-done.1.chip, f32[1,2048]{1,0:T(1,128)S(1)} %bitcast.46), custom_call_target="tpu_custom_call" | custom-call | flops 17179869184 | bytes 1048576 | tf_op jit(solution)/shard_map/norm/pallas_call | solution.py:190
  11.2 3.3 %collective-permute-start.4 = (bf16[16,2176]{1,0:T(8,128)(2,1)S(1)}, bf16[16,2176]{1,0:T(8,128)(2,1)S(1)}, u32[]{:S(2)}, u32[]{:S(2)}) collective-permute-start(bf16[16,2176]{1,0:T(8,128)(2,1)S(1)} %get-tuple-element.16), channel_id=1, source_target_pairs={{0,8},{1,9},{2,10},{3,11},{4,12},{5,13},{6,14},{7,15},{8,0},{9,1},... | collective-permute-start | bytes 208904 | tf_op jit(solution)/shard_map/ppermute | solution.py:27
  14.5 0.0 collective-permute-done.2.chip
  14.5 0.1 norm.3
  14.6 1.5 %collective-permute-start.6 = (bf16[32,2176]{1,0:T(8,128)(2,1)S(1)}, bf16[32,2176]{1,0:T(8,128)(2,1)S(1)}, u32[]{:S(2)}, u32[]{:S(2)}) collective-permute-start(bf16[32,2176]{1,0:T(8,128)(2,1)S(1)} %pad_maximum_fusion), channel_id=1, source_target_pairs={{0,12},{1,13},{2,14},{3,15},{4,8},{5,9},{6,10},{7,11},{8,4},{9,5},... | collective-permute-start | bytes 417800 | tf_op jit(solution)/shard_map/ppermute | solution.py:27
  16.2 0.2 collective-permute-start.3
  16.4 0.7 %collective-permute-done.4 = bf16[16,2176]{1,0:T(8,128)(2,1)S(1)} collective-permute-done((bf16[16,2176]{1,0:T(8,128)(2,1)S(1)}, bf16[16,2176]{1,0:T(8,128)(2,1)S(1)}, u32[]{:S(2)}, u32[]{:S(2)}) %collective-permute-start.4) | collective-permute-done | bytes 69664 | tf_op jit(solution)/shard_map/ppermute | solution.py:27
  17.1 4.8 %collective-permute-start.5 = (bf16[16,2176]{1,0:T(8,128)(2,1)S(1)}, bf16[16,2176]{1,0:T(8,128)(2,1)S(1)}, u32[]{:S(2)}, u32[]{:S(2)}) collective-permute-start(bf16[16,2176]{1,0:T(8,128)(2,1)S(1)} %collective-permute-done.4), channel_id=1, source_target_pairs={{0,2},{1,3},{2,0},{3,1},{4,6},{5,7},{6,4},{7,5},{8,10},{9,11},{10,... | collective-permute-start | bytes 208904 | tf_op jit(solution)/shard_map/ppermute | solution.py:27
  21.8 1.7 %collective-permute-done.3 = bf16[32,2176]{1,0:T(8,128)(2,1)S(1)} collective-permute-done((bf16[32,2176]{1,0:T(8,128)(2,1)S(1)}, bf16[32,2176]{1,0:T(8,128)(2,1)S(1)}, u32[]{:S(2)}, u32[]{:S(2)}) %collective-permute-start.3) | collective-permute-done | bytes 139296 | tf_op jit(solution)/shard_map/ppermute | solution.py:27
  23.5 0.6 %collective-permute-done.5 = bf16[16,2176]{1,0:T(8,128)(2,1)S(1)} collective-permute-done((bf16[16,2176]{1,0:T(8,128)(2,1)S(1)}, bf16[16,2176]{1,0:T(8,128)(2,1)S(1)}, u32[]{:S(2)}, u32[]{:S(2)}) %collective-permute-start.5) | collective-permute-done | bytes 69664 | tf_op jit(solution)/shard_map/ppermute | solution.py:27
  24.2 0.1 collective-permute-start.7
  24.2 1.9 %collective-permute-done.7.other = bf16[128,2176]{1,0:T(8,128)(2,1)S(1)} collective-permute-done((bf16[128,2176]{1,0:T(8,128)(2,1)S(1)}, bf16[128,2176]{1,0:T(8,128)(2,1)S(1)}, u32[]{:S(2)}, u32[]{:S(2)}) %collective-permute-start.7) | collective-permute-done | bytes 557088 | tf_op jit(solution)/shard_map/ppermute | solution.py:27
  26.2 2.6 %expert.1 = (f32[128,2048]{1,0:T(8,128)S(1)}, bf16[128,2048]{1,0:T(8,128)(2,1)S(1)}) custom-call(bf16[128,2176]{1,0:T(8,128)(2,1)S(1)} %constant_dynamic-update-slice_fusion.mine, bf16[128,2176]{1,0:T(8,128)(2,1)S(1)} %collective-permute-done.7.other, bf16[1,2048,768]{2,1,0:T(8,128)(2,1)S(1)} %copy-done, bf16[1,2048,768]{2,1,0:T(8,128)(2,1)S(1)} %copy-done.1, ...), custom_call_target="tpu_custom_call" | custom-call | flops 2147483648 | bytes 8388608 | tf_op jit(solution)/shard_map/expert/pallas_call | solution.py:212
  28.8 0.2 collective-permute-start.8
  29.0 1.8 %collective-permute-done.8 = bf16[128,2048]{1,0:T(8,128)(2,1)S(1)} collective-permute-done((bf16[128,2048]{1,0:T(8,128)(2,1)S(1)}, bf16[128,2048]{1,0:T(8,128)(2,1)S(1)}, u32[]{:S(2)}, u32[]{:S(2)}) %collective-permute-start.8) | collective-permute-done | bytes 524320 | tf_op jit(solution)/shard_map/ppermute | solution.py:27
  30.8 0.1 convert_add_fusion
  30.9 2.1 %collective-permute-start.9 = (bf16[2,16,2048]{2,1,0:T(8,128)(2,1)S(1)}, bf16[2,16,2048]{2,1,0:T(8,128)(2,1)S(1)}, u32[]{:S(2)}, u32[]{:S(2)}) collective-permute-start(bf16[2,16,2048]{2,1,0:T(8,128)(2,1)S(1)} %get-tuple-element.22), channel_id=1, source_target_pairs={{0,2},{1,3},{2,0},{3,1},{4,6},{5,7},{6,4},{7,5},{8,10},{9,11},{10,... | collective-permute-start | bytes 393224 | tf_op jit(solution)/shard_map/ppermute | solution.py:27
  33.0 0.1 collective-permute-start.11
  33.1 4.3 %collective-permute-done.9 = bf16[2,16,2048]{2,1,0:T(8,128)(2,1)S(1)} collective-permute-done((bf16[2,16,2048]{2,1,0:T(8,128)(2,1)S(1)}, bf16[2,16,2048]{2,1,0:T(8,128)(2,1)S(1)}, u32[]{:S(2)}, u32[]{:S(2)}) %collective-permute-start.9) | collective-permute-done | bytes 131104 | tf_op jit(solution)/shard_map/ppermute | solution.py:27
  37.4 2.2 %collective-permute-start.10 = (bf16[16,2048]{1,0:T(8,128)(2,1)S(1)}, bf16[16,2048]{1,0:T(8,128)(2,1)S(1)}, u32[]{:S(2)}, u32[]{:S(2)}) collective-permute-start(bf16[16,2048]{1,0:T(8,128)(2,1)S(1)} %fusion.3), channel_id=1, source_target_pairs={{0,4},{1,5},{2,6},{3,7},{4,0},{5,1},{6,2},{7,3},{8,12},{9,13},{10,... | collective-permute-start | bytes 196616 | tf_op jit(solution)/shard_map/ppermute | solution.py:27
  39.6 0.0 collective-permute-done.11
  39.7 3.6 %collective-permute-start.12 = (bf16[16,2048]{1,0:T(8,128)(2,1)S(1)}, bf16[16,2048]{1,0:T(8,128)(2,1)S(1)}, u32[]{:S(2)}, u32[]{:S(2)}) collective-permute-start(bf16[16,2048]{1,0:T(8,128)(2,1)S(1)} %get-tuple-element.26), channel_id=1, source_target_pairs={{0,8},{1,9},{2,10},{3,11},{4,12},{5,13},{6,14},{7,15},{8,0},{9,1},... | collective-permute-start | bytes 196616 | tf_op jit(solution)/shard_map/ppermute | solution.py:27
  43.3 1.4 %collective-permute-start.13 = (bf16[16,2048]{1,0:T(8,128)(2,1)S(1)}, bf16[16,2048]{1,0:T(8,128)(2,1)S(1)}, u32[]{:S(2)}, u32[]{:S(2)}) collective-permute-start(bf16[16,2048]{1,0:T(8,128)(2,1)S(1)} %get-tuple-element.27), channel_id=1, source_target_pairs={{0,12},{1,13},{2,14},{3,15},{4,8},{5,9},{6,10},{7,11},{8,4},{9,5},... | collective-permute-start | bytes 196616 | tf_op jit(solution)/shard_map/ppermute | solution.py:27
  44.7 3.5 %collective-permute-done.12 = bf16[16,2048]{1,0:T(8,128)(2,1)S(1)} collective-permute-done((bf16[16,2048]{1,0:T(8,128)(2,1)S(1)}, bf16[16,2048]{1,0:T(8,128)(2,1)S(1)}, u32[]{:S(2)}, u32[]{:S(2)}) %collective-permute-start.12) | collective-permute-done | bytes 65568 | tf_op jit(solution)/shard_map/ppermute | solution.py:27
  48.1 1.3 %collective-permute-done.13 = bf16[16,2048]{1,0:T(8,128)(2,1)S(1)} collective-permute-done((bf16[16,2048]{1,0:T(8,128)(2,1)S(1)}, bf16[16,2048]{1,0:T(8,128)(2,1)S(1)}, u32[]{:S(2)}, u32[]{:S(2)}) %collective-permute-start.13) | collective-permute-done | bytes 65568 | tf_op jit(solution)/shard_map/ppermute | solution.py:27
  49.4 0.7 %fusion.8 = bf16[16,2048]{1,0:T(8,128)(2,1)} fusion(f32[4,2,16,2048]{3,2,1,0:T(8,128)S(1)} %bitcast.51, bf16[16,2048]{1,0:T(8,128)(2,1)S(1)} %collective-permute-done.13, bf16[16,2048]{1,0:T(8,128)(2,1)S(1)} %collective-permute-done.12, bf16[16,2048]{1,0:T(8,128)(2,1)S(1)} %collective-permute-done.10, bf16[2,16,2048]{2,1,0:T(8,128)(2,1)S(1)} %collective-permute-done.9), kind=kLoop, calls=%fused_computation.17 | loop fusion | flops 294912 | bytes 458752 | tf_op jit(solution)/shard_map/convert_element_type | solution.py:240
  (23 shorter events, 0.2 us)
Async XLA Ops:
  0.6 9.9 %copy-start.3 = (f32[2048]{0:T(1024)S(1)}, f32[2048]{0:T(1024)}, u32[]{:S(2)}) copy-start(f32[2048]{0:T(1024)} %param.22) | copy-start | bytes 24580
  3.5 1.6 %collective-permute-start = (bf16[32,2176]{1,0:T(8,128)(2,1)S(1)}, bf16[32,2176]{1,0:T(8,128)(2,1)S(1)}, u32[]{:S(2)}, u32[]{:S(2)}) collective-permute-start(bf16[32,2176]{1,0:T(8,128)(2,1)S(1)} %get-tuple-element.14), channel_id=1, source_target_pairs={{0,1},{1,0},{2,3},{3,2},{4,5},{5,4},{6,7},{7,6},{8,9},{9,8},{10,11... | collective-permute-start | bytes 417800 | tf_op jit(solution)/shard_map/ppermute | solution.py:27
  5.1 5.4 %collective-permute-start.1 = (bf16[16,2176]{1,0:T(8,128)(2,1)S(1)}, bf16[16,2176]{1,0:T(8,128)(2,1)S(1)}, u32[]{:S(2)}, u32[]{:S(2)}) collective-permute-start(bf16[16,2176]{1,0:T(8,128)(2,1)S(1)} %get-tuple-element.25), channel_id=1, source_target_pairs={{0,2},{1,3},{2,0},{3,1},{4,6},{5,7},{6,4},{7,5},{8,10},{9,11},{10,... | collective-permute-start | bytes 208904 | tf_op jit(solution)/shard_map/ppermute | solution.py:27
  8.0 6.4 %collective-permute-start.2 = (bf16[16,2176]{1,0:T(8,128)(2,1)S(1)}, bf16[16,2176]{1,0:T(8,128)(2,1)S(1)}, u32[]{:S(2)}, u32[]{:S(2)}) collective-permute-start(bf16[16,2176]{1,0:T(8,128)(2,1)S(1)} %get-tuple-element.24), channel_id=1, source_target_pairs={{0,2},{1,3},{2,0},{3,1},{4,6},{5,7},{6,4},{7,5},{8,10},{9,11},{10,... | collective-permute-start | bytes 208904 | tf_op jit(solution)/shard_map/ppermute | solution.py:27
  11.2 5.9 %collective-permute-start.4 = (bf16[16,2176]{1,0:T(8,128)(2,1)S(1)}, bf16[16,2176]{1,0:T(8,128)(2,1)S(1)}, u32[]{:S(2)}, u32[]{:S(2)}) collective-permute-start(bf16[16,2176]{1,0:T(8,128)(2,1)S(1)} %get-tuple-element.16), channel_id=1, source_target_pairs={{0,8},{1,9},{2,10},{3,11},{4,12},{5,13},{6,14},{7,15},{8,0},{9,1},... | collective-permute-start | bytes 208904 | tf_op jit(solution)/shard_map/ppermute | solution.py:27
  14.5 11.7 %copy-start = (bf16[1,2048,768]{2,1,0:T(8,128)(2,1)S(1)}, bf16[1,2048,768]{2,1,0:T(8,128)(2,1)}, u32[]{:S(2)}) copy-start(bf16[1,2048,768]{2,1,0:T(8,128)(2,1)} %w_gate) | copy-start | bytes 9437188
  14.5 11.7 %copy-start.1 = (bf16[1,2048,768]{2,1,0:T(8,128)(2,1)S(1)}, bf16[1,2048,768]{2,1,0:T(8,128)(2,1)}, u32[]{:S(2)}) copy-start(bf16[1,2048,768]{2,1,0:T(8,128)(2,1)} %w_up) | copy-start | bytes 9437188
  14.5 11.7 %copy-start.2 = (bf16[1,768,2048]{2,1,0:T(8,128)(2,1)S(1)}, bf16[1,768,2048]{2,1,0:T(8,128)(2,1)}, u32[]{:S(2)}) copy-start(bf16[1,768,2048]{2,1,0:T(8,128)(2,1)} %w_down) | copy-start | bytes 9437188
  14.6 9.5 %collective-permute-start.6 = (bf16[32,2176]{1,0:T(8,128)(2,1)S(1)}, bf16[32,2176]{1,0:T(8,128)(2,1)S(1)}, u32[]{:S(2)}, u32[]{:S(2)}) collective-permute-start(bf16[32,2176]{1,0:T(8,128)(2,1)S(1)} %pad_maximum_fusion), channel_id=1, source_target_pairs={{0,12},{1,13},{2,14},{3,15},{4,8},{5,9},{6,10},{7,11},{8,4},{9,5},... | collective-permute-start | bytes 417800 | tf_op jit(solution)/shard_map/ppermute | solution.py:27
  16.2 7.4 %collective-permute-start.3 = (bf16[32,2176]{1,0:T(8,128)(2,1)S(1)}, bf16[32,2176]{1,0:T(8,128)(2,1)S(1)}, u32[]{:S(2)}, u32[]{:S(2)}) collective-permute-start(bf16[32,2176]{1,0:T(8,128)(2,1)S(1)} %pad_maximum_fusion), channel_id=1, source_target_pairs={{0,4},{1,5},{2,6},{3,7},{4,0},{5,1},{6,2},{7,3},{8,12},{9,13},{10,... | collective-permute-start | bytes 417800 | tf_op jit(solution)/shard_map/ppermute | solution.py:27
  17.1 7.0 %collective-permute-start.5 = (bf16[16,2176]{1,0:T(8,128)(2,1)S(1)}, bf16[16,2176]{1,0:T(8,128)(2,1)S(1)}, u32[]{:S(2)}, u32[]{:S(2)}) collective-permute-start(bf16[16,2176]{1,0:T(8,128)(2,1)S(1)} %collective-permute-done.4), channel_id=1, source_target_pairs={{0,2},{1,3},{2,0},{3,1},{4,6},{5,7},{6,4},{7,5},{8,10},{9,11},{10,... | collective-permute-start | bytes 208904 | tf_op jit(solution)/shard_map/ppermute | solution.py:27
  24.2 2.0 %collective-permute-start.7 = (bf16[128,2176]{1,0:T(8,128)(2,1)S(1)}, bf16[128,2176]{1,0:T(8,128)(2,1)S(1)}, u32[]{:S(2)}, u32[]{:S(2)}) collective-permute-start(bf16[128,2176]{1,0:T(8,128)(2,1)S(1)} %constant_dynamic-update-slice_fusion.mine), channel_id=1, source_target_pairs={{0,1},{1,0},{2,3},{3,2},{4,5},{5,4},{6,7},{7,6},{8,9},{9,8},{10,11... | collective-permute-start | bytes 1671176 | tf_op jit(solution)/shard_map/ppermute | solution.py:27
  28.8 2.0 %collective-permute-start.8 = (bf16[128,2048]{1,0:T(8,128)(2,1)S(1)}, bf16[128,2048]{1,0:T(8,128)(2,1)S(1)}, u32[]{:S(2)}, u32[]{:S(2)}) collective-permute-start(bf16[128,2048]{1,0:T(8,128)(2,1)S(1)} %get-tuple-element.21), channel_id=1, source_target_pairs={{0,1},{1,0},{2,3},{3,2},{4,5},{5,4},{6,7},{7,6},{8,9},{9,8},{10,11... | collective-permute-start | bytes 1572872 | tf_op jit(solution)/shard_map/ppermute | solution.py:27
  30.9 6.4 %collective-permute-start.9 = (bf16[2,16,2048]{2,1,0:T(8,128)(2,1)S(1)}, bf16[2,16,2048]{2,1,0:T(8,128)(2,1)S(1)}, u32[]{:S(2)}, u32[]{:S(2)}) collective-permute-start(bf16[2,16,2048]{2,1,0:T(8,128)(2,1)S(1)} %get-tuple-element.22), channel_id=1, source_target_pairs={{0,2},{1,3},{2,0},{3,1},{4,6},{5,7},{6,4},{7,5},{8,10},{9,11},{10,... | collective-permute-start | bytes 393224 | tf_op jit(solution)/shard_map/ppermute | solution.py:27
  33.0 6.6 %collective-permute-start.11 = (bf16[2,16,2048]{2,1,0:T(8,128)(2,1)S(1)}, bf16[2,16,2048]{2,1,0:T(8,128)(2,1)S(1)}, u32[]{:S(2)}, u32[]{:S(2)}) collective-permute-start(bf16[2,16,2048]{2,1,0:T(8,128)(2,1)S(1)} %get-tuple-element.23), channel_id=1, source_target_pairs={{0,2},{1,3},{2,0},{3,1},{4,6},{5,7},{6,4},{7,5},{8,10},{9,11},{10,... | collective-permute-start | bytes 393224 | tf_op jit(solution)/shard_map/ppermute | solution.py:27
  37.4 7.3 %collective-permute-start.10 = (bf16[16,2048]{1,0:T(8,128)(2,1)S(1)}, bf16[16,2048]{1,0:T(8,128)(2,1)S(1)}, u32[]{:S(2)}, u32[]{:S(2)}) collective-permute-start(bf16[16,2048]{1,0:T(8,128)(2,1)S(1)} %fusion.3), channel_id=1, source_target_pairs={{0,4},{1,5},{2,6},{3,7},{4,0},{5,1},{6,2},{7,3},{8,12},{9,13},{10,... | collective-permute-start | bytes 196616 | tf_op jit(solution)/shard_map/ppermute | solution.py:27
  39.7 8.4 %collective-permute-start.12 = (bf16[16,2048]{1,0:T(8,128)(2,1)S(1)}, bf16[16,2048]{1,0:T(8,128)(2,1)S(1)}, u32[]{:S(2)}, u32[]{:S(2)}) collective-permute-start(bf16[16,2048]{1,0:T(8,128)(2,1)S(1)} %get-tuple-element.26), channel_id=1, source_target_pairs={{0,8},{1,9},{2,10},{3,11},{4,12},{5,13},{6,14},{7,15},{8,0},{9,1},... | collective-permute-start | bytes 196616 | tf_op jit(solution)/shard_map/ppermute | solution.py:27
  43.3 6.2 %collective-permute-start.13 = (bf16[16,2048]{1,0:T(8,128)(2,1)S(1)}, bf16[16,2048]{1,0:T(8,128)(2,1)S(1)}, u32[]{:S(2)}, u32[]{:S(2)}) collective-permute-start(bf16[16,2048]{1,0:T(8,128)(2,1)S(1)} %get-tuple-element.27), channel_id=1, source_target_pairs={{0,12},{1,13},{2,14},{3,15},{4,8},{5,9},{6,10},{7,11},{8,4},{9,5},... | collective-permute-start | bytes 196616 | tf_op jit(solution)/shard_map/ppermute | solution.py:27
where the time goes:
time: 50.3 us; the launch traced here: 50.1 us
  starting transfers between devices  22.9 us (46%)
  waiting for transfers between devices  19.2 us (38%)
  Pallas kernels  6.27 us (12%)
  other arithmetic  0.87 us (2%)
  between operations  0.75 us (1%)
    ppermute x14, starting transfers between devices, exchanged(): lax.ppermute(block, 'ep', [(index, index ^ mask) for index in range(count)])  22.9 us
    ppermute x14, waiting for transfers between devices, exchanged(): lax.ppermute(block, 'ep', [(index, index ^ mask) for index in range(count)])  19.2 us
    pallas_call x1, Pallas kernels, every_row(): pl.pallas_call(attend_kernel, out_shape=(jax.ShapeDtypeStruct((2 * rows,...  2.86 us
    pallas_call x1, Pallas kernels, every_row(): pl.pallas_call(expert_kernel, out_shape=(jax.ShapeDtypeStruct((half, MODE...  2.62 us
  transfers between devices with their start and end apart: 14, of which 10 were waited for; matrix products, arithmetic and copies ran while one was open for 0% of the time, Pallas kernels for 2%

commit v1 on v0

--- a/solution.py
+++ b/solution.py
@@ -146,12 +146,15 @@
         send[:, cols] = out[half:].astype(jnp.bfloat16)
 
 
+def sum_kernel(sums, got, out):
+    out[...] = (sums[1, 0] + got[...].astype(jnp.float32)).astype(jnp.bfloat16)
+
+
 def every_row(
     queries, key_cache, value_cache, key_block, value_block, cache_length_list, residual,
     output_weight, norm_gain, routes, route_logits, w_gate, w_up, w_down,
 ):
     rows = residual.shape[0]
-    owners = lax.axis_size("ep")
     anywhere = pl.BlockSpec(memory_space=pl.ANY)
     whole = pl.BlockSpec(memory_space=pltpu.VMEM)
     operands = (
@@ -185,7 +188,7 @@
     chip_pair = exchanged(sums[:rows], 2)
 
     def normed(block, chip):
-        outs = (jax.ShapeDtypeStruct((rows, MODEL_WIDTH), jnp.bfloat16),) * (block == 0)
+        outs = (pltpu.VMEM((rows, MODEL_WIDTH), jnp.bfloat16),) * (block == 0)
         outs += (jax.ShapeDtypeStruct((rows, WIDE), jnp.bfloat16),)
         return pl.pallas_call(
             functools.partial(norm_kernel, block),
@@ -199,44 +202,59 @@
             name="norm",
         )(kept, core, chip, norm_gain[None])
 
+    def expert(mine):
+        half = mine.shape[0]
+        other = exchanged(mine, 1)
+        keep, send = pl.pallas_call(
+            expert_kernel,
+            out_shape=(
+                jax.ShapeDtypeStruct((half, MODEL_WIDTH), jnp.float32),
+                jax.ShapeDtypeStruct((half, MODEL_WIDTH), jnp.bfloat16),
+            ),
+            in_specs=[whole] * 5,
+            out_specs=(whole, whole),
+            scratch_shapes=[
+                pltpu.VMEM((2 * half, WIDE), jnp.bfloat16),
+                pltpu.VMEM((2 * half, w_gate.shape[2]), jnp.bfloat16),
+            ],
+            compiler_params=pltpu.CompilerParams(vmem_limit_bytes=12 << 20),
+            cost_estimate=pl.CostEstimate(
+                flops=1 << 30, bytes_accessed=1 << 23, transcendentals=1 << 18
+            ),
+            name="expert",
+        )(mine, other, w_gate, w_up, w_down)
+        back = exchanged(send, 1)
+        total = keep + back.astype(jnp.float32)
+        return total.reshape(half // (2 * rows), 2, rows, MODEL_WIDTH)
+
     attended, own = normed(0, chip_own)
     far = exchanged(own, 8)
     (pair,) = normed(1, chip_pair)
     packet = jnp.concatenate([own, pair], 0)
+    near = exchanged(packet, 4)
     across = exchanged(packet, 12)
-    near = exchanged(packet, 4)
     passed = exchanged(far, 2)
-    mine = jnp.concatenate([packet, near, far, passed, across], 0)
-    other = exchanged(mine, 1)
-    half = mine.shape[0]
-    keep, send = pl.pallas_call(
-        expert_kernel,
-        out_shape=(
-            jax.ShapeDtypeStruct((half, MODEL_WIDTH), jnp.float32),
-            jax.ShapeDtypeStruct((half, MODEL_WIDTH), jnp.bfloat16),
-        ),
-        in_specs=[whole] * 5,
-        out_specs=(whole, whole),
-        scratch_shapes=[
-            pltpu.VMEM((2 * half, WIDE), jnp.bfloat16),
-            pltpu.VMEM((2 * half, w_gate.shape[2]), jnp.bfloat16),
-        ],
-        compiler_params=pltpu.CompilerParams(vmem_limit_bytes=12 << 20),
-        cost_estimate=pl.CostEstimate(flops=1 << 31, bytes_accessed=1 << 23, transcendentals=1 << 18),
-        name="expert",
-    )(mine, other, w_gate, w_up, w_down)
-    total = keep + exchanged(send, 1).astype(jnp.float32)
-    total = total.reshape(owners // 4, 2, rows, MODEL_WIDTH)
-    to_chip = total[:, 1].astype(jnp.bfloat16)
-    got_far = exchanged(to_chip[2:], 2)
-    got_near = exchanged(to_chip[:2], 2)
-    far_sums = (total[2:, 0] + got_far.astype(jnp.float32)).astype(jnp.bfloat16)
-    across = exchanged(far_sums[1], 12)
-    far = exchanged(far_sums[0], 8)
-    near_sum = (total[1, 0] + got_near[1].astype(jnp.float32)).astype(jnp.bfloat16)
+    sums = expert(jnp.concatenate([packet, near], 0))
+    got = exchanged(sums[:, 1].astype(jnp.bfloat16), 2)
+    summed = sums[0, 0] + got[0].astype(jnp.float32)
+    near_sum = (sums[1, 0] + got[1].astype(jnp.float32)).astype(jnp.bfloat16)
     near = exchanged(near_sum, 4)
-    summed = total[0, 0] + got_near[0].astype(jnp.float32) + near.astype(jnp.float32)
-    summed = summed + far.astype(jnp.float32) + across.astype(jnp.float32)
+    sums = expert(jnp.concatenate([far, passed, across], 0))
+    got_across = exchanged(sums[1, 1].astype(jnp.bfloat16), 2)
+    got_far = exchanged(sums[0, 1].astype(jnp.bfloat16), 2)
+    across_sum = pl.pallas_call(
+        sum_kernel,
+        out_shape=jax.ShapeDtypeStruct((rows, MODEL_WIDTH), jnp.bfloat16),
+        in_specs=[whole] * 2,
+        out_specs=whole,
+        compiler_params=pltpu.CompilerParams(vmem_limit_bytes=4 << 20),
+        cost_estimate=pl.CostEstimate(flops=1 << 16, bytes_accessed=1 << 18, transcendentals=0),
+        name="acrosssum",
+    )(sums, got_across)
+    across = exchanged(across_sum, 12)
+    far_sum = (sums[0, 0] + got_far.astype(jnp.float32)).astype(jnp.bfloat16)
+    far = exchanged(far_sum, 8)
+    summed = summed + near.astype(jnp.float32) + far.astype(jnp.float32) + across.astype(jnp.float32)
     return (attended, summed.astype(jnp.bfloat16))
 
 

time: 50.3 us -> 46 us (0.915)
  waiting for transfers between devices: 19.2 us -> 11.7 us
  starting transfers between devices: 22.9 us -> 25.6 us
  local copies, waits for them, and re-layouts: 0.14 us -> 0.72 us
    ppermute x14 -> x17, waiting for transfers between devices: 19.2 us -> 11.7 us  [exchanged(): lax.ppermute(block, 'ep', [(index, index ^ mask) for index in range(count)])]
    ppermute x14 -> x17, starting transfers between devices: 22.9 us -> 25.6 us  [exchanged(): lax.ppermute(block, 'ep', [(index, index ^ mask) for index in range(count)])]
    unnamed x13 -> x11, local copies, waits for them, and re-layouts: 0.07 us -> 0.66 us
    pallas_call x2, Pallas kernels: 0.79 us -> 0.24 us  [normed(): pl.pallas_call(functools.partial(norm_kernel, block), out_shape=outs, in_...]
    pallas_call x1 -> x3, Pallas kernels: 2.62 us -> 2.97 us  [the longest x2 2.95 us: expert(): pl.pallas_call(expert_kernel, out_shape=(jax.ShapeDtypeStruct((half, MODE...]
  transfers between devices with their start and end apart: 14 -> 17, of which waited for: 10 -> 9; matrix products, arithmetic and copies ran while one was open for 0% -> 2% of each run, Pallas kernels for 2% -> 7%
where the time goes in v1:
time: 46 us; the launch traced here: 45.8 us
  starting transfers between devices  25.6 us (56%)
  waiting for transfers between devices  11.7 us (25%)
  Pallas kernels  6.08 us (13%)
  other arithmetic  0.91 us (2%)
  between operations  0.79 us (2%)
  local copies, waits for them, and re-layouts  0.72 us (2%)
    ppermute x17, starting transfers between devices, exchanged(): lax.ppermute(block, 'ep', [(index, index ^ mask) for index in range(count)])  25.6 us
    ppermute x17, waiting for transfers between devices, exchanged(): lax.ppermute(block, 'ep', [(index, index ^ mask) for index in range(count)])  11.7 us
    pallas_call x2, Pallas kernels, expert(): pl.pallas_call(expert_kernel, out_shape=(jax.ShapeDtypeStruct((half, MODE...  2.95 us
    pallas_call x1, Pallas kernels, every_row(): pl.pallas_call(attend_kernel, out_shape=(jax.ShapeDtypeStruct((2 * rows,...  2.86 us
  transfers between devices with their start and end apart: 17, of which 9 were waited for; matrix products, arithmetic and copies ran while one was open for 2% of the time, Pallas kernels for 7%

profile of v1, /device:TPU:0, one launch (start us, length us, event | category | flops | bytes accessed | tf_op | source)
XLA Modules:
  0.0 45.8 jit_solution(8034908130527307357)
XLA Ops:
  0.6 2.9 %attend.1 = (bf16[32,2176]{1,0:T(8,128)(2,1)S(1)}, f32[32,2176]{1,0:T(8,128)S(1)}) custom-call(s32[8]{0:T(128)} %lens_hbm.1, bf16[1,64,512]{2,1,0:T(8,128)(2,1)} %q_hbm.1, bf16[1,2,512,128]{3,2,1,0:T(8,128)(2,1)} %kc_hbm.1, bf16[1,2,512,128]{3,2,1,0:T(8,128)(2,1)} %vc_hbm.1, bf16[1,64,128]{2,1,0:T(8,128)(2,1)} %kb_hbm.1, bf16[1,64,128]{2,1,0:T(8,128)(2,1)} %vb_hbm.1, ...), custom_call_target="tpu_custom_call" | custom-call | flops 1073741824 | bytes 8388608 | tf_op jit(solution)/shard_map/attend/pallas_call | solution.py:171
  3.5 0.6 %collective-permute-start = (bf16[32,2176]{1,0:T(8,128)(2,1)S(1)}, bf16[32,2176]{1,0:T(8,128)(2,1)S(1)}, u32[]{:S(2)}, u32[]{:S(2)}) collective-permute-start(bf16[32,2176]{1,0:T(8,128)(2,1)S(1)} %get-tuple-element.16), channel_id=1, source_target_pairs={{0,1},{1,0},{2,3},{3,2},{4,5},{5,4},{6,7},{7,6},{8,9},{9,8},{10,11... | collective-permute-start | bytes 417800 | tf_op jit(solution)/shard_map/ppermute | solution.py:27
  4.1 1.0 %collective-permute-done.core = bf16[32,2176]{1,0:T(8,128)(2,1)S(1)} collective-permute-done((bf16[32,2176]{1,0:T(8,128)(2,1)S(1)}, bf16[32,2176]{1,0:T(8,128)(2,1)S(1)}, u32[]{:S(2)}, u32[]{:S(2)}) %collective-permute-start) | collective-permute-done | bytes 139296 | tf_op jit(solution)/shard_map/ppermute | solution.py:27
  5.1 2.9 %collective-permute-start.1 = (bf16[16,2176]{1,0:T(8,128)(2,1)S(1)}, bf16[16,2176]{1,0:T(8,128)(2,1)S(1)}, u32[]{:S(2)}, u32[]{:S(2)}) collective-permute-start(bf16[16,2176]{1,0:T(8,128)(2,1)S(1)} %get-tuple-element.29), channel_id=1, source_target_pairs={{0,2},{1,3},{2,0},{3,1},{4,6},{5,7},{6,4},{7,5},{8,10},{9,11},{10,... | collective-permute-start | bytes 208904 | tf_op jit(solution)/shard_map/ppermute | solution.py:27
  8.0 0.1 collective-permute-start.2
  8.1 2.4 %collective-permute-done.1.chip = bf16[16,2176]{1,0:T(8,128)(2,1)S(1)} collective-permute-done((bf16[16,2176]{1,0:T(8,128)(2,1)S(1)}, bf16[16,2176]{1,0:T(8,128)(2,1)S(1)}, u32[]{:S(2)}, u32[]{:S(2)}) %collective-permute-start.1) | collective-permute-done | bytes 69664 | tf_op jit(solution)/shard_map/ppermute | solution.py:27
  10.5 0.1 norm.2
  10.7 3.3 %collective-permute-start.8 = (bf16[16,2176]{1,0:T(8,128)(2,1)S(1)}, bf16[16,2176]{1,0:T(8,128)(2,1)S(1)}, u32[]{:S(2)}, u32[]{:S(2)}) collective-permute-start(bf16[16,2176]{1,0:T(8,128)(2,1)S(1)} %get-tuple-element.18), channel_id=1, source_target_pairs={{0,8},{1,9},{2,10},{3,11},{4,12},{5,13},{6,14},{7,15},{8,0},{9,1},... | collective-permute-start | bytes 208904 | tf_op jit(solution)/shard_map/ppermute | solution.py:27
  14.0 0.1 norm.3
  14.2 2.0 %collective-permute-start.10 = (bf16[32,2176]{1,0:T(8,128)(2,1)S(1)}, bf16[32,2176]{1,0:T(8,128)(2,1)S(1)}, u32[]{:S(2)}, u32[]{:S(2)}) collective-permute-start(bf16[32,2176]{1,0:T(8,128)(2,1)S(1)} %pad_maximum_fusion.1), channel_id=1, source_target_pairs={{0,12},{1,13},{2,14},{3,15},{4,8},{5,9},{6,10},{7,11},{8,4},{9,5},... | collective-permute-start | bytes 417800 | tf_op jit(solution)/shard_map/ppermute | solution.py:27
  16.2 0.2 collective-permute-done.8
  16.4 5.0 %collective-permute-start.9 = (bf16[16,2176]{1,0:T(8,128)(2,1)S(1)}, bf16[16,2176]{1,0:T(8,128)(2,1)S(1)}, u32[]{:S(2)}, u32[]{:S(2)}) collective-permute-start(bf16[16,2176]{1,0:T(8,128)(2,1)S(1)} %collective-permute-done.8), channel_id=1, source_target_pairs={{0,2},{1,3},{2,0},{3,1},{4,6},{5,7},{6,4},{7,5},{8,10},{9,11},{10,... | collective-permute-start | bytes 208904 | tf_op jit(solution)/shard_map/ppermute | solution.py:27
  21.4 2.3 %collective-permute-done.9 = bf16[16,2176]{1,0:T(8,128)(2,1)S(1)} collective-permute-done((bf16[16,2176]{1,0:T(8,128)(2,1)S(1)}, bf16[16,2176]{1,0:T(8,128)(2,1)S(1)}, u32[]{:S(2)}, u32[]{:S(2)}) %collective-permute-start.9) | collective-permute-done | bytes 69664 | tf_op jit(solution)/shard_map/ppermute | solution.py:27
  23.7 0.1 collective-permute-start.11
  23.8 0.6 %collective-permute-start.4 = (bf16[64,2176]{1,0:T(8,128)(2,1)S(1)}, bf16[64,2176]{1,0:T(8,128)(2,1)S(1)}, u32[]{:S(2)}, u32[]{:S(2)}) collective-permute-start(bf16[64,2176]{1,0:T(8,128)(2,1)S(1)} %pad_maximum_fusion.mine), channel_id=1, source_target_pairs={{0,1},{1,0},{2,3},{3,2},{4,5},{5,4},{6,7},{7,6},{8,9},{9,8},{10,11... | collective-permute-start | bytes 835592 | tf_op jit(solution)/shard_map/ppermute | solution.py:27
  24.4 0.9 %collective-permute-done.11.other = bf16[64,2176]{1,0:T(8,128)(2,1)S(1)} collective-permute-done((bf16[64,2176]{1,0:T(8,128)(2,1)S(1)}, bf16[64,2176]{1,0:T(8,128)(2,1)S(1)}, u32[]{:S(2)}, u32[]{:S(2)}) %collective-permute-start.11) | collective-permute-done | bytes 278560 | tf_op jit(solution)/shard_map/ppermute | solution.py:27
  25.3 1.5 %expert.3 = (f32[64,2048]{1,0:T(8,128)S(1)}, bf16[64,2048]{1,0:T(8,128)(2,1)S(1)}) custom-call(bf16[64,2176]{1,0:T(8,128)(2,1)S(1)} %constant_dynamic-update-slice_fusion.mine, bf16[64,2176]{1,0:T(8,128)(2,1)S(1)} %collective-permute-done.11.other, bf16[1,2048,768]{2,1,0:T(8,128)(2,1)S(1)} %copy-done, bf16[1,2048,768]{2,1,0:T(8,128)(2,1)S(1)} %copy-done.1, ...), custom_call_target="tpu_custom_call" | custom-call | flops 1073741824 | bytes 8388608 | tf_op jit(solution)/shard_map/expert/pallas_call | solution.py:208
  26.8 0.2 collective-permute-start.12
  27.0 1.5 %expert.2 = (f32[64,2048]{1,0:T(8,128)S(1)}, bf16[64,2048]{1,0:T(8,128)(2,1)S(1)}) custom-call(bf16[64,2176]{1,0:T(8,128)(2,1)S(1)} %pad_maximum_fusion.mine, bf16[64,2176]{1,0:T(8,128)(2,1)S(1)} %collective-permute-done.4.other, bf16[1,2048,768]{2,1,0:T(8,128)(2,1)S(1)} %copy-done, bf16[1,2048,768]{2,1,0:T(8,128)(2,1)S(1)} %copy-done.1, ...), custom_call_target="tpu_custom_call" | custom-call | flops 1073741824 | bytes 8388608 | tf_op jit(solution)/shard_map/expert/pallas_call | solution.py:208
  28.5 0.4 collective-permute-start.5
  29.1 2.1 %collective-permute-start.13 = (bf16[16,2048]{1,0:T(8,128)(2,1)S(1)}, bf16[16,2048]{1,0:T(8,128)(2,1)S(1)}, u32[]{:S(2)}, u32[]{:S(2)}) collective-permute-start(bf16[16,2048]{1,0:T(8,128)(2,1)S(1)} %get-tuple-element.26), channel_id=1, source_target_pairs={{0,2},{1,3},{2,0},{3,1},{4,6},{5,7},{6,4},{7,5},{8,10},{9,11},{10,... | collective-permute-start | bytes 196616 | tf_op jit(solution)/shard_map/ppermute | solution.py:27
  31.1 0.1 collective-permute-start.15
  31.3 2.0 %collective-permute-start.6 = (bf16[2,16,2048]{2,1,0:T(8,128)(2,1)S(1)}, bf16[2,16,2048]{2,1,0:T(8,128)(2,1)S(1)}, u32[]{:S(2)}, u32[]{:S(2)}) collective-permute-start(bf16[2,16,2048]{2,1,0:T(8,128)(2,1)S(1)} %fusion), channel_id=1, source_target_pairs={{0,2},{1,3},{2,0},{3,1},{4,6},{5,7},{6,4},{7,5},{8,10},{9,11},{10,... | collective-permute-start | bytes 393224 | tf_op jit(solution)/shard_map/ppermute | solution.py:27
  33.3 0.3 collective-permute-done.13
  33.6 1.6 %collective-permute-start.14 = (bf16[16,2048]{1,0:T(8,128)(2,1)S(1)}, bf16[16,2048]{1,0:T(8,128)(2,1)S(1)}, u32[]{:S(2)}, u32[]{:S(2)}) collective-permute-start(bf16[16,2048]{1,0:T(8,128)(2,1)S(1)} %fusion.2), channel_id=1, source_target_pairs={{0,8},{1,9},{2,10},{3,11},{4,12},{5,13},{6,14},{7,15},{8,0},{9,1},... | collective-permute-start | bytes 196616 | tf_op jit(solution)/shard_map/ppermute | solution.py:27
  35.2 0.9 %collective-permute-done.15.got = bf16[16,2048]{1,0:T(8,128)(2,1)S(1)} collective-permute-done((bf16[16,2048]{1,0:T(8,128)(2,1)S(1)}, bf16[16,2048]{1,0:T(8,128)(2,1)S(1)}, u32[]{:S(2)}, u32[]{:S(2)}) %collective-permute-start.15) | collective-permute-done | bytes 65568 | tf_op jit(solution)/shard_map/ppermute | solution.py:27
  36.1 4.7 %collective-permute-start.16 = (bf16[16,2048]{1,0:T(8,128)(2,1)S(1)}, bf16[16,2048]{1,0:T(8,128)(2,1)S(1)}, u32[]{:S(2)}, u32[]{:S(2)}) collective-permute-start(bf16[16,2048]{1,0:T(8,128)(2,1)S(1)} %acrosssum.1), channel_id=1, source_target_pairs={{0,12},{1,13},{2,14},{3,15},{4,8},{5,9},{6,10},{7,11},{8,4},{9,5},... | collective-permute-start | bytes 196616 | tf_op jit(solution)/shard_map/ppermute | solution.py:27
  40.8 0.1 collective-permute-start.7
  40.9 0.6 %copy.18 = bf16[16,2048]{1,0:T(8,128)(2,1)} copy(bf16[16,2048]{1,0:T(8,128)(2,1)S(1)} %get-tuple-element.30) | data formatting | bytes 131072
  41.5 1.6 %collective-permute-done.16 = bf16[16,2048]{1,0:T(8,128)(2,1)S(1)} collective-permute-done((bf16[16,2048]{1,0:T(8,128)(2,1)S(1)}, bf16[16,2048]{1,0:T(8,128)(2,1)S(1)}, u32[]{:S(2)}, u32[]{:S(2)}) %collective-permute-start.16) | collective-permute-done | bytes 65568 | tf_op jit(solution)/shard_map/ppermute | solution.py:27
  43.2 2.0 %collective-permute-done.7 = bf16[16,2048]{1,0:T(8,128)(2,1)S(1)} collective-permute-done((bf16[16,2048]{1,0:T(8,128)(2,1)S(1)}, bf16[16,2048]{1,0:T(8,128)(2,1)S(1)}, u32[]{:S(2)}, u32[]{:S(2)}) %collective-permute-start.7) | collective-permute-done | bytes 65568 | tf_op jit(solution)/shard_map/ppermute | solution.py:27
  45.1 0.7 %fusion.9 = bf16[16,2048]{1,0:T(8,128)(2,1)} fusion(f32[2,2,16,2048]{3,2,1,0:T(8,128)S(1)} %bitcast.52, bf16[16,2048]{1,0:T(8,128)(2,1)S(1)} %collective-permute-done.16, bf16[16,2048]{1,0:T(8,128)(2,1)S(1)} %collective-permute-done.14, bf16[16,2048]{1,0:T(8,128)(2,1)S(1)} %collective-permute-done.7, bf16[2,16,2048]{2,1,0:T(8,128)(2,1)S(1)} %collective-permute-done.6), kind=kLoop, calls=%fused_computation.18 | loop fusion | flops 294912 | bytes 458752 | tf_op jit(solution)/shard_map/convert_element_type | solution.py:258
  (32 shorter events, 0.4 us)
Async XLA Ops:
  0.6 9.9 %copy-start.3 = (f32[2048]{0:T(1024)S(1)}, f32[2048]{0:T(1024)}, u32[]{:S(2)}) copy-start(f32[2048]{0:T(1024)} %param.22) | copy-start | bytes 24580
  3.5 1.6 %collective-permute-start = (bf16[32,2176]{1,0:T(8,128)(2,1)S(1)}, bf16[32,2176]{1,0:T(8,128)(2,1)S(1)}, u32[]{:S(2)}, u32[]{:S(2)}) collective-permute-start(bf16[32,2176]{1,0:T(8,128)(2,1)S(1)} %get-tuple-element.16), channel_id=1, source_target_pairs={{0,1},{1,0},{2,3},{3,2},{4,5},{5,4},{6,7},{7,6},{8,9},{9,8},{10,11... | collective-permute-start | bytes 417800 | tf_op jit(solution)/shard_map/ppermute | solution.py:27
  5.1 5.4 %collective-permute-start.1 = (bf16[16,2176]{1,0:T(8,128)(2,1)S(1)}, bf16[16,2176]{1,0:T(8,128)(2,1)S(1)}, u32[]{:S(2)}, u32[]{:S(2)}) collective-permute-start(bf16[16,2176]{1,0:T(8,128)(2,1)S(1)} %get-tuple-element.29), channel_id=1, source_target_pairs={{0,2},{1,3},{2,0},{3,1},{4,6},{5,7},{6,4},{7,5},{8,10},{9,11},{10,... | collective-permute-start | bytes 208904 | tf_op jit(solution)/shard_map/ppermute | solution.py:27
  8.0 6.0 %collective-permute-start.2 = (bf16[16,2176]{1,0:T(8,128)(2,1)S(1)}, bf16[16,2176]{1,0:T(8,128)(2,1)S(1)}, u32[]{:S(2)}, u32[]{:S(2)}) collective-permute-start(bf16[16,2176]{1,0:T(8,128)(2,1)S(1)} %get-tuple-element.28), channel_id=1, source_target_pairs={{0,2},{1,3},{2,0},{3,1},{4,6},{5,7},{6,4},{7,5},{8,10},{9,11},{10,... | collective-permute-start | bytes 208904 | tf_op jit(solution)/shard_map/ppermute | solution.py:27
  10.7 5.7 %collective-permute-start.8 = (bf16[16,2176]{1,0:T(8,128)(2,1)S(1)}, bf16[16,2176]{1,0:T(8,128)(2,1)S(1)}, u32[]{:S(2)}, u32[]{:S(2)}) collective-permute-start(bf16[16,2176]{1,0:T(8,128)(2,1)S(1)} %get-tuple-element.18), channel_id=1, source_target_pairs={{0,8},{1,9},{2,10},{3,11},{4,12},{5,13},{6,14},{7,15},{8,0},{9,1},... | collective-permute-start | bytes 208904 | tf_op jit(solution)/shard_map/ppermute | solution.py:27
  14.0 11.3 %copy-start = (bf16[1,2048,768]{2,1,0:T(8,128)(2,1)S(1)}, bf16[1,2048,768]{2,1,0:T(8,128)(2,1)}, u32[]{:S(2)}) copy-start(bf16[1,2048,768]{2,1,0:T(8,128)(2,1)} %w_gate.1) | copy-start | bytes 9437188
  14.0 11.3 %copy-start.1 = (bf16[1,2048,768]{2,1,0:T(8,128)(2,1)S(1)}, bf16[1,2048,768]{2,1,0:T(8,128)(2,1)}, u32[]{:S(2)}) copy-start(bf16[1,2048,768]{2,1,0:T(8,128)(2,1)} %w_up.1) | copy-start | bytes 9437188
  14.0 11.3 %copy-start.2 = (bf16[1,768,2048]{2,1,0:T(8,128)(2,1)S(1)}, bf16[1,768,2048]{2,1,0:T(8,128)(2,1)}, u32[]{:S(2)}) copy-start(bf16[1,768,2048]{2,1,0:T(8,128)(2,1)} %w_down.1) | copy-start | bytes 9437188
  14.2 9.5 %collective-permute-start.10 = (bf16[32,2176]{1,0:T(8,128)(2,1)S(1)}, bf16[32,2176]{1,0:T(8,128)(2,1)S(1)}, u32[]{:S(2)}, u32[]{:S(2)}) collective-permute-start(bf16[32,2176]{1,0:T(8,128)(2,1)S(1)} %pad_maximum_fusion.1), channel_id=1, source_target_pairs={{0,12},{1,13},{2,14},{3,15},{4,8},{5,9},{6,10},{7,11},{8,4},{9,5},... | collective-permute-start | bytes 417800 | tf_op jit(solution)/shard_map/ppermute | solution.py:27
  16.2 7.6 %collective-permute-start.3 = (bf16[32,2176]{1,0:T(8,128)(2,1)S(1)}, bf16[32,2176]{1,0:T(8,128)(2,1)S(1)}, u32[]{:S(2)}, u32[]{:S(2)}) collective-permute-start(bf16[32,2176]{1,0:T(8,128)(2,1)S(1)} %pad_maximum_fusion.1), channel_id=1, source_target_pairs={{0,4},{1,5},{2,6},{3,7},{4,0},{5,1},{6,2},{7,3},{8,12},{9,13},{10,... | collective-permute-start | bytes 417800 | tf_op jit(solution)/shard_map/ppermute | solution.py:27
  16.4 7.3 %collective-permute-start.9 = (bf16[16,2176]{1,0:T(8,128)(2,1)S(1)}, bf16[16,2176]{1,0:T(8,128)(2,1)S(1)}, u32[]{:S(2)}, u32[]{:S(2)}) collective-permute-start(bf16[16,2176]{1,0:T(8,128)(2,1)S(1)} %collective-permute-done.8), channel_id=1, source_target_pairs={{0,2},{1,3},{2,0},{3,1},{4,6},{5,7},{6,4},{7,5},{8,10},{9,11},{10,... | collective-permute-start | bytes 208904 | tf_op jit(solution)/shard_map/ppermute | solution.py:27
  23.7 1.6 %collective-permute-start.11 = (bf16[64,2176]{1,0:T(8,128)(2,1)S(1)}, bf16[64,2176]{1,0:T(8,128)(2,1)S(1)}, u32[]{:S(2)}, u32[]{:S(2)}) collective-permute-start(bf16[64,2176]{1,0:T(8,128)(2,1)S(1)} %constant_dynamic-update-slice_fusion.mine), channel_id=1, source_target_pairs={{0,1},{1,0},{2,3},{3,2},{4,5},{5,4},{6,7},{7,6},{8,9},{9,8},{10,11... | collective-permute-start | bytes 835592 | tf_op jit(solution)/shard_map/ppermute | solution.py:27
  23.8 3.2 %collective-permute-start.4 = (bf16[64,2176]{1,0:T(8,128)(2,1)S(1)}, bf16[64,2176]{1,0:T(8,128)(2,1)S(1)}, u32[]{:S(2)}, u32[]{:S(2)}) collective-permute-start(bf16[64,2176]{1,0:T(8,128)(2,1)S(1)} %pad_maximum_fusion.mine), channel_id=1, source_target_pairs={{0,1},{1,0},{2,3},{3,2},{4,5},{5,4},{6,7},{7,6},{8,9},{9,8},{10,11... | collective-permute-start | bytes 835592 | tf_op jit(solution)/shard_map/ppermute | solution.py:27
  26.8 2.1 %collective-permute-start.12 = (bf16[64,2048]{1,0:T(8,128)(2,1)S(1)}, bf16[64,2048]{1,0:T(8,128)(2,1)S(1)}, u32[]{:S(2)}, u32[]{:S(2)}) collective-permute-start(bf16[64,2048]{1,0:T(8,128)(2,1)S(1)} %get-tuple-element.25), channel_id=1, source_target_pairs={{0,1},{1,0},{2,3},{3,2},{4,5},{5,4},{6,7},{7,6},{8,9},{9,8},{10,11... | collective-permute-start | bytes 786440 | tf_op jit(solution)/shard_map/ppermute | solution.py:27
  28.5 2.7 %collective-permute-start.5 = (bf16[64,2048]{1,0:T(8,128)(2,1)S(1)}, bf16[64,2048]{1,0:T(8,128)(2,1)S(1)}, u32[]{:S(2)}, u32[]{:S(2)}) collective-permute-start(bf16[64,2048]{1,0:T(8,128)(2,1)S(1)} %get-tuple-element.23), channel_id=1, source_target_pairs={{0,1},{1,0},{2,3},{3,2},{4,5},{5,4},{6,7},{7,6},{8,9},{9,8},{10,11... | collective-permute-start | bytes 786440 | tf_op jit(solution)/shard_map/ppermute | solution.py:27
  29.1 4.6 %collective-permute-start.13 = (bf16[16,2048]{1,0:T(8,128)(2,1)S(1)}, bf16[16,2048]{1,0:T(8,128)(2,1)S(1)}, u32[]{:S(2)}, u32[]{:S(2)}) collective-permute-start(bf16[16,2048]{1,0:T(8,128)(2,1)S(1)} %get-tuple-element.26), channel_id=1, source_target_pairs={{0,2},{1,3},{2,0},{3,1},{4,6},{5,7},{6,4},{7,5},{8,10},{9,11},{10,... | collective-permute-start | bytes 196616 | tf_op jit(solution)/shard_map/ppermute | solution.py:27
  31.1 5.0 %collective-permute-start.15 = (bf16[16,2048]{1,0:T(8,128)(2,1)S(1)}, bf16[16,2048]{1,0:T(8,128)(2,1)S(1)}, u32[]{:S(2)}, u32[]{:S(2)}) collective-permute-start(bf16[16,2048]{1,0:T(8,128)(2,1)S(1)} %get-tuple-element.27), channel_id=1, source_target_pairs={{0,2},{1,3},{2,0},{3,1},{4,6},{5,7},{6,4},{7,5},{8,10},{9,11},{10,... | collective-permute-start | bytes 196616 | tf_op jit(solution)/shard_map/ppermute | solution.py:27
  31.3 9.5 %collective-permute-start.6 = (bf16[2,16,2048]{2,1,0:T(8,128)(2,1)S(1)}, bf16[2,16,2048]{2,1,0:T(8,128)(2,1)S(1)}, u32[]{:S(2)}, u32[]{:S(2)}) collective-permute-start(bf16[2,16,2048]{2,1,0:T(8,128)(2,1)S(1)} %fusion), channel_id=1, source_target_pairs={{0,2},{1,3},{2,0},{3,1},{4,6},{5,7},{6,4},{7,5},{8,10},{9,11},{10,... | collective-permute-start | bytes 393224 | tf_op jit(solution)/shard_map/ppermute | solution.py:27
  33.6 7.9 %collective-permute-start.14 = (bf16[16,2048]{1,0:T(8,128)(2,1)S(1)}, bf16[16,2048]{1,0:T(8,128)(2,1)S(1)}, u32[]{:S(2)}, u32[]{:S(2)}) collective-permute-start(bf16[16,2048]{1,0:T(8,128)(2,1)S(1)} %fusion.2), channel_id=1, source_target_pairs={{0,8},{1,9},{2,10},{3,11},{4,12},{5,13},{6,14},{7,15},{8,0},{9,1},... | collective-permute-start | bytes 196616 | tf_op jit(solution)/shard_map/ppermute | solution.py:27
  36.1 7.0 %collective-permute-start.16 = (bf16[16,2048]{1,0:T(8,128)(2,1)S(1)}, bf16[16,2048]{1,0:T(8,128)(2,1)S(1)}, u32[]{:S(2)}, u32[]{:S(2)}) collective-permute-start(bf16[16,2048]{1,0:T(8,128)(2,1)S(1)} %acrosssum.1), channel_id=1, source_target_pairs={{0,12},{1,13},{2,14},{3,15},{4,8},{5,9},{6,10},{7,11},{8,4},{9,5},... | collective-permute-start | bytes 196616 | tf_op jit(solution)/shard_map/ppermute | solution.py:27
  40.8 4.3 %collective-permute-start.7 = (bf16[16,2048]{1,0:T(8,128)(2,1)S(1)}, bf16[16,2048]{1,0:T(8,128)(2,1)S(1)}, u32[]{:S(2)}, u32[]{:S(2)}) collective-permute-start(bf16[16,2048]{1,0:T(8,128)(2,1)S(1)} %fusion.4), channel_id=1, source_target_pairs={{0,4},{1,5},{2,6},{3,7},{4,0},{5,1},{6,2},{7,3},{8,12},{9,13},{10,... | collective-permute-start | bytes 196616 | tf_op jit(solution)/shard_map/ppermute | solution.py:27

commit v2 on v1

--- a/solution.py
+++ b/solution.py
@@ -235,9 +235,10 @@
     across = exchanged(packet, 12)
     passed = exchanged(far, 2)
     sums = expert(jnp.concatenate([packet, near], 0))
-    got = exchanged(sums[:, 1].astype(jnp.bfloat16), 2)
-    summed = sums[0, 0] + got[0].astype(jnp.float32)
-    near_sum = (sums[1, 0] + got[1].astype(jnp.float32)).astype(jnp.bfloat16)
+    got_near = exchanged(sums[1, 1].astype(jnp.bfloat16), 2)
+    got_own = exchanged(sums[0, 1].astype(jnp.bfloat16), 2)
+    near_sum = (sums[1, 0] + got_near.astype(jnp.float32)).astype(jnp.bfloat16)
+    summed = sums[0, 0] + got_own.astype(jnp.float32)
     near = exchanged(near_sum, 4)
     sums = expert(jnp.concatenate([far, passed, across], 0))
     got_across = exchanged(sums[1, 1].astype(jnp.bfloat16), 2)

time: 46 us -> 46 us (level)
    ppermute x17 -> x18, waiting for transfers between devices: 11.7 us -> 11.6 us  [exchanged(): lax.ppermute(block, 'ep', [(index, index ^ mask) for index in range(count)])]
    ppermute x17 -> x18, starting transfers between devices: 25.6 us -> 25.7 us  [exchanged(): lax.ppermute(block, 'ep', [(index, index ^ mask) for index in range(count)])]
  transfers between devices with their start and end apart: 17 -> 18, of which waited for: 9 -> 9; matrix products, arithmetic and copies ran while one was open for 2% -> 2% of each run, Pallas kernels for 7% -> 7%
where the time goes in v2:
time: 46 us; the launch traced here: 45.8 us
  starting transfers between devices  25.7 us (56%)
  waiting for transfers between devices  11.6 us (25%)
  Pallas kernels  6.08 us (13%)
  other arithmetic  0.94 us (2%)
  between operations  0.8 us (2%)
  local copies, waits for them, and re-layouts  0.72 us (2%)
    ppermute x18, starting transfers between devices, exchanged(): lax.ppermute(block, 'ep', [(index, index ^ mask) for index in range(count)])  25.7 us
    ppermute x18, waiting for transfers between devices, exchanged(): lax.ppermute(block, 'ep', [(index, index ^ mask) for index in range(count)])  11.6 us
    pallas_call x2, Pallas kernels, expert(): pl.pallas_call(expert_kernel, out_shape=(jax.ShapeDtypeStruct((half, MODE...  2.95 us
    pallas_call x1, Pallas kernels, every_row(): pl.pallas_call(attend_kernel, out_shape=(jax.ShapeDtypeStruct((2 * rows,...  2.86 us
  transfers between devices with their start and end apart: 18, of which 9 were waited for; matrix products, arithmetic and copies ran while one was open for 2% of the time, Pallas kernels for 7%

profile of v2, /device:TPU:0, one launch (start us, length us, event | category | flops | bytes accessed | tf_op | source)
XLA Modules:
  0.0 45.8 jit_solution(278229120273220441)
XLA Ops:
  0.6 2.9 %attend.1 = (bf16[32,2176]{1,0:T(8,128)(2,1)S(1)}, f32[32,2176]{1,0:T(8,128)S(1)}) custom-call(s32[8]{0:T(128)} %lens_hbm.1, bf16[1,64,512]{2,1,0:T(8,128)(2,1)} %q_hbm.1, bf16[1,2,512,128]{3,2,1,0:T(8,128)(2,1)} %kc_hbm.1, bf16[1,2,512,128]{3,2,1,0:T(8,128)(2,1)} %vc_hbm.1, bf16[1,64,128]{2,1,0:T(8,128)(2,1)} %kb_hbm.1, bf16[1,64,128]{2,1,0:T(8,128)(2,1)} %vb_hbm.1, ...), custom_call_target="tpu_custom_call" | custom-call | flops 1073741824 | bytes 8388608 | tf_op jit(solution)/shard_map/attend/pallas_call | solution.py:171
  3.5 0.6 %collective-permute-start = (bf16[32,2176]{1,0:T(8,128)(2,1)S(1)}, bf16[32,2176]{1,0:T(8,128)(2,1)S(1)}, u32[]{:S(2)}, u32[]{:S(2)}) collective-permute-start(bf16[32,2176]{1,0:T(8,128)(2,1)S(1)} %get-tuple-element.16), channel_id=1, source_target_pairs={{0,1},{1,0},{2,3},{3,2},{4,5},{5,4},{6,7},{7,6},{8,9},{9,8},{10,11... | collective-permute-start | bytes 417800 | tf_op jit(solution)/shard_map/ppermute | solution.py:27
  4.1 1.0 %collective-permute-done.core = bf16[32,2176]{1,0:T(8,128)(2,1)S(1)} collective-permute-done((bf16[32,2176]{1,0:T(8,128)(2,1)S(1)}, bf16[32,2176]{1,0:T(8,128)(2,1)S(1)}, u32[]{:S(2)}, u32[]{:S(2)}) %collective-permute-start) | collective-permute-done | bytes 139296 | tf_op jit(solution)/shard_map/ppermute | solution.py:27
  5.1 2.9 %collective-permute-start.1 = (bf16[16,2176]{1,0:T(8,128)(2,1)S(1)}, bf16[16,2176]{1,0:T(8,128)(2,1)S(1)}, u32[]{:S(2)}, u32[]{:S(2)}) collective-permute-start(bf16[16,2176]{1,0:T(8,128)(2,1)S(1)} %get-tuple-element.31), channel_id=1, source_target_pairs={{0,2},{1,3},{2,0},{3,1},{4,6},{5,7},{6,4},{7,5},{8,10},{9,11},{10,... | collective-permute-start | bytes 208904 | tf_op jit(solution)/shard_map/ppermute | solution.py:27
  8.0 0.1 collective-permute-start.2
  8.1 2.4 %collective-permute-done.1.chip = bf16[16,2176]{1,0:T(8,128)(2,1)S(1)} collective-permute-done((bf16[16,2176]{1,0:T(8,128)(2,1)S(1)}, bf16[16,2176]{1,0:T(8,128)(2,1)S(1)}, u32[]{:S(2)}, u32[]{:S(2)}) %collective-permute-start.1) | collective-permute-done | bytes 69664 | tf_op jit(solution)/shard_map/ppermute | solution.py:27
  10.5 0.1 norm.2
  10.7 3.3 %collective-permute-start.9 = (bf16[16,2176]{1,0:T(8,128)(2,1)S(1)}, bf16[16,2176]{1,0:T(8,128)(2,1)S(1)}, u32[]{:S(2)}, u32[]{:S(2)}) collective-permute-start(bf16[16,2176]{1,0:T(8,128)(2,1)S(1)} %get-tuple-element.18), channel_id=1, source_target_pairs={{0,8},{1,9},{2,10},{3,11},{4,12},{5,13},{6,14},{7,15},{8,0},{9,1},... | collective-permute-start | bytes 208904 | tf_op jit(solution)/shard_map/ppermute | solution.py:27
  14.0 0.1 norm.3
  14.2 2.0 %collective-permute-start.11 = (bf16[32,2176]{1,0:T(8,128)(2,1)S(1)}, bf16[32,2176]{1,0:T(8,128)(2,1)S(1)}, u32[]{:S(2)}, u32[]{:S(2)}) collective-permute-start(bf16[32,2176]{1,0:T(8,128)(2,1)S(1)} %pad_maximum_fusion.1), channel_id=1, source_target_pairs={{0,12},{1,13},{2,14},{3,15},{4,8},{5,9},{6,10},{7,11},{8,4},{9,5},... | collective-permute-start | bytes 417800 | tf_op jit(solution)/shard_map/ppermute | solution.py:27
  16.2 0.2 collective-permute-done.9
  16.4 5.0 %collective-permute-start.10 = (bf16[16,2176]{1,0:T(8,128)(2,1)S(1)}, bf16[16,2176]{1,0:T(8,128)(2,1)S(1)}, u32[]{:S(2)}, u32[]{:S(2)}) collective-permute-start(bf16[16,2176]{1,0:T(8,128)(2,1)S(1)} %collective-permute-done.9), channel_id=1, source_target_pairs={{0,2},{1,3},{2,0},{3,1},{4,6},{5,7},{6,4},{7,5},{8,10},{9,11},{10,... | collective-permute-start | bytes 208904 | tf_op jit(solution)/shard_map/ppermute | solution.py:27
  21.4 2.3 %collective-permute-done.10 = bf16[16,2176]{1,0:T(8,128)(2,1)S(1)} collective-permute-done((bf16[16,2176]{1,0:T(8,128)(2,1)S(1)}, bf16[16,2176]{1,0:T(8,128)(2,1)S(1)}, u32[]{:S(2)}, u32[]{:S(2)}) %collective-permute-start.10) | collective-permute-done | bytes 69664 | tf_op jit(solution)/shard_map/ppermute | solution.py:27
  23.7 0.1 collective-permute-start.12
  23.8 0.6 %collective-permute-start.4 = (bf16[64,2176]{1,0:T(8,128)(2,1)S(1)}, bf16[64,2176]{1,0:T(8,128)(2,1)S(1)}, u32[]{:S(2)}, u32[]{:S(2)}) collective-permute-start(bf16[64,2176]{1,0:T(8,128)(2,1)S(1)} %pad_maximum_fusion.mine), channel_id=1, source_target_pairs={{0,1},{1,0},{2,3},{3,2},{4,5},{5,4},{6,7},{7,6},{8,9},{9,8},{10,11... | collective-permute-start | bytes 835592 | tf_op jit(solution)/shard_map/ppermute | solution.py:27
  24.4 0.9 %collective-permute-done.12.other = bf16[64,2176]{1,0:T(8,128)(2,1)S(1)} collective-permute-done((bf16[64,2176]{1,0:T(8,128)(2,1)S(1)}, bf16[64,2176]{1,0:T(8,128)(2,1)S(1)}, u32[]{:S(2)}, u32[]{:S(2)}) %collective-permute-start.12) | collective-permute-done | bytes 278560 | tf_op jit(solution)/shard_map/ppermute | solution.py:27
  25.3 1.5 %expert.3 = (f32[64,2048]{1,0:T(8,128)S(1)}, bf16[64,2048]{1,0:T(8,128)(2,1)S(1)}) custom-call(bf16[64,2176]{1,0:T(8,128)(2,1)S(1)} %constant_dynamic-update-slice_fusion.mine, bf16[64,2176]{1,0:T(8,128)(2,1)S(1)} %collective-permute-done.12.other, bf16[1,2048,768]{2,1,0:T(8,128)(2,1)S(1)} %copy-done, bf16[1,2048,768]{2,1,0:T(8,128)(2,1)S(1)} %copy-done.1, ...), custom_call_target="tpu_custom_call" | custom-call | flops 1073741824 | bytes 8388608 | tf_op jit(solution)/shard_map/expert/pallas_call | solution.py:208
  26.8 0.2 collective-permute-start.13
  27.0 1.5 %expert.2 = (f32[64,2048]{1,0:T(8,128)S(1)}, bf16[64,2048]{1,0:T(8,128)(2,1)S(1)}) custom-call(bf16[64,2176]{1,0:T(8,128)(2,1)S(1)} %pad_maximum_fusion.mine, bf16[64,2176]{1,0:T(8,128)(2,1)S(1)} %collective-permute-done.4.other, bf16[1,2048,768]{2,1,0:T(8,128)(2,1)S(1)} %copy-done, bf16[1,2048,768]{2,1,0:T(8,128)(2,1)S(1)} %copy-done.1, ...), custom_call_target="tpu_custom_call" | custom-call | flops 1073741824 | bytes 8388608 | tf_op jit(solution)/shard_map/expert/pallas_call | solution.py:208
  28.5 0.4 collective-permute-start.5
  29.1 2.1 %collective-permute-start.14 = (bf16[16,2048]{1,0:T(8,128)(2,1)S(1)}, bf16[16,2048]{1,0:T(8,128)(2,1)S(1)}, u32[]{:S(2)}, u32[]{:S(2)}) collective-permute-start(bf16[16,2048]{1,0:T(8,128)(2,1)S(1)} %get-tuple-element.28), channel_id=1, source_target_pairs={{0,2},{1,3},{2,0},{3,1},{4,6},{5,7},{6,4},{7,5},{8,10},{9,11},{10,... | collective-permute-start | bytes 196616 | tf_op jit(solution)/shard_map/ppermute | solution.py:27
  31.1 0.1 collective-permute-start.16
  31.3 2.0 %collective-permute-start.6 = (bf16[16,2048]{1,0:T(8,128)(2,1)S(1)}, bf16[16,2048]{1,0:T(8,128)(2,1)S(1)}, u32[]{:S(2)}, u32[]{:S(2)}) collective-permute-start(bf16[16,2048]{1,0:T(8,128)(2,1)S(1)} %get-tuple-element.26), channel_id=1, source_target_pairs={{0,2},{1,3},{2,0},{3,1},{4,6},{5,7},{6,4},{7,5},{8,10},{9,11},{10,... | collective-permute-start | bytes 196616 | tf_op jit(solution)/shard_map/ppermute | solution.py:27
  33.3 0.1 collective-permute-start.7
  33.4 0.2 collective-permute-done.14
  33.6 1.6 %collective-permute-start.15 = (bf16[16,2048]{1,0:T(8,128)(2,1)S(1)}, bf16[16,2048]{1,0:T(8,128)(2,1)S(1)}, u32[]{:S(2)}, u32[]{:S(2)}) collective-permute-start(bf16[16,2048]{1,0:T(8,128)(2,1)S(1)} %fusion.1), channel_id=1, source_target_pairs={{0,8},{1,9},{2,10},{3,11},{4,12},{5,13},{6,14},{7,15},{8,0},{9,1},... | collective-permute-start | bytes 196616 | tf_op jit(solution)/shard_map/ppermute | solution.py:27
  35.2 0.9 %collective-permute-done.16.got = bf16[16,2048]{1,0:T(8,128)(2,1)S(1)} collective-permute-done((bf16[16,2048]{1,0:T(8,128)(2,1)S(1)}, bf16[16,2048]{1,0:T(8,128)(2,1)S(1)}, u32[]{:S(2)}, u32[]{:S(2)}) %collective-permute-start.16) | collective-permute-done | bytes 65568 | tf_op jit(solution)/shard_map/ppermute | solution.py:27
  36.1 4.7 %collective-permute-start.17 = (bf16[16,2048]{1,0:T(8,128)(2,1)S(1)}, bf16[16,2048]{1,0:T(8,128)(2,1)S(1)}, u32[]{:S(2)}, u32[]{:S(2)}) collective-permute-start(bf16[16,2048]{1,0:T(8,128)(2,1)S(1)} %acrosssum.1), channel_id=1, source_target_pairs={{0,12},{1,13},{2,14},{3,15},{4,8},{5,9},{6,10},{7,11},{8,4},{9,5},... | collective-permute-start | bytes 196616 | tf_op jit(solution)/shard_map/ppermute | solution.py:27
  40.9 0.6 %copy.18 = bf16[16,2048]{1,0:T(8,128)(2,1)} copy(bf16[16,2048]{1,0:T(8,128)(2,1)S(1)} %get-tuple-element.32) | data formatting | bytes 131072
  41.5 1.6 %collective-permute-done.17 = bf16[16,2048]{1,0:T(8,128)(2,1)S(1)} collective-permute-done((bf16[16,2048]{1,0:T(8,128)(2,1)S(1)}, bf16[16,2048]{1,0:T(8,128)(2,1)S(1)}, u32[]{:S(2)}, u32[]{:S(2)}) %collective-permute-start.17) | collective-permute-done | bytes 65568 | tf_op jit(solution)/shard_map/ppermute | solution.py:27
  43.2 2.0 %collective-permute-done.8 = bf16[16,2048]{1,0:T(8,128)(2,1)S(1)} collective-permute-done((bf16[16,2048]{1,0:T(8,128)(2,1)S(1)}, bf16[16,2048]{1,0:T(8,128)(2,1)S(1)}, u32[]{:S(2)}, u32[]{:S(2)}) %collective-permute-start.8) | collective-permute-done | bytes 65568 | tf_op jit(solution)/shard_map/ppermute | solution.py:27
  45.1 0.7 %fusion.8 = bf16[16,2048]{1,0:T(8,128)(2,1)} fusion(f32[2,2,16,2048]{3,2,1,0:T(8,128)S(1)} %bitcast.44, bf16[16,2048]{1,0:T(8,128)(2,1)S(1)} %collective-permute-done.17, bf16[16,2048]{1,0:T(8,128)(2,1)S(1)} %collective-permute-done.15, bf16[16,2048]{1,0:T(8,128)(2,1)S(1)} %collective-permute-done.8, bf16[16,2048]{1,0:T(8,128)(2,1)S(1)} %collective-permute-done.6), kind=kLoop, calls=%fused_computation.16 | loop fusion | flops 294912 | bytes 458752 | tf_op jit(solution)/shard_map/convert_element_type | solution.py:259
  (35 shorter events, 0.5 us)
Async XLA Ops:
  0.6 9.9 %copy-start.3 = (f32[2048]{0:T(1024)S(1)}, f32[2048]{0:T(1024)}, u32[]{:S(2)}) copy-start(f32[2048]{0:T(1024)} %param.22) | copy-start | bytes 24580
  3.5 1.6 %collective-permute-start = (bf16[32,2176]{1,0:T(8,128)(2,1)S(1)}, bf16[32,2176]{1,0:T(8,128)(2,1)S(1)}, u32[]{:S(2)}, u32[]{:S(2)}) collective-permute-start(bf16[32,2176]{1,0:T(8,128)(2,1)S(1)} %get-tuple-element.16), channel_id=1, source_target_pairs={{0,1},{1,0},{2,3},{3,2},{4,5},{5,4},{6,7},{7,6},{8,9},{9,8},{10,11... | collective-permute-start | bytes 417800 | tf_op jit(solution)/shard_map/ppermute | solution.py:27
  5.1 5.4 %collective-permute-start.1 = (bf16[16,2176]{1,0:T(8,128)(2,1)S(1)}, bf16[16,2176]{1,0:T(8,128)(2,1)S(1)}, u32[]{:S(2)}, u32[]{:S(2)}) collective-permute-start(bf16[16,2176]{1,0:T(8,128)(2,1)S(1)} %get-tuple-element.31), channel_id=1, source_target_pairs={{0,2},{1,3},{2,0},{3,1},{4,6},{5,7},{6,4},{7,5},{8,10},{9,11},{10,... | collective-permute-start | bytes 208904 | tf_op jit(solution)/shard_map/ppermute | solution.py:27
  8.0 6.0 %collective-permute-start.2 = (bf16[16,2176]{1,0:T(8,128)(2,1)S(1)}, bf16[16,2176]{1,0:T(8,128)(2,1)S(1)}, u32[]{:S(2)}, u32[]{:S(2)}) collective-permute-start(bf16[16,2176]{1,0:T(8,128)(2,1)S(1)} %get-tuple-element.30), channel_id=1, source_target_pairs={{0,2},{1,3},{2,0},{3,1},{4,6},{5,7},{6,4},{7,5},{8,10},{9,11},{10,... | collective-permute-start | bytes 208904 | tf_op jit(solution)/shard_map/ppermute | solution.py:27
  10.7 5.7 %collective-permute-start.9 = (bf16[16,2176]{1,0:T(8,128)(2,1)S(1)}, bf16[16,2176]{1,0:T(8,128)(2,1)S(1)}, u32[]{:S(2)}, u32[]{:S(2)}) collective-permute-start(bf16[16,2176]{1,0:T(8,128)(2,1)S(1)} %get-tuple-element.18), channel_id=1, source_target_pairs={{0,8},{1,9},{2,10},{3,11},{4,12},{5,13},{6,14},{7,15},{8,0},{9,1},... | collective-permute-start | bytes 208904 | tf_op jit(solution)/shard_map/ppermute | solution.py:27
  14.0 11.3 %copy-start = (bf16[1,2048,768]{2,1,0:T(8,128)(2,1)S(1)}, bf16[1,2048,768]{2,1,0:T(8,128)(2,1)}, u32[]{:S(2)}) copy-start(bf16[1,2048,768]{2,1,0:T(8,128)(2,1)} %w_gate.1) | copy-start | bytes 9437188
  14.0 11.3 %copy-start.1 = (bf16[1,2048,768]{2,1,0:T(8,128)(2,1)S(1)}, bf16[1,2048,768]{2,1,0:T(8,128)(2,1)}, u32[]{:S(2)}) copy-start(bf16[1,2048,768]{2,1,0:T(8,128)(2,1)} %w_up.1) | copy-start | bytes 9437188
  14.0 11.3 %copy-start.2 = (bf16[1,768,2048]{2,1,0:T(8,128)(2,1)S(1)}, bf16[1,768,2048]{2,1,0:T(8,128)(2,1)}, u32[]{:S(2)}) copy-start(bf16[1,768,2048]{2,1,0:T(8,128)(2,1)} %w_down.1) | copy-start | bytes 9437188
  14.2 9.5 %collective-permute-start.11 = (bf16[32,2176]{1,0:T(8,128)(2,1)S(1)}, bf16[32,2176]{1,0:T(8,128)(2,1)S(1)}, u32[]{:S(2)}, u32[]{:S(2)}) collective-permute-start(bf16[32,2176]{1,0:T(8,128)(2,1)S(1)} %pad_maximum_fusion.1), channel_id=1, source_target_pairs={{0,12},{1,13},{2,14},{3,15},{4,8},{5,9},{6,10},{7,11},{8,4},{9,5},... | collective-permute-start | bytes 417800 | tf_op jit(solution)/shard_map/ppermute | solution.py:27
  16.2 7.6 %collective-permute-start.3 = (bf16[32,2176]{1,0:T(8,128)(2,1)S(1)}, bf16[32,2176]{1,0:T(8,128)(2,1)S(1)}, u32[]{:S(2)}, u32[]{:S(2)}) collective-permute-start(bf16[32,2176]{1,0:T(8,128)(2,1)S(1)} %pad_maximum_fusion.1), channel_id=1, source_target_pairs={{0,4},{1,5},{2,6},{3,7},{4,0},{5,1},{6,2},{7,3},{8,12},{9,13},{10,... | collective-permute-start | bytes 417800 | tf_op jit(solution)/shard_map/ppermute | solution.py:27
  16.4 7.3 %collective-permute-start.10 = (bf16[16,2176]{1,0:T(8,128)(2,1)S(1)}, bf16[16,2176]{1,0:T(8,128)(2,1)S(1)}, u32[]{:S(2)}, u32[]{:S(2)}) collective-permute-start(bf16[16,2176]{1,0:T(8,128)(2,1)S(1)} %collective-permute-done.9), channel_id=1, source_target_pairs={{0,2},{1,3},{2,0},{3,1},{4,6},{5,7},{6,4},{7,5},{8,10},{9,11},{10,... | collective-permute-start | bytes 208904 | tf_op jit(solution)/shard_map/ppermute | solution.py:27
  23.7 1.6 %collective-permute-start.12 = (bf16[64,2176]{1,0:T(8,128)(2,1)S(1)}, bf16[64,2176]{1,0:T(8,128)(2,1)S(1)}, u32[]{:S(2)}, u32[]{:S(2)}) collective-permute-start(bf16[64,2176]{1,0:T(8,128)(2,1)S(1)} %constant_dynamic-update-slice_fusion.mine), channel_id=1, source_target_pairs={{0,1},{1,0},{2,3},{3,2},{4,5},{5,4},{6,7},{7,6},{8,9},{9,8},{10,11... | collective-permute-start | bytes 835592 | tf_op jit(solution)/shard_map/ppermute | solution.py:27
  23.8 3.2 %collective-permute-start.4 = (bf16[64,2176]{1,0:T(8,128)(2,1)S(1)}, bf16[64,2176]{1,0:T(8,128)(2,1)S(1)}, u32[]{:S(2)}, u32[]{:S(2)}) collective-permute-start(bf16[64,2176]{1,0:T(8,128)(2,1)S(1)} %pad_maximum_fusion.mine), channel_id=1, source_target_pairs={{0,1},{1,0},{2,3},{3,2},{4,5},{5,4},{6,7},{7,6},{8,9},{9,8},{10,11... | collective-permute-start | bytes 835592 | tf_op jit(solution)/shard_map/ppermute | solution.py:27
  26.8 2.1 %collective-permute-start.13 = (bf16[64,2048]{1,0:T(8,128)(2,1)S(1)}, bf16[64,2048]{1,0:T(8,128)(2,1)S(1)}, u32[]{:S(2)}, u32[]{:S(2)}) collective-permute-start(bf16[64,2048]{1,0:T(8,128)(2,1)S(1)} %get-tuple-element.25), channel_id=1, source_target_pairs={{0,1},{1,0},{2,3},{3,2},{4,5},{5,4},{6,7},{7,6},{8,9},{9,8},{10,11... | collective-permute-start | bytes 786440 | tf_op jit(solution)/shard_map/ppermute | solution.py:27
  28.5 2.7 %collective-permute-start.5 = (bf16[64,2048]{1,0:T(8,128)(2,1)S(1)}, bf16[64,2048]{1,0:T(8,128)(2,1)S(1)}, u32[]{:S(2)}, u32[]{:S(2)}) collective-permute-start(bf16[64,2048]{1,0:T(8,128)(2,1)S(1)} %get-tuple-element.23), channel_id=1, source_target_pairs={{0,1},{1,0},{2,3},{3,2},{4,5},{5,4},{6,7},{7,6},{8,9},{9,8},{10,11... | collective-permute-start | bytes 786440 | tf_op jit(solution)/shard_map/ppermute | solution.py:27
  29.1 4.6 %collective-permute-start.14 = (bf16[16,2048]{1,0:T(8,128)(2,1)S(1)}, bf16[16,2048]{1,0:T(8,128)(2,1)S(1)}, u32[]{:S(2)}, u32[]{:S(2)}) collective-permute-start(bf16[16,2048]{1,0:T(8,128)(2,1)S(1)} %get-tuple-element.28), channel_id=1, source_target_pairs={{0,2},{1,3},{2,0},{3,1},{4,6},{5,7},{6,4},{7,5},{8,10},{9,11},{10,... | collective-permute-start | bytes 196616 | tf_op jit(solution)/shard_map/ppermute | solution.py:27
  31.1 5.0 %collective-permute-start.16 = (bf16[16,2048]{1,0:T(8,128)(2,1)S(1)}, bf16[16,2048]{1,0:T(8,128)(2,1)S(1)}, u32[]{:S(2)}, u32[]{:S(2)}) collective-permute-start(bf16[16,2048]{1,0:T(8,128)(2,1)S(1)} %get-tuple-element.29), channel_id=1, source_target_pairs={{0,2},{1,3},{2,0},{3,1},{4,6},{5,7},{6,4},{7,5},{8,10},{9,11},{10,... | collective-permute-start | bytes 196616 | tf_op jit(solution)/shard_map/ppermute | solution.py:27
  31.3 10.2 %collective-permute-start.6 = (bf16[16,2048]{1,0:T(8,128)(2,1)S(1)}, bf16[16,2048]{1,0:T(8,128)(2,1)S(1)}, u32[]{:S(2)}, u32[]{:S(2)}) collective-permute-start(bf16[16,2048]{1,0:T(8,128)(2,1)S(1)} %get-tuple-element.26), channel_id=1, source_target_pairs={{0,2},{1,3},{2,0},{3,1},{4,6},{5,7},{6,4},{7,5},{8,10},{9,11},{10,... | collective-permute-start | bytes 196616 | tf_op jit(solution)/shard_map/ppermute | solution.py:27
  33.3 7.5 %collective-permute-start.7 = (bf16[16,2048]{1,0:T(8,128)(2,1)S(1)}, bf16[16,2048]{1,0:T(8,128)(2,1)S(1)}, u32[]{:S(2)}, u32[]{:S(2)}) collective-permute-start(bf16[16,2048]{1,0:T(8,128)(2,1)S(1)} %get-tuple-element.27), channel_id=1, source_target_pairs={{0,2},{1,3},{2,0},{3,1},{4,6},{5,7},{6,4},{7,5},{8,10},{9,11},{10,... | collective-permute-start | bytes 196616 | tf_op jit(solution)/shard_map/ppermute | solution.py:27
  33.6 7.9 %collective-permute-start.15 = (bf16[16,2048]{1,0:T(8,128)(2,1)S(1)}, bf16[16,2048]{1,0:T(8,128)(2,1)S(1)}, u32[]{:S(2)}, u32[]{:S(2)}) collective-permute-start(bf16[16,2048]{1,0:T(8,128)(2,1)S(1)} %fusion.1), channel_id=1, source_target_pairs={{0,8},{1,9},{2,10},{3,11},{4,12},{5,13},{6,14},{7,15},{8,0},{9,1},... | collective-permute-start | bytes 196616 | tf_op jit(solution)/shard_map/ppermute | solution.py:27
  36.1 7.0 %collective-permute-start.17 = (bf16[16,2048]{1,0:T(8,128)(2,1)S(1)}, bf16[16,2048]{1,0:T(8,128)(2,1)S(1)}, u32[]{:S(2)}, u32[]{:S(2)}) collective-permute-start(bf16[16,2048]{1,0:T(8,128)(2,1)S(1)} %acrosssum.1), channel_id=1, source_target_pairs={{0,12},{1,13},{2,14},{3,15},{4,8},{5,9},{6,10},{7,11},{8,4},{9,5},... | collective-permute-start | bytes 196616 | tf_op jit(solution)/shard_map/ppermute | solution.py:27
  40.8 4.3 %collective-permute-start.8 = (bf16[16,2048]{1,0:T(8,128)(2,1)S(1)}, bf16[16,2048]{1,0:T(8,128)(2,1)S(1)}, u32[]{:S(2)}, u32[]{:S(2)}) collective-permute-start(bf16[16,2048]{1,0:T(8,128)(2,1)S(1)} %fusion.3), channel_id=1, source_target_pairs={{0,4},{1,5},{2,6},{3,7},{4,0},{5,1},{6,2},{7,3},{8,12},{9,13},{10,... | collective-permute-start | bytes 196616 | tf_op jit(solution)/shard_map/ppermute | solution.py:27

commit v3 on v2

--- a/solution.py
+++ b/solution.py
@@ -147,7 +147,7 @@
 
 
 def sum_kernel(sums, got, out):
-    out[...] = (sums[1, 0] + got[...].astype(jnp.float32)).astype(jnp.bfloat16)
+    out[...] = (sums[0, 0] + got[...].astype(jnp.float32)).astype(jnp.bfloat16)
 
 
 def every_row(
@@ -241,20 +241,20 @@
     summed = sums[0, 0] + got_own.astype(jnp.float32)
     near = exchanged(near_sum, 4)
     sums = expert(jnp.concatenate([far, passed, across], 0))
+    got_far = exchanged(sums[0, 1].astype(jnp.bfloat16), 2)
     got_across = exchanged(sums[1, 1].astype(jnp.bfloat16), 2)
-    got_far = exchanged(sums[0, 1].astype(jnp.bfloat16), 2)
-    across_sum = pl.pallas_call(
+    far_sum = pl.pallas_call(
         sum_kernel,
         out_shape=jax.ShapeDtypeStruct((rows, MODEL_WIDTH), jnp.bfloat16),
         in_specs=[whole] * 2,
         out_specs=whole,
         compiler_params=pltpu.CompilerParams(vmem_limit_bytes=4 << 20),
         cost_estimate=pl.CostEstimate(flops=1 << 16, bytes_accessed=1 << 18, transcendentals=0),
-        name="acrosssum",
-    )(sums, got_across)
+        name="farsum",
+    )(sums, got_far)
+    far = exchanged(far_sum, 8)
+    across_sum = (sums[1, 0] + got_across.astype(jnp.float32)).astype(jnp.bfloat16)
     across = exchanged(across_sum, 12)
-    far_sum = (sums[0, 0] + got_far.astype(jnp.float32)).astype(jnp.bfloat16)
-    far = exchanged(far_sum, 8)
     summed = summed + near.astype(jnp.float32) + far.astype(jnp.float32) + across.astype(jnp.float32)
     return (attended, summed.astype(jnp.bfloat16))
 

time: 46 us -> 46 us (level)
  no operation moved by 1% of the time
where the time goes in v3:
time: 46 us; the launch traced here: 45.8 us
  starting transfers between devices  25.7 us (56%)
  waiting for transfers between devices  11.6 us (25%)
  Pallas kernels  6.08 us (13%)
  other arithmetic  0.94 us (2%)
  between operations  0.8 us (2%)
  local copies, waits for them, and re-layouts  0.72 us (2%)
    ppermute x18, starting transfers between devices, exchanged(): lax.ppermute(block, 'ep', [(index, index ^ mask) for index in range(count)])  25.7 us
    ppermute x18, waiting for transfers between devices, exchanged(): lax.ppermute(block, 'ep', [(index, index ^ mask) for index in range(count)])  11.6 us
    pallas_call x2, Pallas kernels, expert(): pl.pallas_call(expert_kernel, out_shape=(jax.ShapeDtypeStruct((half, MODE...  2.95 us
    pallas_call x1, Pallas kernels, every_row(): pl.pallas_call(attend_kernel, out_shape=(jax.ShapeDtypeStruct((2 * rows,...  2.86 us
  transfers between devices with their start and end apart: 18, of which 9 were waited for; matrix products, arithmetic and copies ran while one was open for 2% of the time, Pallas kernels for 7%

profile of v3, /device:TPU:0, one launch (start us, length us, event | category | flops | bytes accessed | tf_op | source)
XLA Modules:
  0.0 45.8 jit_solution(13936853885601121778)
XLA Ops:
  0.6 2.9 %attend.1 = (bf16[32,2176]{1,0:T(8,128)(2,1)S(1)}, f32[32,2176]{1,0:T(8,128)S(1)}) custom-call(s32[8]{0:T(128)} %lens_hbm.1, bf16[1,64,512]{2,1,0:T(8,128)(2,1)} %q_hbm.1, bf16[1,2,512,128]{3,2,1,0:T(8,128)(2,1)} %kc_hbm.1, bf16[1,2,512,128]{3,2,1,0:T(8,128)(2,1)} %vc_hbm.1, bf16[1,64,128]{2,1,0:T(8,128)(2,1)} %kb_hbm.1, bf16[1,64,128]{2,1,0:T(8,128)(2,1)} %vb_hbm.1, ...), custom_call_target="tpu_custom_call" | custom-call | flops 1073741824 | bytes 8388608 | tf_op jit(solution)/shard_map/attend/pallas_call | solution.py:171
  3.5 0.6 %collective-permute-start = (bf16[32,2176]{1,0:T(8,128)(2,1)S(1)}, bf16[32,2176]{1,0:T(8,128)(2,1)S(1)}, u32[]{:S(2)}, u32[]{:S(2)}) collective-permute-start(bf16[32,2176]{1,0:T(8,128)(2,1)S(1)} %get-tuple-element.16), channel_id=1, source_target_pairs={{0,1},{1,0},{2,3},{3,2},{4,5},{5,4},{6,7},{7,6},{8,9},{9,8},{10,11... | collective-permute-start | bytes 417800 | tf_op jit(solution)/shard_map/ppermute | solution.py:27
  4.1 1.0 %collective-permute-done.core = bf16[32,2176]{1,0:T(8,128)(2,1)S(1)} collective-permute-done((bf16[32,2176]{1,0:T(8,128)(2,1)S(1)}, bf16[32,2176]{1,0:T(8,128)(2,1)S(1)}, u32[]{:S(2)}, u32[]{:S(2)}) %collective-permute-start) | collective-permute-done | bytes 139296 | tf_op jit(solution)/shard_map/ppermute | solution.py:27
  5.1 2.9 %collective-permute-start.1 = (bf16[16,2176]{1,0:T(8,128)(2,1)S(1)}, bf16[16,2176]{1,0:T(8,128)(2,1)S(1)}, u32[]{:S(2)}, u32[]{:S(2)}) collective-permute-start(bf16[16,2176]{1,0:T(8,128)(2,1)S(1)} %get-tuple-element.31), channel_id=1, source_target_pairs={{0,2},{1,3},{2,0},{3,1},{4,6},{5,7},{6,4},{7,5},{8,10},{9,11},{10,... | collective-permute-start | bytes 208904 | tf_op jit(solution)/shard_map/ppermute | solution.py:27
  8.0 0.1 collective-permute-start.2
  8.1 2.4 %collective-permute-done.1.chip = bf16[16,2176]{1,0:T(8,128)(2,1)S(1)} collective-permute-done((bf16[16,2176]{1,0:T(8,128)(2,1)S(1)}, bf16[16,2176]{1,0:T(8,128)(2,1)S(1)}, u32[]{:S(2)}, u32[]{:S(2)}) %collective-permute-start.1) | collective-permute-done | bytes 69664 | tf_op jit(solution)/shard_map/ppermute | solution.py:27
  10.5 0.1 norm.2
  10.7 3.3 %collective-permute-start.9 = (bf16[16,2176]{1,0:T(8,128)(2,1)S(1)}, bf16[16,2176]{1,0:T(8,128)(2,1)S(1)}, u32[]{:S(2)}, u32[]{:S(2)}) collective-permute-start(bf16[16,2176]{1,0:T(8,128)(2,1)S(1)} %get-tuple-element.18), channel_id=1, source_target_pairs={{0,8},{1,9},{2,10},{3,11},{4,12},{5,13},{6,14},{7,15},{8,0},{9,1},... | collective-permute-start | bytes 208904 | tf_op jit(solution)/shard_map/ppermute | solution.py:27
  14.0 0.1 norm.3
  14.2 2.0 %collective-permute-start.11 = (bf16[32,2176]{1,0:T(8,128)(2,1)S(1)}, bf16[32,2176]{1,0:T(8,128)(2,1)S(1)}, u32[]{:S(2)}, u32[]{:S(2)}) collective-permute-start(bf16[32,2176]{1,0:T(8,128)(2,1)S(1)} %pad_maximum_fusion.1), channel_id=1, source_target_pairs={{0,12},{1,13},{2,14},{3,15},{4,8},{5,9},{6,10},{7,11},{8,4},{9,5},... | collective-permute-start | bytes 417800 | tf_op jit(solution)/shard_map/ppermute | solution.py:27
  16.2 0.2 collective-permute-done.9
  16.4 5.0 %collective-permute-start.10 = (bf16[16,2176]{1,0:T(8,128)(2,1)S(1)}, bf16[16,2176]{1,0:T(8,128)(2,1)S(1)}, u32[]{:S(2)}, u32[]{:S(2)}) collective-permute-start(bf16[16,2176]{1,0:T(8,128)(2,1)S(1)} %collective-permute-done.9), channel_id=1, source_target_pairs={{0,2},{1,3},{2,0},{3,1},{4,6},{5,7},{6,4},{7,5},{8,10},{9,11},{10,... | collective-permute-start | bytes 208904 | tf_op jit(solution)/shard_map/ppermute | solution.py:27
  21.4 2.3 %collective-permute-done.10 = bf16[16,2176]{1,0:T(8,128)(2,1)S(1)} collective-permute-done((bf16[16,2176]{1,0:T(8,128)(2,1)S(1)}, bf16[16,2176]{1,0:T(8,128)(2,1)S(1)}, u32[]{:S(2)}, u32[]{:S(2)}) %collective-permute-start.10) | collective-permute-done | bytes 69664 | tf_op jit(solution)/shard_map/ppermute | solution.py:27
  23.7 0.1 collective-permute-start.12
  23.8 0.6 %collective-permute-start.4 = (bf16[64,2176]{1,0:T(8,128)(2,1)S(1)}, bf16[64,2176]{1,0:T(8,128)(2,1)S(1)}, u32[]{:S(2)}, u32[]{:S(2)}) collective-permute-start(bf16[64,2176]{1,0:T(8,128)(2,1)S(1)} %pad_maximum_fusion.mine), channel_id=1, source_target_pairs={{0,1},{1,0},{2,3},{3,2},{4,5},{5,4},{6,7},{7,6},{8,9},{9,8},{10,11... | collective-permute-start | bytes 835592 | tf_op jit(solution)/shard_map/ppermute | solution.py:27
  24.4 0.9 %collective-permute-done.12.other = bf16[64,2176]{1,0:T(8,128)(2,1)S(1)} collective-permute-done((bf16[64,2176]{1,0:T(8,128)(2,1)S(1)}, bf16[64,2176]{1,0:T(8,128)(2,1)S(1)}, u32[]{:S(2)}, u32[]{:S(2)}) %collective-permute-start.12) | collective-permute-done | bytes 278560 | tf_op jit(solution)/shard_map/ppermute | solution.py:27
  25.3 1.5 %expert.3 = (f32[64,2048]{1,0:T(8,128)S(1)}, bf16[64,2048]{1,0:T(8,128)(2,1)S(1)}) custom-call(bf16[64,2176]{1,0:T(8,128)(2,1)S(1)} %constant_dynamic-update-slice_fusion.mine, bf16[64,2176]{1,0:T(8,128)(2,1)S(1)} %collective-permute-done.12.other, bf16[1,2048,768]{2,1,0:T(8,128)(2,1)S(1)} %copy-done, bf16[1,2048,768]{2,1,0:T(8,128)(2,1)S(1)} %copy-done.1, ...), custom_call_target="tpu_custom_call" | custom-call | flops 1073741824 | bytes 8388608 | tf_op jit(solution)/shard_map/expert/pallas_call | solution.py:208
  26.8 0.2 collective-permute-start.13
  27.0 1.5 %expert.2 = (f32[64,2048]{1,0:T(8,128)S(1)}, bf16[64,2048]{1,0:T(8,128)(2,1)S(1)}) custom-call(bf16[64,2176]{1,0:T(8,128)(2,1)S(1)} %pad_maximum_fusion.mine, bf16[64,2176]{1,0:T(8,128)(2,1)S(1)} %collective-permute-done.4.other, bf16[1,2048,768]{2,1,0:T(8,128)(2,1)S(1)} %copy-done, bf16[1,2048,768]{2,1,0:T(8,128)(2,1)S(1)} %copy-done.1, ...), custom_call_target="tpu_custom_call" | custom-call | flops 1073741824 | bytes 8388608 | tf_op jit(solution)/shard_map/expert/pallas_call | solution.py:208
  28.5 0.4 collective-permute-start.5
  29.1 2.1 %collective-permute-start.14 = (bf16[16,2048]{1,0:T(8,128)(2,1)S(1)}, bf16[16,2048]{1,0:T(8,128)(2,1)S(1)}, u32[]{:S(2)}, u32[]{:S(2)}) collective-permute-start(bf16[16,2048]{1,0:T(8,128)(2,1)S(1)} %get-tuple-element.28), channel_id=1, source_target_pairs={{0,2},{1,3},{2,0},{3,1},{4,6},{5,7},{6,4},{7,5},{8,10},{9,11},{10,... | collective-permute-start | bytes 196616 | tf_op jit(solution)/shard_map/ppermute | solution.py:27
  31.1 0.1 collective-permute-start.16
  31.3 2.0 %collective-permute-start.6 = (bf16[16,2048]{1,0:T(8,128)(2,1)S(1)}, bf16[16,2048]{1,0:T(8,128)(2,1)S(1)}, u32[]{:S(2)}, u32[]{:S(2)}) collective-permute-start(bf16[16,2048]{1,0:T(8,128)(2,1)S(1)} %get-tuple-element.26), channel_id=1, source_target_pairs={{0,2},{1,3},{2,0},{3,1},{4,6},{5,7},{6,4},{7,5},{8,10},{9,11},{10,... | collective-permute-start | bytes 196616 | tf_op jit(solution)/shard_map/ppermute | solution.py:27
  33.3 0.1 collective-permute-start.7
  33.4 0.2 collective-permute-done.14.got
  33.6 1.6 %collective-permute-start.15 = (bf16[16,2048]{1,0:T(8,128)(2,1)S(1)}, bf16[16,2048]{1,0:T(8,128)(2,1)S(1)}, u32[]{:S(2)}, u32[]{:S(2)}) collective-permute-start(bf16[16,2048]{1,0:T(8,128)(2,1)S(1)} %farsum.1), channel_id=1, source_target_pairs={{0,8},{1,9},{2,10},{3,11},{4,12},{5,13},{6,14},{7,15},{8,0},{9,1},... | collective-permute-start | bytes 196616 | tf_op jit(solution)/shard_map/ppermute | solution.py:27
  35.2 0.9 %collective-permute-done.16 = bf16[16,2048]{1,0:T(8,128)(2,1)S(1)} collective-permute-done((bf16[16,2048]{1,0:T(8,128)(2,1)S(1)}, bf16[16,2048]{1,0:T(8,128)(2,1)S(1)}, u32[]{:S(2)}, u32[]{:S(2)}) %collective-permute-start.16) | collective-permute-done | bytes 65568 | tf_op jit(solution)/shard_map/ppermute | solution.py:27
  36.1 4.7 %collective-permute-start.17 = (bf16[16,2048]{1,0:T(8,128)(2,1)S(1)}, bf16[16,2048]{1,0:T(8,128)(2,1)S(1)}, u32[]{:S(2)}, u32[]{:S(2)}) collective-permute-start(bf16[16,2048]{1,0:T(8,128)(2,1)S(1)} %fusion.1), channel_id=1, source_target_pairs={{0,12},{1,13},{2,14},{3,15},{4,8},{5,9},{6,10},{7,11},{8,4},{9,5},... | collective-permute-start | bytes 196616 | tf_op jit(solution)/shard_map/ppermute | solution.py:27
  40.9 0.6 %copy.18 = bf16[16,2048]{1,0:T(8,128)(2,1)} copy(bf16[16,2048]{1,0:T(8,128)(2,1)S(1)} %get-tuple-element.32) | data formatting | bytes 131072
  41.5 1.6 %collective-permute-done.17 = bf16[16,2048]{1,0:T(8,128)(2,1)S(1)} collective-permute-done((bf16[16,2048]{1,0:T(8,128)(2,1)S(1)}, bf16[16,2048]{1,0:T(8,128)(2,1)S(1)}, u32[]{:S(2)}, u32[]{:S(2)}) %collective-permute-start.17) | collective-permute-done | bytes 65568 | tf_op jit(solution)/shard_map/ppermute | solution.py:27
  43.2 2.0 %collective-permute-done.8 = bf16[16,2048]{1,0:T(8,128)(2,1)S(1)} collective-permute-done((bf16[16,2048]{1,0:T(8,128)(2,1)S(1)}, bf16[16,2048]{1,0:T(8,128)(2,1)S(1)}, u32[]{:S(2)}, u32[]{:S(2)}) %collective-permute-start.8) | collective-permute-done | bytes 65568 | tf_op jit(solution)/shard_map/ppermute | solution.py:27
  45.1 0.7 %fusion.8 = bf16[16,2048]{1,0:T(8,128)(2,1)} fusion(f32[2,2,16,2048]{3,2,1,0:T(8,128)S(1)} %bitcast.44, bf16[16,2048]{1,0:T(8,128)(2,1)S(1)} %collective-permute-done.17, bf16[16,2048]{1,0:T(8,128)(2,1)S(1)} %collective-permute-done.15, bf16[16,2048]{1,0:T(8,128)(2,1)S(1)} %collective-permute-done.8, bf16[16,2048]{1,0:T(8,128)(2,1)S(1)} %collective-permute-done.6), kind=kLoop, calls=%fused_computation.16 | loop fusion | flops 294912 | bytes 458752 | tf_op jit(solution)/shard_map/convert_element_type | solution.py:259
  (35 shorter events, 0.5 us)
Async XLA Ops:
  0.6 9.9 %copy-start.3 = (f32[2048]{0:T(1024)S(1)}, f32[2048]{0:T(1024)}, u32[]{:S(2)}) copy-start(f32[2048]{0:T(1024)} %param.22) | copy-start | bytes 24580
  3.5 1.6 %collective-permute-start = (bf16[32,2176]{1,0:T(8,128)(2,1)S(1)}, bf16[32,2176]{1,0:T(8,128)(2,1)S(1)}, u32[]{:S(2)}, u32[]{:S(2)}) collective-permute-start(bf16[32,2176]{1,0:T(8,128)(2,1)S(1)} %get-tuple-element.16), channel_id=1, source_target_pairs={{0,1},{1,0},{2,3},{3,2},{4,5},{5,4},{6,7},{7,6},{8,9},{9,8},{10,11... | collective-permute-start | bytes 417800 | tf_op jit(solution)/shard_map/ppermute | solution.py:27
  5.1 5.4 %collective-permute-start.1 = (bf16[16,2176]{1,0:T(8,128)(2,1)S(1)}, bf16[16,2176]{1,0:T(8,128)(2,1)S(1)}, u32[]{:S(2)}, u32[]{:S(2)}) collective-permute-start(bf16[16,2176]{1,0:T(8,128)(2,1)S(1)} %get-tuple-element.31), channel_id=1, source_target_pairs={{0,2},{1,3},{2,0},{3,1},{4,6},{5,7},{6,4},{7,5},{8,10},{9,11},{10,... | collective-permute-start | bytes 208904 | tf_op jit(solution)/shard_map/ppermute | solution.py:27
  8.0 6.0 %collective-permute-start.2 = (bf16[16,2176]{1,0:T(8,128)(2,1)S(1)}, bf16[16,2176]{1,0:T(8,128)(2,1)S(1)}, u32[]{:S(2)}, u32[]{:S(2)}) collective-permute-start(bf16[16,2176]{1,0:T(8,128)(2,1)S(1)} %get-tuple-element.30), channel_id=1, source_target_pairs={{0,2},{1,3},{2,0},{3,1},{4,6},{5,7},{6,4},{7,5},{8,10},{9,11},{10,... | collective-permute-start | bytes 208904 | tf_op jit(solution)/shard_map/ppermute | solution.py:27
  10.7 5.7 %collective-permute-start.9 = (bf16[16,2176]{1,0:T(8,128)(2,1)S(1)}, bf16[16,2176]{1,0:T(8,128)(2,1)S(1)}, u32[]{:S(2)}, u32[]{:S(2)}) collective-permute-start(bf16[16,2176]{1,0:T(8,128)(2,1)S(1)} %get-tuple-element.18), channel_id=1, source_target_pairs={{0,8},{1,9},{2,10},{3,11},{4,12},{5,13},{6,14},{7,15},{8,0},{9,1},... | collective-permute-start | bytes 208904 | tf_op jit(solution)/shard_map/ppermute | solution.py:27
  14.0 11.3 %copy-start = (bf16[1,2048,768]{2,1,0:T(8,128)(2,1)S(1)}, bf16[1,2048,768]{2,1,0:T(8,128)(2,1)}, u32[]{:S(2)}) copy-start(bf16[1,2048,768]{2,1,0:T(8,128)(2,1)} %w_gate.1) | copy-start | bytes 9437188
  14.0 11.3 %copy-start.1 = (bf16[1,2048,768]{2,1,0:T(8,128)(2,1)S(1)}, bf16[1,2048,768]{2,1,0:T(8,128)(2,1)}, u32[]{:S(2)}) copy-start(bf16[1,2048,768]{2,1,0:T(8,128)(2,1)} %w_up.1) | copy-start | bytes 9437188
  14.0 11.3 %copy-start.2 = (bf16[1,768,2048]{2,1,0:T(8,128)(2,1)S(1)}, bf16[1,768,2048]{2,1,0:T(8,128)(2,1)}, u32[]{:S(2)}) copy-start(bf16[1,768,2048]{2,1,0:T(8,128)(2,1)} %w_down.1) | copy-start | bytes 9437188
  14.2 9.5 %collective-permute-start.11 = (bf16[32,2176]{1,0:T(8,128)(2,1)S(1)}, bf16[32,2176]{1,0:T(8,128)(2,1)S(1)}, u32[]{:S(2)}, u32[]{:S(2)}) collective-permute-start(bf16[32,2176]{1,0:T(8,128)(2,1)S(1)} %pad_maximum_fusion.1), channel_id=1, source_target_pairs={{0,12},{1,13},{2,14},{3,15},{4,8},{5,9},{6,10},{7,11},{8,4},{9,5},... | collective-permute-start | bytes 417800 | tf_op jit(solution)/shard_map/ppermute | solution.py:27
  16.2 7.6 %collective-permute-start.3 = (bf16[32,2176]{1,0:T(8,128)(2,1)S(1)}, bf16[32,2176]{1,0:T(8,128)(2,1)S(1)}, u32[]{:S(2)}, u32[]{:S(2)}) collective-permute-start(bf16[32,2176]{1,0:T(8,128)(2,1)S(1)} %pad_maximum_fusion.1), channel_id=1, source_target_pairs={{0,4},{1,5},{2,6},{3,7},{4,0},{5,1},{6,2},{7,3},{8,12},{9,13},{10,... | collective-permute-start | bytes 417800 | tf_op jit(solution)/shard_map/ppermute | solution.py:27
  16.4 7.3 %collective-permute-start.10 = (bf16[16,2176]{1,0:T(8,128)(2,1)S(1)}, bf16[16,2176]{1,0:T(8,128)(2,1)S(1)}, u32[]{:S(2)}, u32[]{:S(2)}) collective-permute-start(bf16[16,2176]{1,0:T(8,128)(2,1)S(1)} %collective-permute-done.9), channel_id=1, source_target_pairs={{0,2},{1,3},{2,0},{3,1},{4,6},{5,7},{6,4},{7,5},{8,10},{9,11},{10,... | collective-permute-start | bytes 208904 | tf_op jit(solution)/shard_map/ppermute | solution.py:27
  23.7 1.6 %collective-permute-start.12 = (bf16[64,2176]{1,0:T(8,128)(2,1)S(1)}, bf16[64,2176]{1,0:T(8,128)(2,1)S(1)}, u32[]{:S(2)}, u32[]{:S(2)}) collective-permute-start(bf16[64,2176]{1,0:T(8,128)(2,1)S(1)} %constant_dynamic-update-slice_fusion.mine), channel_id=1, source_target_pairs={{0,1},{1,0},{2,3},{3,2},{4,5},{5,4},{6,7},{7,6},{8,9},{9,8},{10,11... | collective-permute-start | bytes 835592 | tf_op jit(solution)/shard_map/ppermute | solution.py:27
  23.8 3.2 %collective-permute-start.4 = (bf16[64,2176]{1,0:T(8,128)(2,1)S(1)}, bf16[64,2176]{1,0:T(8,128)(2,1)S(1)}, u32[]{:S(2)}, u32[]{:S(2)}) collective-permute-start(bf16[64,2176]{1,0:T(8,128)(2,1)S(1)} %pad_maximum_fusion.mine), channel_id=1, source_target_pairs={{0,1},{1,0},{2,3},{3,2},{4,5},{5,4},{6,7},{7,6},{8,9},{9,8},{10,11... | collective-permute-start | bytes 835592 | tf_op jit(solution)/shard_map/ppermute | solution.py:27
  26.8 2.1 %collective-permute-start.13 = (bf16[64,2048]{1,0:T(8,128)(2,1)S(1)}, bf16[64,2048]{1,0:T(8,128)(2,1)S(1)}, u32[]{:S(2)}, u32[]{:S(2)}) collective-permute-start(bf16[64,2048]{1,0:T(8,128)(2,1)S(1)} %get-tuple-element.25), channel_id=1, source_target_pairs={{0,1},{1,0},{2,3},{3,2},{4,5},{5,4},{6,7},{7,6},{8,9},{9,8},{10,11... | collective-permute-start | bytes 786440 | tf_op jit(solution)/shard_map/ppermute | solution.py:27
  28.5 2.7 %collective-permute-start.5 = (bf16[64,2048]{1,0:T(8,128)(2,1)S(1)}, bf16[64,2048]{1,0:T(8,128)(2,1)S(1)}, u32[]{:S(2)}, u32[]{:S(2)}) collective-permute-start(bf16[64,2048]{1,0:T(8,128)(2,1)S(1)} %get-tuple-element.23), channel_id=1, source_target_pairs={{0,1},{1,0},{2,3},{3,2},{4,5},{5,4},{6,7},{7,6},{8,9},{9,8},{10,11... | collective-permute-start | bytes 786440 | tf_op jit(solution)/shard_map/ppermute | solution.py:27
  29.1 4.6 %collective-permute-start.14 = (bf16[16,2048]{1,0:T(8,128)(2,1)S(1)}, bf16[16,2048]{1,0:T(8,128)(2,1)S(1)}, u32[]{:S(2)}, u32[]{:S(2)}) collective-permute-start(bf16[16,2048]{1,0:T(8,128)(2,1)S(1)} %get-tuple-element.28), channel_id=1, source_target_pairs={{0,2},{1,3},{2,0},{3,1},{4,6},{5,7},{6,4},{7,5},{8,10},{9,11},{10,... | collective-permute-start | bytes 196616 | tf_op jit(solution)/shard_map/ppermute | solution.py:27
  31.1 5.0 %collective-permute-start.16 = (bf16[16,2048]{1,0:T(8,128)(2,1)S(1)}, bf16[16,2048]{1,0:T(8,128)(2,1)S(1)}, u32[]{:S(2)}, u32[]{:S(2)}) collective-permute-start(bf16[16,2048]{1,0:T(8,128)(2,1)S(1)} %get-tuple-element.29), channel_id=1, source_target_pairs={{0,2},{1,3},{2,0},{3,1},{4,6},{5,7},{6,4},{7,5},{8,10},{9,11},{10,... | collective-permute-start | bytes 196616 | tf_op jit(solution)/shard_map/ppermute | solution.py:27
  31.3 10.2 %collective-permute-start.6 = (bf16[16,2048]{1,0:T(8,128)(2,1)S(1)}, bf16[16,2048]{1,0:T(8,128)(2,1)S(1)}, u32[]{:S(2)}, u32[]{:S(2)}) collective-permute-start(bf16[16,2048]{1,0:T(8,128)(2,1)S(1)} %get-tuple-element.26), channel_id=1, source_target_pairs={{0,2},{1,3},{2,0},{3,1},{4,6},{5,7},{6,4},{7,5},{8,10},{9,11},{10,... | collective-permute-start | bytes 196616 | tf_op jit(solution)/shard_map/ppermute | solution.py:27
  33.3 7.5 %collective-permute-start.7 = (bf16[16,2048]{1,0:T(8,128)(2,1)S(1)}, bf16[16,2048]{1,0:T(8,128)(2,1)S(1)}, u32[]{:S(2)}, u32[]{:S(2)}) collective-permute-start(bf16[16,2048]{1,0:T(8,128)(2,1)S(1)} %get-tuple-element.27), channel_id=1, source_target_pairs={{0,2},{1,3},{2,0},{3,1},{4,6},{5,7},{6,4},{7,5},{8,10},{9,11},{10,... | collective-permute-start | bytes 196616 | tf_op jit(solution)/shard_map/ppermute | solution.py:27
  33.6 7.9 %collective-permute-start.15 = (bf16[16,2048]{1,0:T(8,128)(2,1)S(1)}, bf16[16,2048]{1,0:T(8,128)(2,1)S(1)}, u32[]{:S(2)}, u32[]{:S(2)}) collective-permute-start(bf16[16,2048]{1,0:T(8,128)(2,1)S(1)} %farsum.1), channel_id=1, source_target_pairs={{0,8},{1,9},{2,10},{3,11},{4,12},{5,13},{6,14},{7,15},{8,0},{9,1},... | collective-permute-start | bytes 196616 | tf_op jit(solution)/shard_map/ppermute | solution.py:27
  36.1 7.0 %collective-permute-start.17 = (bf16[16,2048]{1,0:T(8,128)(2,1)S(1)}, bf16[16,2048]{1,0:T(8,128)(2,1)S(1)}, u32[]{:S(2)}, u32[]{:S(2)}) collective-permute-start(bf16[16,2048]{1,0:T(8,128)(2,1)S(1)} %fusion.1), channel_id=1, source_target_pairs={{0,12},{1,13},{2,14},{3,15},{4,8},{5,9},{6,10},{7,11},{8,4},{9,5},... | collective-permute-start | bytes 196616 | tf_op jit(solution)/shard_map/ppermute | solution.py:27
  40.8 4.3 %collective-permute-start.8 = (bf16[16,2048]{1,0:T(8,128)(2,1)S(1)}, bf16[16,2048]{1,0:T(8,128)(2,1)S(1)}, u32[]{:S(2)}, u32[]{:S(2)}) collective-permute-start(bf16[16,2048]{1,0:T(8,128)(2,1)S(1)} %fusion.3), channel_id=1, source_target_pairs={{0,4},{1,5},{2,6},{3,7},{4,0},{5,1},{6,2},{7,3},{8,12},{9,13},{10,... | collective-permute-start | bytes 196616 | tf_op jit(solution)/shard_map/ppermute | solution.py:27

commit v4 on v3

--- a/solution.py
+++ b/solution.py
@@ -48,8 +48,9 @@
     rows = res.shape[0]
     scale = 1.0 / math.sqrt(HEAD_SIZE)
     nt = (((1,), (1,)), ((), ()))
-    for copy in copies[:6]:
+    for copy in copies[:4]:
         copy.wait()
+    probs = []
     for t in range(seqs):
         live = lens[group * seqs + t]
         part = slice(t * block, (t + 1) * block)
@@ -60,6 +61,9 @@
         fresh = lax.dot_general(queries, kb[0, part], nt, preferred_element_type=jnp.float32) * scale
         position = lax.broadcasted_iota(jnp.int32, cache.shape, 1)
         cache = jnp.where(position < live, cache, -1e30)
+        probs.append((cache, fresh))
+    for t in range(seqs):
+        cache, fresh = probs[t]
         largest = jnp.maximum(
             jnp.max(cache, -1, keepdims=True), jnp.max(fresh, -1, keepdims=True)
         )
@@ -67,10 +71,14 @@
         fresh = jnp.exp(fresh - largest)
         total = jnp.sum(cache, -1, keepdims=True) + jnp.sum(fresh, -1, keepdims=True)
         share = 1.0 / total
-        mixed = jnp.dot(
-            (cache * share).astype(jnp.bfloat16), vc[0, t], preferred_element_type=jnp.float32
-        ) + jnp.dot(
-            (fresh * share).astype(jnp.bfloat16), vb[0, part], preferred_element_type=jnp.float32
+        probs[t] = (cache * share).astype(jnp.bfloat16), (fresh * share).astype(jnp.bfloat16)
+    copies[4].wait()
+    copies[5].wait()
+    for t in range(seqs):
+        cache, fresh = probs[t]
+        part = slice(t * block, (t + 1) * block)
+        mixed = jnp.dot(cache, vc[0, t], preferred_element_type=jnp.float32) + jnp.dot(
+            fresh, vb[0, part], preferred_element_type=jnp.float32
         )
         for g in range(heads):
             attn[part, g * HEAD_SIZE : (g + 1) * HEAD_SIZE] = mixed[
@@ -127,8 +135,10 @@
     experts = lax.axis_size("ep")
     own = lax.axis_index("ep")
     x[:half, :] = mine[...]
-    x[half:, :] = other[...]
-    lane = lax.broadcasted_iota(jnp.int32, (2 * half, LANES), 1)
+    x[half : 2 * half, :] = other[...]
+    if x.shape[0] > 2 * half:
+        x[2 * half :, :] = jnp.zeros((x.shape[0] - 2 * half, WIDE), jnp.bfloat16)
+    lane = lax.broadcasted_iota(jnp.int32, (x.shape[0], LANES), 1)
     codes = x[:, MODEL_WIDTH:].astype(jnp.float32)
     chosen = (lane == own) | (lane == own + experts)
     weight = jnp.sum(jnp.where(chosen, codes, 0.0), 1, keepdims=True)
@@ -143,7 +153,7 @@
         cols = slice(n, n + CHUNK)
         out = jnp.dot(act[...], w_down[0, :, cols], preferred_element_type=jnp.float32) * weight
         keep[:, cols] = out[:half]
-        send[:, cols] = out[half:].astype(jnp.bfloat16)
+        send[:, cols] = out[half : 2 * half].astype(jnp.bfloat16)
 
 
 def sum_kernel(sums, got, out):
@@ -214,8 +224,8 @@
             in_specs=[whole] * 5,
             out_specs=(whole, whole),
             scratch_shapes=[
-                pltpu.VMEM((2 * half, WIDE), jnp.bfloat16),
-                pltpu.VMEM((2 * half, w_gate.shape[2]), jnp.bfloat16),
+                pltpu.VMEM((max(2 * half, LANES), WIDE), jnp.bfloat16),
+                pltpu.VMEM((max(2 * half, LANES), w_gate.shape[2]), jnp.bfloat16),
             ],
             compiler_params=pltpu.CompilerParams(vmem_limit_bytes=12 << 20),
             cost_estimate=pl.CostEstimate(
@@ -240,9 +250,8 @@
     near_sum = (sums[1, 0] + got_near.astype(jnp.float32)).astype(jnp.bfloat16)
     summed = sums[0, 0] + got_own.astype(jnp.float32)
     near = exchanged(near_sum, 4)
-    sums = expert(jnp.concatenate([far, passed, across], 0))
+    sums = expert(jnp.concatenate([far, passed], 0))
     got_far = exchanged(sums[0, 1].astype(jnp.bfloat16), 2)
-    got_across = exchanged(sums[1, 1].astype(jnp.bfloat16), 2)
     far_sum = pl.pallas_call(
         sum_kernel,
         out_shape=jax.ShapeDtypeStruct((rows, MODEL_WIDTH), jnp.bfloat16),
@@ -253,7 +262,9 @@
         name="farsum",
     )(sums, got_far)
     far = exchanged(far_sum, 8)
-    across_sum = (sums[1, 0] + got_across.astype(jnp.float32)).astype(jnp.bfloat16)
+    sums = expert(across)
+    got_across = exchanged(sums[0, 1].astype(jnp.bfloat16), 2)
+    across_sum = (sums[0, 0] + got_across.astype(jnp.float32)).astype(jnp.bfloat16)
     across = exchanged(across_sum, 12)
     summed = summed + near.astype(jnp.float32) + far.astype(jnp.float32) + across.astype(jnp.float32)
     return (attended, summed.astype(jnp.bfloat16))

time: 46 us -> 50.8 us (1.10)
  starting transfers between devices: 25.7 us -> 30.3 us
  Pallas kernels: 6.08 us -> 7.17 us
  waiting for transfers between devices: 11.6 us -> 10.7 us
    ppermute x18 -> x20, starting transfers between devices: 25.7 us -> 30.3 us  [exchanged(): lax.ppermute(block, 'ep', [(index, index ^ mask) for index in range(count)])]
    pallas_call x2 -> x3, Pallas kernels: 2.95 us -> 4.41 us  [expert(): pl.pallas_call(expert_kernel, out_shape=(jax.ShapeDtypeStruct((half, MODE...]
    ppermute x18 -> x20, waiting for transfers between devices: 11.6 us -> 10.7 us  [exchanged(): lax.ppermute(block, 'ep', [(index, index ^ mask) for index in range(count)])]
  transfers between devices with their start and end apart: 18 -> 20, of which waited for: 9 -> 8; matrix products, arithmetic and copies ran while one was open for 2% -> 2% of each run, Pallas kernels for 7% -> 9%
where the time goes in v4:
time: 50.8 us; the launch traced here: 50.7 us
  starting transfers between devices  30.3 us (60%)
  waiting for transfers between devices  10.7 us (21%)
  Pallas kernels  7.17 us (14%)
  other arithmetic  0.91 us (2%)
  between operations  0.85 us (2%)
  local copies, waits for them, and re-layouts  0.71 us (1%)
    ppermute x20, starting transfers between devices, exchanged(): lax.ppermute(block, 'ep', [(index, index ^ mask) for index in range(count)])  30.3 us
    ppermute x20, waiting for transfers between devices, exchanged(): lax.ppermute(block, 'ep', [(index, index ^ mask) for index in range(count)])  10.7 us
    pallas_call x3, Pallas kernels, expert(): pl.pallas_call(expert_kernel, out_shape=(jax.ShapeDtypeStruct((half, MODE...  4.41 us
    pallas_call x1, Pallas kernels, every_row(): pl.pallas_call(attend_kernel, out_shape=(jax.ShapeDtypeStruct((2 * rows,...  2.51 us
  transfers between devices with their start and end apart: 20, of which 8 were waited for; matrix products, arithmetic and copies ran while one was open for 2% of the time, Pallas kernels for 9%

profile of v4, /device:TPU:0, one launch (start us, length us, event | category | flops | bytes accessed | tf_op | source)
XLA Modules:
  0.0 50.7 jit_solution(16218692773520195618)
XLA Ops:
  0.6 2.5 %attend.1 = (bf16[32,2176]{1,0:T(8,128)(2,1)S(1)}, f32[32,2176]{1,0:T(8,128)S(1)}) custom-call(s32[8]{0:T(128)} %lens_hbm.1, bf16[1,64,512]{2,1,0:T(8,128)(2,1)} %q_hbm.1, bf16[1,2,512,128]{3,2,1,0:T(8,128)(2,1)} %kc_hbm.1, bf16[1,2,512,128]{3,2,1,0:T(8,128)(2,1)} %vc_hbm.1, bf16[1,64,128]{2,1,0:T(8,128)(2,1)} %kb_hbm.1, bf16[1,64,128]{2,1,0:T(8,128)(2,1)} %vb_hbm.1, ...), custom_call_target="tpu_custom_call" | custom-call | flops 1073741824 | bytes 8388608 | tf_op jit(solution)/shard_map/attend/pallas_call | solution.py:181
  3.2 0.6 %collective-permute-start = (bf16[32,2176]{1,0:T(8,128)(2,1)S(1)}, bf16[32,2176]{1,0:T(8,128)(2,1)S(1)}, u32[]{:S(2)}, u32[]{:S(2)}) collective-permute-start(bf16[32,2176]{1,0:T(8,128)(2,1)S(1)} %get-tuple-element.18), channel_id=1, source_target_pairs={{0,1},{1,0},{2,3},{3,2},{4,5},{5,4},{6,7},{7,6},{8,9},{9,8},{10,11... | collective-permute-start | bytes 417800 | tf_op jit(solution)/shard_map/ppermute | solution.py:27
  3.7 1.0 %collective-permute-done.core = bf16[32,2176]{1,0:T(8,128)(2,1)S(1)} collective-permute-done((bf16[32,2176]{1,0:T(8,128)(2,1)S(1)}, bf16[32,2176]{1,0:T(8,128)(2,1)S(1)}, u32[]{:S(2)}, u32[]{:S(2)}) %collective-permute-start) | collective-permute-done | bytes 139296 | tf_op jit(solution)/shard_map/ppermute | solution.py:27
  4.8 2.9 %collective-permute-start.1 = (bf16[16,2176]{1,0:T(8,128)(2,1)S(1)}, bf16[16,2176]{1,0:T(8,128)(2,1)S(1)}, u32[]{:S(2)}, u32[]{:S(2)}) collective-permute-start(bf16[16,2176]{1,0:T(8,128)(2,1)S(1)} %get-tuple-element.33), channel_id=1, source_target_pairs={{0,2},{1,3},{2,0},{3,1},{4,6},{5,7},{6,4},{7,5},{8,10},{9,11},{10,... | collective-permute-start | bytes 208904 | tf_op jit(solution)/shard_map/ppermute | solution.py:27
  7.7 2.4 %collective-permute-done.1.chip = bf16[16,2176]{1,0:T(8,128)(2,1)S(1)} collective-permute-done((bf16[16,2176]{1,0:T(8,128)(2,1)S(1)}, bf16[16,2176]{1,0:T(8,128)(2,1)S(1)}, u32[]{:S(2)}, u32[]{:S(2)}) %collective-permute-start.1) | collective-permute-done | bytes 69664 | tf_op jit(solution)/shard_map/ppermute | solution.py:27
  10.2 0.1 norm.2
  10.4 3.3 %collective-permute-start.9 = (bf16[16,2176]{1,0:T(8,128)(2,1)S(1)}, bf16[16,2176]{1,0:T(8,128)(2,1)S(1)}, u32[]{:S(2)}, u32[]{:S(2)}) collective-permute-start(bf16[16,2176]{1,0:T(8,128)(2,1)S(1)} %get-tuple-element.20), channel_id=1, source_target_pairs={{0,8},{1,9},{2,10},{3,11},{4,12},{5,13},{6,14},{7,15},{8,0},{9,1},... | collective-permute-start | bytes 208904 | tf_op jit(solution)/shard_map/ppermute | solution.py:27
  13.7 0.1 norm.3
  13.8 2.0 %collective-permute-start.15 = (bf16[32,2176]{1,0:T(8,128)(2,1)S(1)}, bf16[32,2176]{1,0:T(8,128)(2,1)S(1)}, u32[]{:S(2)}, u32[]{:S(2)}) collective-permute-start(bf16[32,2176]{1,0:T(8,128)(2,1)S(1)} %pad_maximum_fusion.1), channel_id=1, source_target_pairs={{0,12},{1,13},{2,14},{3,15},{4,8},{5,9},{6,10},{7,11},{8,4},{9,5},... | collective-permute-start | bytes 417800 | tf_op jit(solution)/shard_map/ppermute | solution.py:27
  15.8 0.3 collective-permute-done.9
  16.1 5.0 %collective-permute-start.10 = (bf16[16,2176]{1,0:T(8,128)(2,1)S(1)}, bf16[16,2176]{1,0:T(8,128)(2,1)S(1)}, u32[]{:S(2)}, u32[]{:S(2)}) collective-permute-start(bf16[16,2176]{1,0:T(8,128)(2,1)S(1)} %collective-permute-done.9), channel_id=1, source_target_pairs={{0,2},{1,3},{2,0},{3,1},{4,6},{5,7},{6,4},{7,5},{8,10},{9,11},{10,... | collective-permute-start | bytes 208904 | tf_op jit(solution)/shard_map/ppermute | solution.py:27
  21.1 2.3 %collective-permute-done.10 = bf16[16,2176]{1,0:T(8,128)(2,1)S(1)} collective-permute-done((bf16[16,2176]{1,0:T(8,128)(2,1)S(1)}, bf16[16,2176]{1,0:T(8,128)(2,1)S(1)}, u32[]{:S(2)}, u32[]{:S(2)}) %collective-permute-start.10) | collective-permute-done | bytes 69664 | tf_op jit(solution)/shard_map/ppermute | solution.py:27
  23.4 2.4 %collective-permute-start.3 = (bf16[32,2176]{1,0:T(8,128)(2,1)S(1)}, bf16[32,2176]{1,0:T(8,128)(2,1)S(1)}, u32[]{:S(2)}, u32[]{:S(2)}) collective-permute-start(bf16[32,2176]{1,0:T(8,128)(2,1)S(1)} %pad_maximum_fusion.1), channel_id=1, source_target_pairs={{0,4},{1,5},{2,6},{3,7},{4,0},{5,1},{6,2},{7,3},{8,12},{9,13},{10,... | collective-permute-start | bytes 417800 | tf_op jit(solution)/shard_map/ppermute | solution.py:27
  25.8 0.2 collective-permute-start.16
  26.0 1.5 %expert.4 = (f32[32,2048]{1,0:T(8,128)S(1)}, bf16[32,2048]{1,0:T(8,128)(2,1)S(1)}) custom-call(bf16[32,2176]{1,0:T(8,128)(2,1)S(1)} %constant_dynamic-update-slice_fusion.mine, bf16[32,2176]{1,0:T(8,128)(2,1)S(1)} %collective-permute-done.11.other, bf16[1,2048,768]{2,1,0:T(8,128)(2,1)S(1)} %copy-done, bf16[1,2048,768]{2,1,0:T(8,128)(2,1)S(1)} %copy-done.1, ...), custom_call_target="tpu_custom_call" | custom-call | flops 1073741824 | bytes 8388608 | tf_op jit(solution)/shard_map/expert/pallas_call | solution.py:218
  27.5 0.4 collective-permute-start.12
  27.9 2.2 %collective-permute-done.3 = bf16[32,2176]{1,0:T(8,128)(2,1)S(1)} collective-permute-done((bf16[32,2176]{1,0:T(8,128)(2,1)S(1)}, bf16[32,2176]{1,0:T(8,128)(2,1)S(1)}, u32[]{:S(2)}, u32[]{:S(2)}) %collective-permute-start.3) | collective-permute-done | bytes 139296 | tf_op jit(solution)/shard_map/ppermute | solution.py:27
  30.2 1.5 %expert.5 = (f32[32,2048]{1,0:T(8,128)S(1)}, bf16[32,2048]{1,0:T(8,128)(2,1)S(1)}) custom-call(bf16[32,2176]{1,0:T(8,128)(2,1)S(1)} %collective-permute-done.15.mine, bf16[32,2176]{1,0:T(8,128)(2,1)S(1)} %collective-permute-done.16.other, bf16[1,2048,768]{2,1,0:T(8,128)(2,1)S(1)} %copy-done, bf16[1,2048,768]{2,1,0:T(8,128)(2,1)S(1)} %copy-done.1, ...), custom_call_target="tpu_custom_call" | custom-call | flops 1073741824 | bytes 8388608 | tf_op jit(solution)/shard_map/expert/pallas_call | solution.py:218
  31.7 0.6 %collective-permute-start.17 = (bf16[32,2048]{1,0:T(8,128)(2,1)S(1)}, bf16[32,2048]{1,0:T(8,128)(2,1)S(1)}, u32[]{:S(2)}, u32[]{:S(2)}) collective-permute-start(bf16[32,2048]{1,0:T(8,128)(2,1)S(1)} %get-tuple-element.29), channel_id=1, source_target_pairs={{0,1},{1,0},{2,3},{3,2},{4,5},{5,4},{6,7},{7,6},{8,9},{9,8},{10,11... | collective-permute-start | bytes 393224 | tf_op jit(solution)/shard_map/ppermute | solution.py:27
  32.3 1.6 %collective-permute-start.13 = (bf16[16,2048]{1,0:T(8,128)(2,1)S(1)}, bf16[16,2048]{1,0:T(8,128)(2,1)S(1)}, u32[]{:S(2)}, u32[]{:S(2)}) collective-permute-start(bf16[16,2048]{1,0:T(8,128)(2,1)S(1)} %fusion.9), channel_id=1, source_target_pairs={{0,2},{1,3},{2,0},{3,1},{4,6},{5,7},{6,4},{7,5},{8,10},{9,11},{10,... | collective-permute-start | bytes 196616 | tf_op jit(solution)/shard_map/ppermute | solution.py:27
  33.9 1.5 %expert.3 = (f32[64,2048]{1,0:T(8,128)S(1)}, bf16[64,2048]{1,0:T(8,128)(2,1)S(1)}) custom-call(bf16[64,2176]{1,0:T(8,128)(2,1)S(1)} %pad_maximum_fusion.mine, bf16[64,2176]{1,0:T(8,128)(2,1)S(1)} %collective-permute-done.4.other, bf16[1,2048,768]{2,1,0:T(8,128)(2,1)S(1)} %copy-done, bf16[1,2048,768]{2,1,0:T(8,128)(2,1)S(1)} %copy-done.1, ...), custom_call_target="tpu_custom_call" | custom-call | flops 1073741824 | bytes 8388608 | tf_op jit(solution)/shard_map/expert/pallas_call | solution.py:218
  35.4 1.3 %collective-permute-start.18 = (bf16[16,2048]{1,0:T(8,128)(2,1)S(1)}, bf16[16,2048]{1,0:T(8,128)(2,1)S(1)}, u32[]{:S(2)}, u32[]{:S(2)}) collective-permute-start(bf16[16,2048]{1,0:T(8,128)(2,1)S(1)} %fusion.10), channel_id=1, source_target_pairs={{0,2},{1,3},{2,0},{3,1},{4,6},{5,7},{6,4},{7,5},{8,10},{9,11},{10,... | collective-permute-start | bytes 196616 | tf_op jit(solution)/shard_map/ppermute | solution.py:27
  36.7 3.4 %collective-permute-start.14 = (bf16[16,2048]{1,0:T(8,128)(2,1)S(1)}, bf16[16,2048]{1,0:T(8,128)(2,1)S(1)}, u32[]{:S(2)}, u32[]{:S(2)}) collective-permute-start(bf16[16,2048]{1,0:T(8,128)(2,1)S(1)} %farsum.1), channel_id=1, source_target_pairs={{0,8},{1,9},{2,10},{3,11},{4,12},{5,13},{6,14},{7,15},{8,0},{9,1},... | collective-permute-start | bytes 196616 | tf_op jit(solution)/shard_map/ppermute | solution.py:27
  40.3 1.4 %collective-permute-start.7 = (bf16[16,2048]{1,0:T(8,128)(2,1)S(1)}, bf16[16,2048]{1,0:T(8,128)(2,1)S(1)}, u32[]{:S(2)}, u32[]{:S(2)}) collective-permute-start(bf16[16,2048]{1,0:T(8,128)(2,1)S(1)} %get-tuple-element.31), channel_id=1, source_target_pairs={{0,2},{1,3},{2,0},{3,1},{4,6},{5,7},{6,4},{7,5},{8,10},{9,11},{10,... | collective-permute-start | bytes 196616 | tf_op jit(solution)/shard_map/ppermute | solution.py:27
  41.7 3.0 %collective-permute-start.19 = (bf16[16,2048]{1,0:T(8,128)(2,1)S(1)}, bf16[16,2048]{1,0:T(8,128)(2,1)S(1)}, u32[]{:S(2)}, u32[]{:S(2)}) collective-permute-start(bf16[16,2048]{1,0:T(8,128)(2,1)S(1)} %fusion.1), channel_id=1, source_target_pairs={{0,12},{1,13},{2,14},{3,15},{4,8},{5,9},{6,10},{7,11},{8,4},{9,5},... | collective-permute-start | bytes 196616 | tf_op jit(solution)/shard_map/ppermute | solution.py:27
  44.8 0.9 %collective-permute-start.6 = (bf16[16,2048]{1,0:T(8,128)(2,1)S(1)}, bf16[16,2048]{1,0:T(8,128)(2,1)S(1)}, u32[]{:S(2)}, u32[]{:S(2)}) collective-permute-start(bf16[16,2048]{1,0:T(8,128)(2,1)S(1)} %get-tuple-element.30), channel_id=1, source_target_pairs={{0,2},{1,3},{2,0},{3,1},{4,6},{5,7},{6,4},{7,5},{8,10},{9,11},{10,... | collective-permute-start | bytes 196616 | tf_op jit(solution)/shard_map/ppermute | solution.py:27
  45.7 1.2 %collective-permute-start.8 = (bf16[16,2048]{1,0:T(8,128)(2,1)S(1)}, bf16[16,2048]{1,0:T(8,128)(2,1)S(1)}, u32[]{:S(2)}, u32[]{:S(2)}) collective-permute-start(bf16[16,2048]{1,0:T(8,128)(2,1)S(1)} %fusion.3), channel_id=1, source_target_pairs={{0,4},{1,5},{2,6},{3,7},{4,0},{5,1},{6,2},{7,3},{8,12},{9,13},{10,... | collective-permute-start | bytes 196616 | tf_op jit(solution)/shard_map/ppermute | solution.py:27
  46.8 0.6 %copy.17 = bf16[16,2048]{1,0:T(8,128)(2,1)} copy(bf16[16,2048]{1,0:T(8,128)(2,1)S(1)} %get-tuple-element.34) | data formatting | bytes 131072
  47.5 0.6 %collective-permute-done.19 = bf16[16,2048]{1,0:T(8,128)(2,1)S(1)} collective-permute-done((bf16[16,2048]{1,0:T(8,128)(2,1)S(1)}, bf16[16,2048]{1,0:T(8,128)(2,1)S(1)}, u32[]{:S(2)}, u32[]{:S(2)}) %collective-permute-start.19) | collective-permute-done | bytes 65568 | tf_op jit(solution)/shard_map/ppermute | solution.py:27
  48.0 1.0 %collective-permute-done.6 = bf16[16,2048]{1,0:T(8,128)(2,1)S(1)} collective-permute-done((bf16[16,2048]{1,0:T(8,128)(2,1)S(1)}, bf16[16,2048]{1,0:T(8,128)(2,1)S(1)}, u32[]{:S(2)}, u32[]{:S(2)}) %collective-permute-start.6) | collective-permute-done | bytes 65568 | tf_op jit(solution)/shard_map/ppermute | solution.py:27
  49.0 1.0 %collective-permute-done.8 = bf16[16,2048]{1,0:T(8,128)(2,1)S(1)} collective-permute-done((bf16[16,2048]{1,0:T(8,128)(2,1)S(1)}, bf16[16,2048]{1,0:T(8,128)(2,1)S(1)}, u32[]{:S(2)}, u32[]{:S(2)}) %collective-permute-start.8) | collective-permute-done | bytes 65568 | tf_op jit(solution)/shard_map/ppermute | solution.py:27
  50.0 0.7 %fusion.8 = bf16[16,2048]{1,0:T(8,128)(2,1)} fusion(f32[2,2,16,2048]{3,2,1,0:T(8,128)S(1)} %bitcast.44, bf16[16,2048]{1,0:T(8,128)(2,1)S(1)} %collective-permute-done.19, bf16[16,2048]{1,0:T(8,128)(2,1)S(1)} %collective-permute-done.14, bf16[16,2048]{1,0:T(8,128)(2,1)S(1)} %collective-permute-done.8, bf16[16,2048]{1,0:T(8,128)(2,1)S(1)} %collective-permute-done.6), kind=kLoop, calls=%fused_computation.19 | loop fusion | flops 294912 | bytes 458752 | tf_op jit(solution)/shard_map/convert_element_type | solution.py:270
  (40 shorter events, 0.6 us)
Async XLA Ops:
  0.6 9.6 %copy-start.3 = (f32[2048]{0:T(1024)S(1)}, f32[2048]{0:T(1024)}, u32[]{:S(2)}) copy-start(f32[2048]{0:T(1024)} %param.22) | copy-start | bytes 24580
  3.2 1.6 %collective-permute-start = (bf16[32,2176]{1,0:T(8,128)(2,1)S(1)}, bf16[32,2176]{1,0:T(8,128)(2,1)S(1)}, u32[]{:S(2)}, u32[]{:S(2)}) collective-permute-start(bf16[32,2176]{1,0:T(8,128)(2,1)S(1)} %get-tuple-element.18), channel_id=1, source_target_pairs={{0,1},{1,0},{2,3},{3,2},{4,5},{5,4},{6,7},{7,6},{8,9},{9,8},{10,11... | collective-permute-start | bytes 417800 | tf_op jit(solution)/shard_map/ppermute | solution.py:27
  4.8 5.4 %collective-permute-start.1 = (bf16[16,2176]{1,0:T(8,128)(2,1)S(1)}, bf16[16,2176]{1,0:T(8,128)(2,1)S(1)}, u32[]{:S(2)}, u32[]{:S(2)}) collective-permute-start(bf16[16,2176]{1,0:T(8,128)(2,1)S(1)} %get-tuple-element.33), channel_id=1, source_target_pairs={{0,2},{1,3},{2,0},{3,1},{4,6},{5,7},{6,4},{7,5},{8,10},{9,11},{10,... | collective-permute-start | bytes 208904 | tf_op jit(solution)/shard_map/ppermute | solution.py:27
  7.7 6.0 %collective-permute-start.2 = (bf16[16,2176]{1,0:T(8,128)(2,1)S(1)}, bf16[16,2176]{1,0:T(8,128)(2,1)S(1)}, u32[]{:S(2)}, u32[]{:S(2)}) collective-permute-start(bf16[16,2176]{1,0:T(8,128)(2,1)S(1)} %get-tuple-element.32), channel_id=1, source_target_pairs={{0,2},{1,3},{2,0},{3,1},{4,6},{5,7},{6,4},{7,5},{8,10},{9,11},{10,... | collective-permute-start | bytes 208904 | tf_op jit(solution)/shard_map/ppermute | solution.py:27
  10.3 15.6 %copy-start = (bf16[1,2048,768]{2,1,0:T(8,128)(2,1)S(1)}, bf16[1,2048,768]{2,1,0:T(8,128)(2,1)}, u32[]{:S(2)}) copy-start(bf16[1,2048,768]{2,1,0:T(8,128)(2,1)} %w_gate.2) | copy-start | bytes 9437188
  10.3 15.6 %copy-start.1 = (bf16[1,2048,768]{2,1,0:T(8,128)(2,1)S(1)}, bf16[1,2048,768]{2,1,0:T(8,128)(2,1)}, u32[]{:S(2)}) copy-start(bf16[1,2048,768]{2,1,0:T(8,128)(2,1)} %w_up.2) | copy-start | bytes 9437188
  10.3 15.6 %copy-start.2 = (bf16[1,768,2048]{2,1,0:T(8,128)(2,1)S(1)}, bf16[1,768,2048]{2,1,0:T(8,128)(2,1)}, u32[]{:S(2)}) copy-start(bf16[1,768,2048]{2,1,0:T(8,128)(2,1)} %w_down.2) | copy-start | bytes 9437188
  10.4 5.7 %collective-permute-start.9 = (bf16[16,2176]{1,0:T(8,128)(2,1)S(1)}, bf16[16,2176]{1,0:T(8,128)(2,1)S(1)}, u32[]{:S(2)}, u32[]{:S(2)}) collective-permute-start(bf16[16,2176]{1,0:T(8,128)(2,1)S(1)} %get-tuple-element.20), channel_id=1, source_target_pairs={{0,8},{1,9},{2,10},{3,11},{4,12},{5,13},{6,14},{7,15},{8,0},{9,1},... | collective-permute-start | bytes 208904 | tf_op jit(solution)/shard_map/ppermute | solution.py:27
  13.8 12.0 %collective-permute-start.15 = (bf16[32,2176]{1,0:T(8,128)(2,1)S(1)}, bf16[32,2176]{1,0:T(8,128)(2,1)S(1)}, u32[]{:S(2)}, u32[]{:S(2)}) collective-permute-start(bf16[32,2176]{1,0:T(8,128)(2,1)S(1)} %pad_maximum_fusion.1), channel_id=1, source_target_pairs={{0,12},{1,13},{2,14},{3,15},{4,8},{5,9},{6,10},{7,11},{8,4},{9,5},... | collective-permute-start | bytes 417800 | tf_op jit(solution)/shard_map/ppermute | solution.py:27
  16.1 7.3 %collective-permute-start.10 = (bf16[16,2176]{1,0:T(8,128)(2,1)S(1)}, bf16[16,2176]{1,0:T(8,128)(2,1)S(1)}, u32[]{:S(2)}, u32[]{:S(2)}) collective-permute-start(bf16[16,2176]{1,0:T(8,128)(2,1)S(1)} %collective-permute-done.9), channel_id=1, source_target_pairs={{0,2},{1,3},{2,0},{3,1},{4,6},{5,7},{6,4},{7,5},{8,10},{9,11},{10,... | collective-permute-start | bytes 208904 | tf_op jit(solution)/shard_map/ppermute | solution.py:27
  23.4 2.6 %collective-permute-start.11 = (bf16[32,2176]{1,0:T(8,128)(2,1)S(1)}, bf16[32,2176]{1,0:T(8,128)(2,1)S(1)}, u32[]{:S(2)}, u32[]{:S(2)}) collective-permute-start(bf16[32,2176]{1,0:T(8,128)(2,1)S(1)} %constant_dynamic-update-slice_fusion.mine), channel_id=1, source_target_pairs={{0,1},{1,0},{2,3},{3,2},{4,5},{5,4},{6,7},{7,6},{8,9},{9,8},{10,11... | collective-permute-start | bytes 417800 | tf_op jit(solution)/shard_map/ppermute | solution.py:27
  23.4 6.6 %collective-permute-start.3 = (bf16[32,2176]{1,0:T(8,128)(2,1)S(1)}, bf16[32,2176]{1,0:T(8,128)(2,1)S(1)}, u32[]{:S(2)}, u32[]{:S(2)}) collective-permute-start(bf16[32,2176]{1,0:T(8,128)(2,1)S(1)} %pad_maximum_fusion.1), channel_id=1, source_target_pairs={{0,4},{1,5},{2,6},{3,7},{4,0},{5,1},{6,2},{7,3},{8,12},{9,13},{10,... | collective-permute-start | bytes 417800 | tf_op jit(solution)/shard_map/ppermute | solution.py:27
  25.8 4.4 %collective-permute-start.16 = (bf16[32,2176]{1,0:T(8,128)(2,1)S(1)}, bf16[32,2176]{1,0:T(8,128)(2,1)S(1)}, u32[]{:S(2)}, u32[]{:S(2)}) collective-permute-start(bf16[32,2176]{1,0:T(8,128)(2,1)S(1)} %collective-permute-done.15.mine), channel_id=1, source_target_pairs={{0,1},{1,0},{2,3},{3,2},{4,5},{5,4},{6,7},{7,6},{8,9},{9,8},{10,11... | collective-permute-start | bytes 417800 | tf_op jit(solution)/shard_map/ppermute | solution.py:27
  27.5 4.8 %collective-permute-start.12 = (bf16[32,2048]{1,0:T(8,128)(2,1)S(1)}, bf16[32,2048]{1,0:T(8,128)(2,1)S(1)}, u32[]{:S(2)}, u32[]{:S(2)}) collective-permute-start(bf16[32,2048]{1,0:T(8,128)(2,1)S(1)} %get-tuple-element.27), channel_id=1, source_target_pairs={{0,1},{1,0},{2,3},{3,2},{4,5},{5,4},{6,7},{7,6},{8,9},{9,8},{10,11... | collective-permute-start | bytes 393224 | tf_op jit(solution)/shard_map/ppermute | solution.py:27
  30.1 3.8 %collective-permute-start.4 = (bf16[64,2176]{1,0:T(8,128)(2,1)S(1)}, bf16[64,2176]{1,0:T(8,128)(2,1)S(1)}, u32[]{:S(2)}, u32[]{:S(2)}) collective-permute-start(bf16[64,2176]{1,0:T(8,128)(2,1)S(1)} %pad_maximum_fusion.mine), channel_id=1, source_target_pairs={{0,1},{1,0},{2,3},{3,2},{4,5},{5,4},{6,7},{7,6},{8,9},{9,8},{10,11... | collective-permute-start | bytes 835592 | tf_op jit(solution)/shard_map/ppermute | solution.py:27
  31.7 2.2 %collective-permute-start.17 = (bf16[32,2048]{1,0:T(8,128)(2,1)S(1)}, bf16[32,2048]{1,0:T(8,128)(2,1)S(1)}, u32[]{:S(2)}, u32[]{:S(2)}) collective-permute-start(bf16[32,2048]{1,0:T(8,128)(2,1)S(1)} %get-tuple-element.29), channel_id=1, source_target_pairs={{0,1},{1,0},{2,3},{3,2},{4,5},{5,4},{6,7},{7,6},{8,9},{9,8},{10,11... | collective-permute-start | bytes 393224 | tf_op jit(solution)/shard_map/ppermute | solution.py:27
  32.3 4.4 %collective-permute-start.13 = (bf16[16,2048]{1,0:T(8,128)(2,1)S(1)}, bf16[16,2048]{1,0:T(8,128)(2,1)S(1)}, u32[]{:S(2)}, u32[]{:S(2)}) collective-permute-start(bf16[16,2048]{1,0:T(8,128)(2,1)S(1)} %fusion.9), channel_id=1, source_target_pairs={{0,2},{1,3},{2,0},{3,1},{4,6},{5,7},{6,4},{7,5},{8,10},{9,11},{10,... | collective-permute-start | bytes 196616 | tf_op jit(solution)/shard_map/ppermute | solution.py:27
  35.3 4.8 %collective-permute-start.5 = (bf16[64,2048]{1,0:T(8,128)(2,1)S(1)}, bf16[64,2048]{1,0:T(8,128)(2,1)S(1)}, u32[]{:S(2)}, u32[]{:S(2)}) collective-permute-start(bf16[64,2048]{1,0:T(8,128)(2,1)S(1)} %get-tuple-element.25), channel_id=1, source_target_pairs={{0,1},{1,0},{2,3},{3,2},{4,5},{5,4},{6,7},{7,6},{8,9},{9,8},{10,11... | collective-permute-start | bytes 786440 | tf_op jit(solution)/shard_map/ppermute | solution.py:27
  35.4 6.3 %collective-permute-start.18 = (bf16[16,2048]{1,0:T(8,128)(2,1)S(1)}, bf16[16,2048]{1,0:T(8,128)(2,1)S(1)}, u32[]{:S(2)}, u32[]{:S(2)}) collective-permute-start(bf16[16,2048]{1,0:T(8,128)(2,1)S(1)} %fusion.10), channel_id=1, source_target_pairs={{0,2},{1,3},{2,0},{3,1},{4,6},{5,7},{6,4},{7,5},{8,10},{9,11},{10,... | collective-permute-start | bytes 196616 | tf_op jit(solution)/shard_map/ppermute | solution.py:27
  36.7 10.7 %collective-permute-start.14 = (bf16[16,2048]{1,0:T(8,128)(2,1)S(1)}, bf16[16,2048]{1,0:T(8,128)(2,1)S(1)}, u32[]{:S(2)}, u32[]{:S(2)}) collective-permute-start(bf16[16,2048]{1,0:T(8,128)(2,1)S(1)} %farsum.1), channel_id=1, source_target_pairs={{0,8},{1,9},{2,10},{3,11},{4,12},{5,13},{6,14},{7,15},{8,0},{9,1},... | collective-permute-start | bytes 196616 | tf_op jit(solution)/shard_map/ppermute | solution.py:27
  40.3 5.4 %collective-permute-start.7 = (bf16[16,2048]{1,0:T(8,128)(2,1)S(1)}, bf16[16,2048]{1,0:T(8,128)(2,1)S(1)}, u32[]{:S(2)}, u32[]{:S(2)}) collective-permute-start(bf16[16,2048]{1,0:T(8,128)(2,1)S(1)} %get-tuple-element.31), channel_id=1, source_target_pairs={{0,2},{1,3},{2,0},{3,1},{4,6},{5,7},{6,4},{7,5},{8,10},{9,11},{10,... | collective-permute-start | bytes 196616 | tf_op jit(solution)/shard_map/ppermute | solution.py:27
  41.7 6.3 %collective-permute-start.19 = (bf16[16,2048]{1,0:T(8,128)(2,1)S(1)}, bf16[16,2048]{1,0:T(8,128)(2,1)S(1)}, u32[]{:S(2)}, u32[]{:S(2)}) collective-permute-start(bf16[16,2048]{1,0:T(8,128)(2,1)S(1)} %fusion.1), channel_id=1, source_target_pairs={{0,12},{1,13},{2,14},{3,15},{4,8},{5,9},{6,10},{7,11},{8,4},{9,5},... | collective-permute-start | bytes 196616 | tf_op jit(solution)/shard_map/ppermute | solution.py:27
  44.8 4.3 %collective-permute-start.6 = (bf16[16,2048]{1,0:T(8,128)(2,1)S(1)}, bf16[16,2048]{1,0:T(8,128)(2,1)S(1)}, u32[]{:S(2)}, u32[]{:S(2)}) collective-permute-start(bf16[16,2048]{1,0:T(8,128)(2,1)S(1)} %get-tuple-element.30), channel_id=1, source_target_pairs={{0,2},{1,3},{2,0},{3,1},{4,6},{5,7},{6,4},{7,5},{8,10},{9,11},{10,... | collective-permute-start | bytes 196616 | tf_op jit(solution)/shard_map/ppermute | solution.py:27
  45.7 4.3 %collective-permute-start.8 = (bf16[16,2048]{1,0:T(8,128)(2,1)S(1)}, bf16[16,2048]{1,0:T(8,128)(2,1)S(1)}, u32[]{:S(2)}, u32[]{:S(2)}) collective-permute-start(bf16[16,2048]{1,0:T(8,128)(2,1)S(1)} %fusion.3), channel_id=1, source_target_pairs={{0,4},{1,5},{2,6},{3,7},{4,0},{5,1},{6,2},{7,3},{8,12},{9,13},{10,... | collective-permute-start | bytes 196616 | tf_op jit(solution)/shard_map/ppermute | solution.py:27

commit v5 on v3

--- a/solution.py
+++ b/solution.py
@@ -48,8 +48,9 @@
     rows = res.shape[0]
     scale = 1.0 / math.sqrt(HEAD_SIZE)
     nt = (((1,), (1,)), ((), ()))
-    for copy in copies[:6]:
+    for copy in copies[:4]:
         copy.wait()
+    probs = []
     for t in range(seqs):
         live = lens[group * seqs + t]
         part = slice(t * block, (t + 1) * block)
@@ -60,6 +61,9 @@
         fresh = lax.dot_general(queries, kb[0, part], nt, preferred_element_type=jnp.float32) * scale
         position = lax.broadcasted_iota(jnp.int32, cache.shape, 1)
         cache = jnp.where(position < live, cache, -1e30)
+        probs.append((cache, fresh))
+    for t in range(seqs):
+        cache, fresh = probs[t]
         largest = jnp.maximum(
             jnp.max(cache, -1, keepdims=True), jnp.max(fresh, -1, keepdims=True)
         )
@@ -67,10 +71,14 @@
         fresh = jnp.exp(fresh - largest)
         total = jnp.sum(cache, -1, keepdims=True) + jnp.sum(fresh, -1, keepdims=True)
         share = 1.0 / total
-        mixed = jnp.dot(
-            (cache * share).astype(jnp.bfloat16), vc[0, t], preferred_element_type=jnp.float32
-        ) + jnp.dot(
-            (fresh * share).astype(jnp.bfloat16), vb[0, part], preferred_element_type=jnp.float32
+        probs[t] = (cache * share).astype(jnp.bfloat16), (fresh * share).astype(jnp.bfloat16)
+    copies[4].wait()
+    copies[5].wait()
+    for t in range(seqs):
+        cache, fresh = probs[t]
+        part = slice(t * block, (t + 1) * block)
+        mixed = jnp.dot(cache, vc[0, t], preferred_element_type=jnp.float32) + jnp.dot(
+            fresh, vb[0, part], preferred_element_type=jnp.float32
         )
         for g in range(heads):
             attn[part, g * HEAD_SIZE : (g + 1) * HEAD_SIZE] = mixed[
@@ -106,6 +114,12 @@
         sent[:, cols] = out[: 2 * rows].astype(jnp.bfloat16)
         kept[:rows, cols] = out[2 * rows : 3 * rows] + res[:, cols].astype(jnp.float32)
         kept[rows:, cols] = out[3 * rows :]
+
+
+def core_kernel(kept, core, own, pair):
+    rows = own.shape[0]
+    own[...] = (kept[:rows, :] + core[:rows, :].astype(jnp.float32)).astype(jnp.bfloat16)
+    pair[...] = (kept[rows:, :] + core[rows:, :].astype(jnp.float32)).astype(jnp.bfloat16)
 
 
 def norm_kernel(block, kept, core, chip, gain, *outs):
@@ -183,9 +197,18 @@
     )(*operands)
     sent, w_gate, w_up, w_down = lax.optimization_barrier((sent, w_gate, w_up, w_down))
     core = exchanged(sent, 1)
-    sums = (kept + core.astype(jnp.float32)).astype(jnp.bfloat16)
-    chip_own = exchanged(sums[rows:], 2)
-    chip_pair = exchanged(sums[:rows], 2)
+    half_sums = jax.ShapeDtypeStruct((rows, WIDE), jnp.bfloat16)
+    own_sums, pair_sums = pl.pallas_call(
+        core_kernel,
+        out_shape=(half_sums, half_sums),
+        in_specs=[whole] * 2,
+        out_specs=(whole, whole),
+        compiler_params=pltpu.CompilerParams(vmem_limit_bytes=4 << 20),
+        cost_estimate=pl.CostEstimate(flops=1 << 34, bytes_accessed=1 << 20, transcendentals=0),
+        name="coresum",
+    )(kept, core)
+    chip_own = exchanged(pair_sums, 2)
+    chip_pair = exchanged(own_sums, 2)
 
     def normed(block, chip):
         outs = (pltpu.VMEM((rows, MODEL_WIDTH), jnp.bfloat16),) * (block == 0)
@@ -197,7 +220,7 @@
             out_specs=(whole,) * len(outs),
             compiler_params=pltpu.CompilerParams(vmem_limit_bytes=6 << 20),
             cost_estimate=pl.CostEstimate(
-                flops=1 << 34, bytes_accessed=1 << 20, transcendentals=1 << 10
+                flops=1 << 20, bytes_accessed=1 << 20, transcendentals=1 << 10
             ),
             name="norm",
         )(kept, core, chip, norm_gain[None])

time: 46 us -> 45.6 us (level)
  no operation moved by 1% of the time
where the time goes in v5:
time: 45.6 us; the launch traced here: 45.4 us
  starting transfers between devices  25.6 us (56%)
  waiting for transfers between devices  11.7 us (26%)
  Pallas kernels  5.74 us (13%)
  other arithmetic  0.9 us (2%)
  between operations  0.78 us (2%)
  local copies, waits for them, and re-layouts  0.7 us (2%)
    ppermute x18, starting transfers between devices, exchanged(): lax.ppermute(block, 'ep', [(index, index ^ mask) for index in range(count)])  25.6 us
    ppermute x18, waiting for transfers between devices, exchanged(): lax.ppermute(block, 'ep', [(index, index ^ mask) for index in range(count)])  11.7 us
    pallas_call x2, Pallas kernels, expert(): pl.pallas_call(expert_kernel, out_shape=(jax.ShapeDtypeStruct((half, MODE...  2.94 us
    pallas_call x1, Pallas kernels, every_row(): pl.pallas_call(attend_kernel, out_shape=(jax.ShapeDtypeStruct((2 * rows,...  2.5 us
  transfers between devices with their start and end apart: 18, of which 9 were waited for; matrix products, arithmetic and copies ran while one was open for 2% of the time, Pallas kernels for 7%

profile of v5, /device:TPU:0, one launch (start us, length us, event | category | flops | bytes accessed | tf_op | source)
XLA Modules:
  0.0 45.4 jit_solution(689816099650626388)
XLA Ops:
  0.6 2.5 %attend.1 = (bf16[32,2176]{1,0:T(8,128)(2,1)S(1)}, f32[32,2176]{1,0:T(8,128)S(1)}) custom-call(s32[8]{0:T(128)} %lens_hbm.1, bf16[1,64,512]{2,1,0:T(8,128)(2,1)} %q_hbm.1, bf16[1,2,512,128]{3,2,1,0:T(8,128)(2,1)} %kc_hbm.1, bf16[1,2,512,128]{3,2,1,0:T(8,128)(2,1)} %vc_hbm.1, bf16[1,64,128]{2,1,0:T(8,128)(2,1)} %kb_hbm.1, bf16[1,64,128]{2,1,0:T(8,128)(2,1)} %vb_hbm.1, ...), custom_call_target="tpu_custom_call" | custom-call | flops 1073741824 | bytes 8388608 | tf_op jit(solution)/shard_map/attend/pallas_call | solution.py:185
  3.1 0.6 %collective-permute-start = (bf16[32,2176]{1,0:T(8,128)(2,1)S(1)}, bf16[32,2176]{1,0:T(8,128)(2,1)S(1)}, u32[]{:S(2)}, u32[]{:S(2)}) collective-permute-start(bf16[32,2176]{1,0:T(8,128)(2,1)S(1)} %get-tuple-element.18), channel_id=1, source_target_pairs={{0,1},{1,0},{2,3},{3,2},{4,5},{5,4},{6,7},{7,6},{8,9},{9,8},{10,11... | collective-permute-start | bytes 417800 | tf_op jit(solution)/shard_map/ppermute | solution.py:27
  3.7 1.0 %collective-permute-done.core = bf16[32,2176]{1,0:T(8,128)(2,1)S(1)} collective-permute-done((bf16[32,2176]{1,0:T(8,128)(2,1)S(1)}, bf16[32,2176]{1,0:T(8,128)(2,1)S(1)}, u32[]{:S(2)}, u32[]{:S(2)}) %collective-permute-start) | collective-permute-done | bytes 139296 | tf_op jit(solution)/shard_map/ppermute | solution.py:27
  4.7 2.9 %collective-permute-start.1 = (bf16[16,2176]{1,0:T(8,128)(2,1)S(1)}, bf16[16,2176]{1,0:T(8,128)(2,1)S(1)}, u32[]{:S(2)}, u32[]{:S(2)}) collective-permute-start(bf16[16,2176]{1,0:T(8,128)(2,1)S(1)} %get-tuple-element.19), channel_id=1, source_target_pairs={{0,2},{1,3},{2,0},{3,1},{4,6},{5,7},{6,4},{7,5},{8,10},{9,11},{10,... | collective-permute-start | bytes 208904 | tf_op jit(solution)/shard_map/ppermute | solution.py:27
  7.7 0.1 collective-permute-start.2
  7.7 2.4 %collective-permute-done.1.chip = bf16[16,2176]{1,0:T(8,128)(2,1)S(1)} collective-permute-done((bf16[16,2176]{1,0:T(8,128)(2,1)S(1)}, bf16[16,2176]{1,0:T(8,128)(2,1)S(1)}, u32[]{:S(2)}, u32[]{:S(2)}) %collective-permute-start.1) | collective-permute-done | bytes 69664 | tf_op jit(solution)/shard_map/ppermute | solution.py:27
  10.2 0.1 norm.2
  10.3 3.3 %collective-permute-start.9 = (bf16[16,2176]{1,0:T(8,128)(2,1)S(1)}, bf16[16,2176]{1,0:T(8,128)(2,1)S(1)}, u32[]{:S(2)}, u32[]{:S(2)}) collective-permute-start(bf16[16,2176]{1,0:T(8,128)(2,1)S(1)} %get-tuple-element.21), channel_id=1, source_target_pairs={{0,8},{1,9},{2,10},{3,11},{4,12},{5,13},{6,14},{7,15},{8,0},{9,1},... | collective-permute-start | bytes 208904 | tf_op jit(solution)/shard_map/ppermute | solution.py:27
  13.6 0.1 norm.3
  13.8 2.0 %collective-permute-start.11 = (bf16[32,2176]{1,0:T(8,128)(2,1)S(1)}, bf16[32,2176]{1,0:T(8,128)(2,1)S(1)}, u32[]{:S(2)}, u32[]{:S(2)}) collective-permute-start(bf16[32,2176]{1,0:T(8,128)(2,1)S(1)} %pad_maximum_fusion.1), channel_id=1, source_target_pairs={{0,12},{1,13},{2,14},{3,15},{4,8},{5,9},{6,10},{7,11},{8,4},{9,5},... | collective-permute-start | bytes 417800 | tf_op jit(solution)/shard_map/ppermute | solution.py:27
  15.8 0.2 collective-permute-done.9
  16.0 5.0 %collective-permute-start.10 = (bf16[16,2176]{1,0:T(8,128)(2,1)S(1)}, bf16[16,2176]{1,0:T(8,128)(2,1)S(1)}, u32[]{:S(2)}, u32[]{:S(2)}) collective-permute-start(bf16[16,2176]{1,0:T(8,128)(2,1)S(1)} %collective-permute-done.9), channel_id=1, source_target_pairs={{0,2},{1,3},{2,0},{3,1},{4,6},{5,7},{6,4},{7,5},{8,10},{9,11},{10,... | collective-permute-start | bytes 208904 | tf_op jit(solution)/shard_map/ppermute | solution.py:27
  21.0 2.3 %collective-permute-done.10 = bf16[16,2176]{1,0:T(8,128)(2,1)S(1)} collective-permute-done((bf16[16,2176]{1,0:T(8,128)(2,1)S(1)}, bf16[16,2176]{1,0:T(8,128)(2,1)S(1)}, u32[]{:S(2)}, u32[]{:S(2)}) %collective-permute-start.10) | collective-permute-done | bytes 69664 | tf_op jit(solution)/shard_map/ppermute | solution.py:27
  23.4 0.1 collective-permute-start.12
  23.5 0.6 %collective-permute-start.4 = (bf16[64,2176]{1,0:T(8,128)(2,1)S(1)}, bf16[64,2176]{1,0:T(8,128)(2,1)S(1)}, u32[]{:S(2)}, u32[]{:S(2)}) collective-permute-start(bf16[64,2176]{1,0:T(8,128)(2,1)S(1)} %pad_maximum_fusion.mine), channel_id=1, source_target_pairs={{0,1},{1,0},{2,3},{3,2},{4,5},{5,4},{6,7},{7,6},{8,9},{9,8},{10,11... | collective-permute-start | bytes 835592 | tf_op jit(solution)/shard_map/ppermute | solution.py:27
  24.0 1.0 %collective-permute-done.12.other = bf16[64,2176]{1,0:T(8,128)(2,1)S(1)} collective-permute-done((bf16[64,2176]{1,0:T(8,128)(2,1)S(1)}, bf16[64,2176]{1,0:T(8,128)(2,1)S(1)}, u32[]{:S(2)}, u32[]{:S(2)}) %collective-permute-start.12) | collective-permute-done | bytes 278560 | tf_op jit(solution)/shard_map/ppermute | solution.py:27
  25.0 1.5 %expert.3 = (f32[64,2048]{1,0:T(8,128)S(1)}, bf16[64,2048]{1,0:T(8,128)(2,1)S(1)}) custom-call(bf16[64,2176]{1,0:T(8,128)(2,1)S(1)} %constant_dynamic-update-slice_fusion.mine, bf16[64,2176]{1,0:T(8,128)(2,1)S(1)} %collective-permute-done.12.other, bf16[1,2048,768]{2,1,0:T(8,128)(2,1)S(1)} %copy-done, bf16[1,2048,768]{2,1,0:T(8,128)(2,1)S(1)} %copy-done.1, ...), custom_call_target="tpu_custom_call" | custom-call | flops 1073741824 | bytes 8388608 | tf_op jit(solution)/shard_map/expert/pallas_call | solution.py:231
  26.5 0.2 collective-permute-start.13
  26.7 1.5 %expert.2 = (f32[64,2048]{1,0:T(8,128)S(1)}, bf16[64,2048]{1,0:T(8,128)(2,1)S(1)}) custom-call(bf16[64,2176]{1,0:T(8,128)(2,1)S(1)} %pad_maximum_fusion.mine, bf16[64,2176]{1,0:T(8,128)(2,1)S(1)} %collective-permute-done.4.other, bf16[1,2048,768]{2,1,0:T(8,128)(2,1)S(1)} %copy-done, bf16[1,2048,768]{2,1,0:T(8,128)(2,1)S(1)} %copy-done.1, ...), custom_call_target="tpu_custom_call" | custom-call | flops 1073741824 | bytes 8388608 | tf_op jit(solution)/shard_map/expert/pallas_call | solution.py:231
  28.2 0.4 collective-permute-start.5
  28.7 2.1 %collective-permute-start.14 = (bf16[16,2048]{1,0:T(8,128)(2,1)S(1)}, bf16[16,2048]{1,0:T(8,128)(2,1)S(1)}, u32[]{:S(2)}, u32[]{:S(2)}) collective-permute-start(bf16[16,2048]{1,0:T(8,128)(2,1)S(1)} %get-tuple-element.32), channel_id=1, source_target_pairs={{0,2},{1,3},{2,0},{3,1},{4,6},{5,7},{6,4},{7,5},{8,10},{9,11},{10,... | collective-permute-start | bytes 196616 | tf_op jit(solution)/shard_map/ppermute | solution.py:27
  30.8 0.1 collective-permute-start.16
  31.0 2.0 %collective-permute-start.6 = (bf16[16,2048]{1,0:T(8,128)(2,1)S(1)}, bf16[16,2048]{1,0:T(8,128)(2,1)S(1)}, u32[]{:S(2)}, u32[]{:S(2)}) collective-permute-start(bf16[16,2048]{1,0:T(8,128)(2,1)S(1)} %get-tuple-element.30), channel_id=1, source_target_pairs={{0,2},{1,3},{2,0},{3,1},{4,6},{5,7},{6,4},{7,5},{8,10},{9,11},{10,... | collective-permute-start | bytes 196616 | tf_op jit(solution)/shard_map/ppermute | solution.py:27
  33.0 0.1 collective-permute-start.7
  33.1 0.2 collective-permute-done.14.got
  33.3 1.5 %collective-permute-start.15 = (bf16[16,2048]{1,0:T(8,128)(2,1)S(1)}, bf16[16,2048]{1,0:T(8,128)(2,1)S(1)}, u32[]{:S(2)}, u32[]{:S(2)}) collective-permute-start(bf16[16,2048]{1,0:T(8,128)(2,1)S(1)} %farsum.1), channel_id=1, source_target_pairs={{0,8},{1,9},{2,10},{3,11},{4,12},{5,13},{6,14},{7,15},{8,0},{9,1},... | collective-permute-start | bytes 196616 | tf_op jit(solution)/shard_map/ppermute | solution.py:27
  34.8 1.0 %collective-permute-done.16 = bf16[16,2048]{1,0:T(8,128)(2,1)S(1)} collective-permute-done((bf16[16,2048]{1,0:T(8,128)(2,1)S(1)}, bf16[16,2048]{1,0:T(8,128)(2,1)S(1)}, u32[]{:S(2)}, u32[]{:S(2)}) %collective-permute-start.16) | collective-permute-done | bytes 65568 | tf_op jit(solution)/shard_map/ppermute | solution.py:27
  35.8 4.6 %collective-permute-start.17 = (bf16[16,2048]{1,0:T(8,128)(2,1)S(1)}, bf16[16,2048]{1,0:T(8,128)(2,1)S(1)}, u32[]{:S(2)}, u32[]{:S(2)}) collective-permute-start(bf16[16,2048]{1,0:T(8,128)(2,1)S(1)} %fusion.1), channel_id=1, source_target_pairs={{0,12},{1,13},{2,14},{3,15},{4,8},{5,9},{6,10},{7,11},{8,4},{9,5},... | collective-permute-start | bytes 196616 | tf_op jit(solution)/shard_map/ppermute | solution.py:27
  40.5 0.6 %copy.18 = bf16[16,2048]{1,0:T(8,128)(2,1)} copy(bf16[16,2048]{1,0:T(8,128)(2,1)S(1)} %get-tuple-element.34) | data formatting | bytes 131072
  41.1 1.6 %collective-permute-done.17 = bf16[16,2048]{1,0:T(8,128)(2,1)S(1)} collective-permute-done((bf16[16,2048]{1,0:T(8,128)(2,1)S(1)}, bf16[16,2048]{1,0:T(8,128)(2,1)S(1)}, u32[]{:S(2)}, u32[]{:S(2)}) %collective-permute-start.17) | collective-permute-done | bytes 65568 | tf_op jit(solution)/shard_map/ppermute | solution.py:27
  42.8 2.0 %collective-permute-done.8 = bf16[16,2048]{1,0:T(8,128)(2,1)S(1)} collective-permute-done((bf16[16,2048]{1,0:T(8,128)(2,1)S(1)}, bf16[16,2048]{1,0:T(8,128)(2,1)S(1)}, u32[]{:S(2)}, u32[]{:S(2)}) %collective-permute-start.8) | collective-permute-done | bytes 65568 | tf_op jit(solution)/shard_map/ppermute | solution.py:27
  44.8 0.7 %fusion.8 = bf16[16,2048]{1,0:T(8,128)(2,1)} fusion(f32[2,2,16,2048]{3,2,1,0:T(8,128)S(1)} %bitcast.44, bf16[16,2048]{1,0:T(8,128)(2,1)S(1)} %collective-permute-done.17, bf16[16,2048]{1,0:T(8,128)(2,1)S(1)} %collective-permute-done.15, bf16[16,2048]{1,0:T(8,128)(2,1)S(1)} %collective-permute-done.8, bf16[16,2048]{1,0:T(8,128)(2,1)S(1)} %collective-permute-done.6), kind=kLoop, calls=%fused_computation.15 | loop fusion | flops 294912 | bytes 458752 | tf_op jit(solution)/shard_map/convert_element_type | solution.py:282
  (34 shorter events, 0.5 us)
Async XLA Ops:
  3.1 1.6 %collective-permute-start = (bf16[32,2176]{1,0:T(8,128)(2,1)S(1)}, bf16[32,2176]{1,0:T(8,128)(2,1)S(1)}, u32[]{:S(2)}, u32[]{:S(2)}) collective-permute-start(bf16[32,2176]{1,0:T(8,128)(2,1)S(1)} %get-tuple-element.18), channel_id=1, source_target_pairs={{0,1},{1,0},{2,3},{3,2},{4,5},{5,4},{6,7},{7,6},{8,9},{9,8},{10,11... | collective-permute-start | bytes 417800 | tf_op jit(solution)/shard_map/ppermute | solution.py:27
  4.7 5.5 %copy-start.3 = (f32[2048]{0:T(1024)S(1)}, f32[2048]{0:T(1024)}, u32[]{:S(2)}) copy-start(f32[2048]{0:T(1024)} %param.22) | copy-start | bytes 24580
  4.7 20.3 %copy-start = (bf16[1,2048,768]{2,1,0:T(8,128)(2,1)S(1)}, bf16[1,2048,768]{2,1,0:T(8,128)(2,1)}, u32[]{:S(2)}) copy-start(bf16[1,2048,768]{2,1,0:T(8,128)(2,1)} %w_gate.1) | copy-start | bytes 9437188
  4.7 20.3 %copy-start.1 = (bf16[1,2048,768]{2,1,0:T(8,128)(2,1)S(1)}, bf16[1,2048,768]{2,1,0:T(8,128)(2,1)}, u32[]{:S(2)}) copy-start(bf16[1,2048,768]{2,1,0:T(8,128)(2,1)} %w_up.1) | copy-start | bytes 9437188
  4.7 20.3 %copy-start.2 = (bf16[1,768,2048]{2,1,0:T(8,128)(2,1)S(1)}, bf16[1,768,2048]{2,1,0:T(8,128)(2,1)}, u32[]{:S(2)}) copy-start(bf16[1,768,2048]{2,1,0:T(8,128)(2,1)} %w_down.1) | copy-start | bytes 9437188
  4.7 5.4 %collective-permute-start.1 = (bf16[16,2176]{1,0:T(8,128)(2,1)S(1)}, bf16[16,2176]{1,0:T(8,128)(2,1)S(1)}, u32[]{:S(2)}, u32[]{:S(2)}) collective-permute-start(bf16[16,2176]{1,0:T(8,128)(2,1)S(1)} %get-tuple-element.19), channel_id=1, source_target_pairs={{0,2},{1,3},{2,0},{3,1},{4,6},{5,7},{6,4},{7,5},{8,10},{9,11},{10,... | collective-permute-start | bytes 208904 | tf_op jit(solution)/shard_map/ppermute | solution.py:27
  7.7 6.0 %collective-permute-start.2 = (bf16[16,2176]{1,0:T(8,128)(2,1)S(1)}, bf16[16,2176]{1,0:T(8,128)(2,1)S(1)}, u32[]{:S(2)}, u32[]{:S(2)}) collective-permute-start(bf16[16,2176]{1,0:T(8,128)(2,1)S(1)} %get-tuple-element.22), channel_id=1, source_target_pairs={{0,2},{1,3},{2,0},{3,1},{4,6},{5,7},{6,4},{7,5},{8,10},{9,11},{10,... | collective-permute-start | bytes 208904 | tf_op jit(solution)/shard_map/ppermute | solution.py:27
  10.3 5.7 %collective-permute-start.9 = (bf16[16,2176]{1,0:T(8,128)(2,1)S(1)}, bf16[16,2176]{1,0:T(8,128)(2,1)S(1)}, u32[]{:S(2)}, u32[]{:S(2)}) collective-permute-start(bf16[16,2176]{1,0:T(8,128)(2,1)S(1)} %get-tuple-element.21), channel_id=1, source_target_pairs={{0,8},{1,9},{2,10},{3,11},{4,12},{5,13},{6,14},{7,15},{8,0},{9,1},... | collective-permute-start | bytes 208904 | tf_op jit(solution)/shard_map/ppermute | solution.py:27
  13.8 9.6 %collective-permute-start.11 = (bf16[32,2176]{1,0:T(8,128)(2,1)S(1)}, bf16[32,2176]{1,0:T(8,128)(2,1)S(1)}, u32[]{:S(2)}, u32[]{:S(2)}) collective-permute-start(bf16[32,2176]{1,0:T(8,128)(2,1)S(1)} %pad_maximum_fusion.1), channel_id=1, source_target_pairs={{0,12},{1,13},{2,14},{3,15},{4,8},{5,9},{6,10},{7,11},{8,4},{9,5},... | collective-permute-start | bytes 417800 | tf_op jit(solution)/shard_map/ppermute | solution.py:27
  15.8 7.7 %collective-permute-start.3 = (bf16[32,2176]{1,0:T(8,128)(2,1)S(1)}, bf16[32,2176]{1,0:T(8,128)(2,1)S(1)}, u32[]{:S(2)}, u32[]{:S(2)}) collective-permute-start(bf16[32,2176]{1,0:T(8,128)(2,1)S(1)} %pad_maximum_fusion.1), channel_id=1, source_target_pairs={{0,4},{1,5},{2,6},{3,7},{4,0},{5,1},{6,2},{7,3},{8,12},{9,13},{10,... | collective-permute-start | bytes 417800 | tf_op jit(solution)/shard_map/ppermute | solution.py:27
  16.0 7.3 %collective-permute-start.10 = (bf16[16,2176]{1,0:T(8,128)(2,1)S(1)}, bf16[16,2176]{1,0:T(8,128)(2,1)S(1)}, u32[]{:S(2)}, u32[]{:S(2)}) collective-permute-start(bf16[16,2176]{1,0:T(8,128)(2,1)S(1)} %collective-permute-done.9), channel_id=1, source_target_pairs={{0,2},{1,3},{2,0},{3,1},{4,6},{5,7},{6,4},{7,5},{8,10},{9,11},{10,... | collective-permute-start | bytes 208904 | tf_op jit(solution)/shard_map/ppermute | solution.py:27
  23.4 1.6 %collective-permute-start.12 = (bf16[64,2176]{1,0:T(8,128)(2,1)S(1)}, bf16[64,2176]{1,0:T(8,128)(2,1)S(1)}, u32[]{:S(2)}, u32[]{:S(2)}) collective-permute-start(bf16[64,2176]{1,0:T(8,128)(2,1)S(1)} %constant_dynamic-update-slice_fusion.mine), channel_id=1, source_target_pairs={{0,1},{1,0},{2,3},{3,2},{4,5},{5,4},{6,7},{7,6},{8,9},{9,8},{10,11... | collective-permute-start | bytes 835592 | tf_op jit(solution)/shard_map/ppermute | solution.py:27
  23.5 3.2 %collective-permute-start.4 = (bf16[64,2176]{1,0:T(8,128)(2,1)S(1)}, bf16[64,2176]{1,0:T(8,128)(2,1)S(1)}, u32[]{:S(2)}, u32[]{:S(2)}) collective-permute-start(bf16[64,2176]{1,0:T(8,128)(2,1)S(1)} %pad_maximum_fusion.mine), channel_id=1, source_target_pairs={{0,1},{1,0},{2,3},{3,2},{4,5},{5,4},{6,7},{7,6},{8,9},{9,8},{10,11... | collective-permute-start | bytes 835592 | tf_op jit(solution)/shard_map/ppermute | solution.py:27
  26.5 2.1 %collective-permute-start.13 = (bf16[64,2048]{1,0:T(8,128)(2,1)S(1)}, bf16[64,2048]{1,0:T(8,128)(2,1)S(1)}, u32[]{:S(2)}, u32[]{:S(2)}) collective-permute-start(bf16[64,2048]{1,0:T(8,128)(2,1)S(1)} %get-tuple-element.29), channel_id=1, source_target_pairs={{0,1},{1,0},{2,3},{3,2},{4,5},{5,4},{6,7},{7,6},{8,9},{9,8},{10,11... | collective-permute-start | bytes 786440 | tf_op jit(solution)/shard_map/ppermute | solution.py:27
  28.2 2.7 %collective-permute-start.5 = (bf16[64,2048]{1,0:T(8,128)(2,1)S(1)}, bf16[64,2048]{1,0:T(8,128)(2,1)S(1)}, u32[]{:S(2)}, u32[]{:S(2)}) collective-permute-start(bf16[64,2048]{1,0:T(8,128)(2,1)S(1)} %get-tuple-element.27), channel_id=1, source_target_pairs={{0,1},{1,0},{2,3},{3,2},{4,5},{5,4},{6,7},{7,6},{8,9},{9,8},{10,11... | collective-permute-start | bytes 786440 | tf_op jit(solution)/shard_map/ppermute | solution.py:27
  28.7 4.6 %collective-permute-start.14 = (bf16[16,2048]{1,0:T(8,128)(2,1)S(1)}, bf16[16,2048]{1,0:T(8,128)(2,1)S(1)}, u32[]{:S(2)}, u32[]{:S(2)}) collective-permute-start(bf16[16,2048]{1,0:T(8,128)(2,1)S(1)} %get-tuple-element.32), channel_id=1, source_target_pairs={{0,2},{1,3},{2,0},{3,1},{4,6},{5,7},{6,4},{7,5},{8,10},{9,11},{10,... | collective-permute-start | bytes 196616 | tf_op jit(solution)/shard_map/ppermute | solution.py:27
  30.8 5.0 %collective-permute-start.16 = (bf16[16,2048]{1,0:T(8,128)(2,1)S(1)}, bf16[16,2048]{1,0:T(8,128)(2,1)S(1)}, u32[]{:S(2)}, u32[]{:S(2)}) collective-permute-start(bf16[16,2048]{1,0:T(8,128)(2,1)S(1)} %get-tuple-element.33), channel_id=1, source_target_pairs={{0,2},{1,3},{2,0},{3,1},{4,6},{5,7},{6,4},{7,5},{8,10},{9,11},{10,... | collective-permute-start | bytes 196616 | tf_op jit(solution)/shard_map/ppermute | solution.py:27
  31.0 10.1 %collective-permute-start.6 = (bf16[16,2048]{1,0:T(8,128)(2,1)S(1)}, bf16[16,2048]{1,0:T(8,128)(2,1)S(1)}, u32[]{:S(2)}, u32[]{:S(2)}) collective-permute-start(bf16[16,2048]{1,0:T(8,128)(2,1)S(1)} %get-tuple-element.30), channel_id=1, source_target_pairs={{0,2},{1,3},{2,0},{3,1},{4,6},{5,7},{6,4},{7,5},{8,10},{9,11},{10,... | collective-permute-start | bytes 196616 | tf_op jit(solution)/shard_map/ppermute | solution.py:27
  33.0 7.4 %collective-permute-start.7 = (bf16[16,2048]{1,0:T(8,128)(2,1)S(1)}, bf16[16,2048]{1,0:T(8,128)(2,1)S(1)}, u32[]{:S(2)}, u32[]{:S(2)}) collective-permute-start(bf16[16,2048]{1,0:T(8,128)(2,1)S(1)} %get-tuple-element.31), channel_id=1, source_target_pairs={{0,2},{1,3},{2,0},{3,1},{4,6},{5,7},{6,4},{7,5},{8,10},{9,11},{10,... | collective-permute-start | bytes 196616 | tf_op jit(solution)/shard_map/ppermute | solution.py:27
  33.3 7.8 %collective-permute-start.15 = (bf16[16,2048]{1,0:T(8,128)(2,1)S(1)}, bf16[16,2048]{1,0:T(8,128)(2,1)S(1)}, u32[]{:S(2)}, u32[]{:S(2)}) collective-permute-start(bf16[16,2048]{1,0:T(8,128)(2,1)S(1)} %farsum.1), channel_id=1, source_target_pairs={{0,8},{1,9},{2,10},{3,11},{4,12},{5,13},{6,14},{7,15},{8,0},{9,1},... | collective-permute-start | bytes 196616 | tf_op jit(solution)/shard_map/ppermute | solution.py:27
  35.8 7.0 %collective-permute-start.17 = (bf16[16,2048]{1,0:T(8,128)(2,1)S(1)}, bf16[16,2048]{1,0:T(8,128)(2,1)S(1)}, u32[]{:S(2)}, u32[]{:S(2)}) collective-permute-start(bf16[16,2048]{1,0:T(8,128)(2,1)S(1)} %fusion.1), channel_id=1, source_target_pairs={{0,12},{1,13},{2,14},{3,15},{4,8},{5,9},{6,10},{7,11},{8,4},{9,5},... | collective-permute-start | bytes 196616 | tf_op jit(solution)/shard_map/ppermute | solution.py:27
  40.4 4.3 %collective-permute-start.8 = (bf16[16,2048]{1,0:T(8,128)(2,1)S(1)}, bf16[16,2048]{1,0:T(8,128)(2,1)S(1)}, u32[]{:S(2)}, u32[]{:S(2)}) collective-permute-start(bf16[16,2048]{1,0:T(8,128)(2,1)S(1)} %fusion.3), channel_id=1, source_target_pairs={{0,4},{1,5},{2,6},{3,7},{4,0},{5,1},{6,2},{7,3},{8,12},{9,13},{10,... | collective-permute-start | bytes 196616 | tf_op jit(solution)/shard_map/ppermute | solution.py:27

commit v6 on v3

--- a/solution.py
+++ b/solution.py
@@ -48,8 +48,9 @@
     rows = res.shape[0]
     scale = 1.0 / math.sqrt(HEAD_SIZE)
     nt = (((1,), (1,)), ((), ()))
-    for copy in copies[:6]:
+    for copy in copies[:4]:
         copy.wait()
+    probs = []
     for t in range(seqs):
         live = lens[group * seqs + t]
         part = slice(t * block, (t + 1) * block)
@@ -60,6 +61,9 @@
         fresh = lax.dot_general(queries, kb[0, part], nt, preferred_element_type=jnp.float32) * scale
         position = lax.broadcasted_iota(jnp.int32, cache.shape, 1)
         cache = jnp.where(position < live, cache, -1e30)
+        probs.append((cache, fresh))
+    for t in range(seqs):
+        cache, fresh = probs[t]
         largest = jnp.maximum(
             jnp.max(cache, -1, keepdims=True), jnp.max(fresh, -1, keepdims=True)
         )
@@ -67,10 +71,14 @@
         fresh = jnp.exp(fresh - largest)
         total = jnp.sum(cache, -1, keepdims=True) + jnp.sum(fresh, -1, keepdims=True)
         share = 1.0 / total
-        mixed = jnp.dot(
-            (cache * share).astype(jnp.bfloat16), vc[0, t], preferred_element_type=jnp.float32
-        ) + jnp.dot(
-            (fresh * share).astype(jnp.bfloat16), vb[0, part], preferred_element_type=jnp.float32
+        probs[t] = (cache * share).astype(jnp.bfloat16), (fresh * share).astype(jnp.bfloat16)
+    copies[4].wait()
+    copies[5].wait()
+    for t in range(seqs):
+        cache, fresh = probs[t]
+        part = slice(t * block, (t + 1) * block)
+        mixed = jnp.dot(cache, vc[0, t], preferred_element_type=jnp.float32) + jnp.dot(
+            fresh, vb[0, part], preferred_element_type=jnp.float32
         )
         for g in range(heads):
             attn[part, g * HEAD_SIZE : (g + 1) * HEAD_SIZE] = mixed[

time: 46 us -> 45.6 us (level)
  no operation moved by 1% of the time
where the time goes in v6:
time: 45.6 us; the launch traced here: 45.5 us
  starting transfers between devices  25.7 us (56%)
  waiting for transfers between devices  11.6 us (25%)
  Pallas kernels  5.72 us (13%)
  other arithmetic  0.94 us (2%)
  between operations  0.8 us (2%)
  local copies, waits for them, and re-layouts  0.72 us (2%)
    ppermute x18, starting transfers between devices, exchanged(): lax.ppermute(block, 'ep', [(index, index ^ mask) for index in range(count)])  25.7 us
    ppermute x18, waiting for transfers between devices, exchanged(): lax.ppermute(block, 'ep', [(index, index ^ mask) for index in range(count)])  11.6 us
    pallas_call x2, Pallas kernels, expert(): pl.pallas_call(expert_kernel, out_shape=(jax.ShapeDtypeStruct((half, MODE...  2.94 us
    pallas_call x1, Pallas kernels, every_row(): pl.pallas_call(attend_kernel, out_shape=(jax.ShapeDtypeStruct((2 * rows,...  2.51 us
  transfers between devices with their start and end apart: 18, of which 9 were waited for; matrix products, arithmetic and copies ran while one was open for 2% of the time, Pallas kernels for 7%

profile of v6, /device:TPU:0, one launch (start us, length us, event | category | flops | bytes accessed | tf_op | source)
XLA Modules:
  0.0 45.5 jit_solution(6606081092267185188)
XLA Ops:
  0.6 2.5 %attend.1 = (bf16[32,2176]{1,0:T(8,128)(2,1)S(1)}, f32[32,2176]{1,0:T(8,128)S(1)}) custom-call(s32[8]{0:T(128)} %lens_hbm.1, bf16[1,64,512]{2,1,0:T(8,128)(2,1)} %q_hbm.1, bf16[1,2,512,128]{3,2,1,0:T(8,128)(2,1)} %kc_hbm.1, bf16[1,2,512,128]{3,2,1,0:T(8,128)(2,1)} %vc_hbm.1, bf16[1,64,128]{2,1,0:T(8,128)(2,1)} %kb_hbm.1, bf16[1,64,128]{2,1,0:T(8,128)(2,1)} %vb_hbm.1, ...), custom_call_target="tpu_custom_call" | custom-call | flops 1073741824 | bytes 8388608 | tf_op jit(solution)/shard_map/attend/pallas_call | solution.py:179
  3.2 0.6 %collective-permute-start = (bf16[32,2176]{1,0:T(8,128)(2,1)S(1)}, bf16[32,2176]{1,0:T(8,128)(2,1)S(1)}, u32[]{:S(2)}, u32[]{:S(2)}) collective-permute-start(bf16[32,2176]{1,0:T(8,128)(2,1)S(1)} %get-tuple-element.16), channel_id=1, source_target_pairs={{0,1},{1,0},{2,3},{3,2},{4,5},{5,4},{6,7},{7,6},{8,9},{9,8},{10,11... | collective-permute-start | bytes 417800 | tf_op jit(solution)/shard_map/ppermute | solution.py:27
  3.7 1.0 %collective-permute-done.core = bf16[32,2176]{1,0:T(8,128)(2,1)S(1)} collective-permute-done((bf16[32,2176]{1,0:T(8,128)(2,1)S(1)}, bf16[32,2176]{1,0:T(8,128)(2,1)S(1)}, u32[]{:S(2)}, u32[]{:S(2)}) %collective-permute-start) | collective-permute-done | bytes 139296 | tf_op jit(solution)/shard_map/ppermute | solution.py:27
  4.8 2.9 %collective-permute-start.1 = (bf16[16,2176]{1,0:T(8,128)(2,1)S(1)}, bf16[16,2176]{1,0:T(8,128)(2,1)S(1)}, u32[]{:S(2)}, u32[]{:S(2)}) collective-permute-start(bf16[16,2176]{1,0:T(8,128)(2,1)S(1)} %get-tuple-element.31), channel_id=1, source_target_pairs={{0,2},{1,3},{2,0},{3,1},{4,6},{5,7},{6,4},{7,5},{8,10},{9,11},{10,... | collective-permute-start | bytes 208904 | tf_op jit(solution)/shard_map/ppermute | solution.py:27
  7.7 0.1 collective-permute-start.2
  7.8 2.4 %collective-permute-done.1.chip = bf16[16,2176]{1,0:T(8,128)(2,1)S(1)} collective-permute-done((bf16[16,2176]{1,0:T(8,128)(2,1)S(1)}, bf16[16,2176]{1,0:T(8,128)(2,1)S(1)}, u32[]{:S(2)}, u32[]{:S(2)}) %collective-permute-start.1) | collective-permute-done | bytes 69664 | tf_op jit(solution)/shard_map/ppermute | solution.py:27
  10.2 0.1 norm.2
  10.3 3.3 %collective-permute-start.9 = (bf16[16,2176]{1,0:T(8,128)(2,1)S(1)}, bf16[16,2176]{1,0:T(8,128)(2,1)S(1)}, u32[]{:S(2)}, u32[]{:S(2)}) collective-permute-start(bf16[16,2176]{1,0:T(8,128)(2,1)S(1)} %get-tuple-element.18), channel_id=1, source_target_pairs={{0,8},{1,9},{2,10},{3,11},{4,12},{5,13},{6,14},{7,15},{8,0},{9,1},... | collective-permute-start | bytes 208904 | tf_op jit(solution)/shard_map/ppermute | solution.py:27
  13.7 0.1 norm.3
  13.8 2.0 %collective-permute-start.11 = (bf16[32,2176]{1,0:T(8,128)(2,1)S(1)}, bf16[32,2176]{1,0:T(8,128)(2,1)S(1)}, u32[]{:S(2)}, u32[]{:S(2)}) collective-permute-start(bf16[32,2176]{1,0:T(8,128)(2,1)S(1)} %pad_maximum_fusion.1), channel_id=1, source_target_pairs={{0,12},{1,13},{2,14},{3,15},{4,8},{5,9},{6,10},{7,11},{8,4},{9,5},... | collective-permute-start | bytes 417800 | tf_op jit(solution)/shard_map/ppermute | solution.py:27
  15.8 0.2 collective-permute-done.9
  16.0 5.0 %collective-permute-start.10 = (bf16[16,2176]{1,0:T(8,128)(2,1)S(1)}, bf16[16,2176]{1,0:T(8,128)(2,1)S(1)}, u32[]{:S(2)}, u32[]{:S(2)}) collective-permute-start(bf16[16,2176]{1,0:T(8,128)(2,1)S(1)} %collective-permute-done.9), channel_id=1, source_target_pairs={{0,2},{1,3},{2,0},{3,1},{4,6},{5,7},{6,4},{7,5},{8,10},{9,11},{10,... | collective-permute-start | bytes 208904 | tf_op jit(solution)/shard_map/ppermute | solution.py:27
  21.0 2.3 %collective-permute-done.10 = bf16[16,2176]{1,0:T(8,128)(2,1)S(1)} collective-permute-done((bf16[16,2176]{1,0:T(8,128)(2,1)S(1)}, bf16[16,2176]{1,0:T(8,128)(2,1)S(1)}, u32[]{:S(2)}, u32[]{:S(2)}) %collective-permute-start.10) | collective-permute-done | bytes 69664 | tf_op jit(solution)/shard_map/ppermute | solution.py:27
  23.3 0.1 collective-permute-start.12
  23.5 0.6 %collective-permute-start.4 = (bf16[64,2176]{1,0:T(8,128)(2,1)S(1)}, bf16[64,2176]{1,0:T(8,128)(2,1)S(1)}, u32[]{:S(2)}, u32[]{:S(2)}) collective-permute-start(bf16[64,2176]{1,0:T(8,128)(2,1)S(1)} %pad_maximum_fusion.mine), channel_id=1, source_target_pairs={{0,1},{1,0},{2,3},{3,2},{4,5},{5,4},{6,7},{7,6},{8,9},{9,8},{10,11... | collective-permute-start | bytes 835592 | tf_op jit(solution)/shard_map/ppermute | solution.py:27
  24.0 0.9 %collective-permute-done.12.other = bf16[64,2176]{1,0:T(8,128)(2,1)S(1)} collective-permute-done((bf16[64,2176]{1,0:T(8,128)(2,1)S(1)}, bf16[64,2176]{1,0:T(8,128)(2,1)S(1)}, u32[]{:S(2)}, u32[]{:S(2)}) %collective-permute-start.12) | collective-permute-done | bytes 278560 | tf_op jit(solution)/shard_map/ppermute | solution.py:27
  25.0 1.5 %expert.3 = (f32[64,2048]{1,0:T(8,128)S(1)}, bf16[64,2048]{1,0:T(8,128)(2,1)S(1)}) custom-call(bf16[64,2176]{1,0:T(8,128)(2,1)S(1)} %constant_dynamic-update-slice_fusion.mine, bf16[64,2176]{1,0:T(8,128)(2,1)S(1)} %collective-permute-done.12.other, bf16[1,2048,768]{2,1,0:T(8,128)(2,1)S(1)} %copy-done, bf16[1,2048,768]{2,1,0:T(8,128)(2,1)S(1)} %copy-done.1, ...), custom_call_target="tpu_custom_call" | custom-call | flops 1073741824 | bytes 8388608 | tf_op jit(solution)/shard_map/expert/pallas_call | solution.py:216
  26.5 0.2 collective-permute-start.13
  26.7 1.5 %expert.2 = (f32[64,2048]{1,0:T(8,128)S(1)}, bf16[64,2048]{1,0:T(8,128)(2,1)S(1)}) custom-call(bf16[64,2176]{1,0:T(8,128)(2,1)S(1)} %pad_maximum_fusion.mine, bf16[64,2176]{1,0:T(8,128)(2,1)S(1)} %collective-permute-done.4.other, bf16[1,2048,768]{2,1,0:T(8,128)(2,1)S(1)} %copy-done, bf16[1,2048,768]{2,1,0:T(8,128)(2,1)S(1)} %copy-done.1, ...), custom_call_target="tpu_custom_call" | custom-call | flops 1073741824 | bytes 8388608 | tf_op jit(solution)/shard_map/expert/pallas_call | solution.py:216
  28.2 0.4 collective-permute-start.5
  28.7 2.1 %collective-permute-start.14 = (bf16[16,2048]{1,0:T(8,128)(2,1)S(1)}, bf16[16,2048]{1,0:T(8,128)(2,1)S(1)}, u32[]{:S(2)}, u32[]{:S(2)}) collective-permute-start(bf16[16,2048]{1,0:T(8,128)(2,1)S(1)} %get-tuple-element.28), channel_id=1, source_target_pairs={{0,2},{1,3},{2,0},{3,1},{4,6},{5,7},{6,4},{7,5},{8,10},{9,11},{10,... | collective-permute-start | bytes 196616 | tf_op jit(solution)/shard_map/ppermute | solution.py:27
  30.8 0.1 collective-permute-start.16
  31.0 2.0 %collective-permute-start.6 = (bf16[16,2048]{1,0:T(8,128)(2,1)S(1)}, bf16[16,2048]{1,0:T(8,128)(2,1)S(1)}, u32[]{:S(2)}, u32[]{:S(2)}) collective-permute-start(bf16[16,2048]{1,0:T(8,128)(2,1)S(1)} %get-tuple-element.26), channel_id=1, source_target_pairs={{0,2},{1,3},{2,0},{3,1},{4,6},{5,7},{6,4},{7,5},{8,10},{9,11},{10,... | collective-permute-start | bytes 196616 | tf_op jit(solution)/shard_map/ppermute | solution.py:27
  33.0 0.1 collective-permute-start.7
  33.1 0.2 collective-permute-done.14.got
  33.3 1.6 %collective-permute-start.15 = (bf16[16,2048]{1,0:T(8,128)(2,1)S(1)}, bf16[16,2048]{1,0:T(8,128)(2,1)S(1)}, u32[]{:S(2)}, u32[]{:S(2)}) collective-permute-start(bf16[16,2048]{1,0:T(8,128)(2,1)S(1)} %farsum.1), channel_id=1, source_target_pairs={{0,8},{1,9},{2,10},{3,11},{4,12},{5,13},{6,14},{7,15},{8,0},{9,1},... | collective-permute-start | bytes 196616 | tf_op jit(solution)/shard_map/ppermute | solution.py:27
  34.8 0.9 %collective-permute-done.16 = bf16[16,2048]{1,0:T(8,128)(2,1)S(1)} collective-permute-done((bf16[16,2048]{1,0:T(8,128)(2,1)S(1)}, bf16[16,2048]{1,0:T(8,128)(2,1)S(1)}, u32[]{:S(2)}, u32[]{:S(2)}) %collective-permute-start.16) | collective-permute-done | bytes 65568 | tf_op jit(solution)/shard_map/ppermute | solution.py:27
  35.8 4.7 %collective-permute-start.17 = (bf16[16,2048]{1,0:T(8,128)(2,1)S(1)}, bf16[16,2048]{1,0:T(8,128)(2,1)S(1)}, u32[]{:S(2)}, u32[]{:S(2)}) collective-permute-start(bf16[16,2048]{1,0:T(8,128)(2,1)S(1)} %fusion.1), channel_id=1, source_target_pairs={{0,12},{1,13},{2,14},{3,15},{4,8},{5,9},{6,10},{7,11},{8,4},{9,5},... | collective-permute-start | bytes 196616 | tf_op jit(solution)/shard_map/ppermute | solution.py:27
  40.5 0.6 %copy.18 = bf16[16,2048]{1,0:T(8,128)(2,1)} copy(bf16[16,2048]{1,0:T(8,128)(2,1)S(1)} %get-tuple-element.32) | data formatting | bytes 131072
  41.2 1.6 %collective-permute-done.17 = bf16[16,2048]{1,0:T(8,128)(2,1)S(1)} collective-permute-done((bf16[16,2048]{1,0:T(8,128)(2,1)S(1)}, bf16[16,2048]{1,0:T(8,128)(2,1)S(1)}, u32[]{:S(2)}, u32[]{:S(2)}) %collective-permute-start.17) | collective-permute-done | bytes 65568 | tf_op jit(solution)/shard_map/ppermute | solution.py:27
  42.8 2.0 %collective-permute-done.8 = bf16[16,2048]{1,0:T(8,128)(2,1)S(1)} collective-permute-done((bf16[16,2048]{1,0:T(8,128)(2,1)S(1)}, bf16[16,2048]{1,0:T(8,128)(2,1)S(1)}, u32[]{:S(2)}, u32[]{:S(2)}) %collective-permute-start.8) | collective-permute-done | bytes 65568 | tf_op jit(solution)/shard_map/ppermute | solution.py:27
  44.8 0.7 %fusion.8 = bf16[16,2048]{1,0:T(8,128)(2,1)} fusion(f32[2,2,16,2048]{3,2,1,0:T(8,128)S(1)} %bitcast.44, bf16[16,2048]{1,0:T(8,128)(2,1)S(1)} %collective-permute-done.17, bf16[16,2048]{1,0:T(8,128)(2,1)S(1)} %collective-permute-done.15, bf16[16,2048]{1,0:T(8,128)(2,1)S(1)} %collective-permute-done.8, bf16[16,2048]{1,0:T(8,128)(2,1)S(1)} %collective-permute-done.6), kind=kLoop, calls=%fused_computation.16 | loop fusion | flops 294912 | bytes 458752 | tf_op jit(solution)/shard_map/convert_element_type | solution.py:267
  (35 shorter events, 0.5 us)
Async XLA Ops:
  0.6 9.6 %copy-start.3 = (f32[2048]{0:T(1024)S(1)}, f32[2048]{0:T(1024)}, u32[]{:S(2)}) copy-start(f32[2048]{0:T(1024)} %param.22) | copy-start | bytes 24580
  3.2 1.6 %collective-permute-start = (bf16[32,2176]{1,0:T(8,128)(2,1)S(1)}, bf16[32,2176]{1,0:T(8,128)(2,1)S(1)}, u32[]{:S(2)}, u32[]{:S(2)}) collective-permute-start(bf16[32,2176]{1,0:T(8,128)(2,1)S(1)} %get-tuple-element.16), channel_id=1, source_target_pairs={{0,1},{1,0},{2,3},{3,2},{4,5},{5,4},{6,7},{7,6},{8,9},{9,8},{10,11... | collective-permute-start | bytes 417800 | tf_op jit(solution)/shard_map/ppermute | solution.py:27
  4.8 5.4 %collective-permute-start.1 = (bf16[16,2176]{1,0:T(8,128)(2,1)S(1)}, bf16[16,2176]{1,0:T(8,128)(2,1)S(1)}, u32[]{:S(2)}, u32[]{:S(2)}) collective-permute-start(bf16[16,2176]{1,0:T(8,128)(2,1)S(1)} %get-tuple-element.31), channel_id=1, source_target_pairs={{0,2},{1,3},{2,0},{3,1},{4,6},{5,7},{6,4},{7,5},{8,10},{9,11},{10,... | collective-permute-start | bytes 208904 | tf_op jit(solution)/shard_map/ppermute | solution.py:27
  7.7 6.0 %collective-permute-start.2 = (bf16[16,2176]{1,0:T(8,128)(2,1)S(1)}, bf16[16,2176]{1,0:T(8,128)(2,1)S(1)}, u32[]{:S(2)}, u32[]{:S(2)}) collective-permute-start(bf16[16,2176]{1,0:T(8,128)(2,1)S(1)} %get-tuple-element.30), channel_id=1, source_target_pairs={{0,2},{1,3},{2,0},{3,1},{4,6},{5,7},{6,4},{7,5},{8,10},{9,11},{10,... | collective-permute-start | bytes 208904 | tf_op jit(solution)/shard_map/ppermute | solution.py:27
  10.3 5.7 %collective-permute-start.9 = (bf16[16,2176]{1,0:T(8,128)(2,1)S(1)}, bf16[16,2176]{1,0:T(8,128)(2,1)S(1)}, u32[]{:S(2)}, u32[]{:S(2)}) collective-permute-start(bf16[16,2176]{1,0:T(8,128)(2,1)S(1)} %get-tuple-element.18), channel_id=1, source_target_pairs={{0,8},{1,9},{2,10},{3,11},{4,12},{5,13},{6,14},{7,15},{8,0},{9,1},... | collective-permute-start | bytes 208904 | tf_op jit(solution)/shard_map/ppermute | solution.py:27
  13.6 11.3 %copy-start = (bf16[1,2048,768]{2,1,0:T(8,128)(2,1)S(1)}, bf16[1,2048,768]{2,1,0:T(8,128)(2,1)}, u32[]{:S(2)}) copy-start(bf16[1,2048,768]{2,1,0:T(8,128)(2,1)} %w_gate.1) | copy-start | bytes 9437188
  13.6 11.3 %copy-start.1 = (bf16[1,2048,768]{2,1,0:T(8,128)(2,1)S(1)}, bf16[1,2048,768]{2,1,0:T(8,128)(2,1)}, u32[]{:S(2)}) copy-start(bf16[1,2048,768]{2,1,0:T(8,128)(2,1)} %w_up.1) | copy-start | bytes 9437188
  13.6 11.3 %copy-start.2 = (bf16[1,768,2048]{2,1,0:T(8,128)(2,1)S(1)}, bf16[1,768,2048]{2,1,0:T(8,128)(2,1)}, u32[]{:S(2)}) copy-start(bf16[1,768,2048]{2,1,0:T(8,128)(2,1)} %w_down.1) | copy-start | bytes 9437188
  13.8 9.5 %collective-permute-start.11 = (bf16[32,2176]{1,0:T(8,128)(2,1)S(1)}, bf16[32,2176]{1,0:T(8,128)(2,1)S(1)}, u32[]{:S(2)}, u32[]{:S(2)}) collective-permute-start(bf16[32,2176]{1,0:T(8,128)(2,1)S(1)} %pad_maximum_fusion.1), channel_id=1, source_target_pairs={{0,12},{1,13},{2,14},{3,15},{4,8},{5,9},{6,10},{7,11},{8,4},{9,5},... | collective-permute-start | bytes 417800 | tf_op jit(solution)/shard_map/ppermute | solution.py:27
  15.8 7.6 %collective-permute-start.3 = (bf16[32,2176]{1,0:T(8,128)(2,1)S(1)}, bf16[32,2176]{1,0:T(8,128)(2,1)S(1)}, u32[]{:S(2)}, u32[]{:S(2)}) collective-permute-start(bf16[32,2176]{1,0:T(8,128)(2,1)S(1)} %pad_maximum_fusion.1), channel_id=1, source_target_pairs={{0,4},{1,5},{2,6},{3,7},{4,0},{5,1},{6,2},{7,3},{8,12},{9,13},{10,... | collective-permute-start | bytes 417800 | tf_op jit(solution)/shard_map/ppermute | solution.py:27
  16.0 7.3 %collective-permute-start.10 = (bf16[16,2176]{1,0:T(8,128)(2,1)S(1)}, bf16[16,2176]{1,0:T(8,128)(2,1)S(1)}, u32[]{:S(2)}, u32[]{:S(2)}) collective-permute-start(bf16[16,2176]{1,0:T(8,128)(2,1)S(1)} %collective-permute-done.9), channel_id=1, source_target_pairs={{0,2},{1,3},{2,0},{3,1},{4,6},{5,7},{6,4},{7,5},{8,10},{9,11},{10,... | collective-permute-start | bytes 208904 | tf_op jit(solution)/shard_map/ppermute | solution.py:27
  23.3 1.6 %collective-permute-start.12 = (bf16[64,2176]{1,0:T(8,128)(2,1)S(1)}, bf16[64,2176]{1,0:T(8,128)(2,1)S(1)}, u32[]{:S(2)}, u32[]{:S(2)}) collective-permute-start(bf16[64,2176]{1,0:T(8,128)(2,1)S(1)} %constant_dynamic-update-slice_fusion.mine), channel_id=1, source_target_pairs={{0,1},{1,0},{2,3},{3,2},{4,5},{5,4},{6,7},{7,6},{8,9},{9,8},{10,11... | collective-permute-start | bytes 835592 | tf_op jit(solution)/shard_map/ppermute | solution.py:27
  23.5 3.2 %collective-permute-start.4 = (bf16[64,2176]{1,0:T(8,128)(2,1)S(1)}, bf16[64,2176]{1,0:T(8,128)(2,1)S(1)}, u32[]{:S(2)}, u32[]{:S(2)}) collective-permute-start(bf16[64,2176]{1,0:T(8,128)(2,1)S(1)} %pad_maximum_fusion.mine), channel_id=1, source_target_pairs={{0,1},{1,0},{2,3},{3,2},{4,5},{5,4},{6,7},{7,6},{8,9},{9,8},{10,11... | collective-permute-start | bytes 835592 | tf_op jit(solution)/shard_map/ppermute | solution.py:27
  26.5 2.1 %collective-permute-start.13 = (bf16[64,2048]{1,0:T(8,128)(2,1)S(1)}, bf16[64,2048]{1,0:T(8,128)(2,1)S(1)}, u32[]{:S(2)}, u32[]{:S(2)}) collective-permute-start(bf16[64,2048]{1,0:T(8,128)(2,1)S(1)} %get-tuple-element.25), channel_id=1, source_target_pairs={{0,1},{1,0},{2,3},{3,2},{4,5},{5,4},{6,7},{7,6},{8,9},{9,8},{10,11... | collective-permute-start | bytes 786440 | tf_op jit(solution)/shard_map/ppermute | solution.py:27
  28.2 2.7 %collective-permute-start.5 = (bf16[64,2048]{1,0:T(8,128)(2,1)S(1)}, bf16[64,2048]{1,0:T(8,128)(2,1)S(1)}, u32[]{:S(2)}, u32[]{:S(2)}) collective-permute-start(bf16[64,2048]{1,0:T(8,128)(2,1)S(1)} %get-tuple-element.23), channel_id=1, source_target_pairs={{0,1},{1,0},{2,3},{3,2},{4,5},{5,4},{6,7},{7,6},{8,9},{9,8},{10,11... | collective-permute-start | bytes 786440 | tf_op jit(solution)/shard_map/ppermute | solution.py:27
  28.7 4.6 %collective-permute-start.14 = (bf16[16,2048]{1,0:T(8,128)(2,1)S(1)}, bf16[16,2048]{1,0:T(8,128)(2,1)S(1)}, u32[]{:S(2)}, u32[]{:S(2)}) collective-permute-start(bf16[16,2048]{1,0:T(8,128)(2,1)S(1)} %get-tuple-element.28), channel_id=1, source_target_pairs={{0,2},{1,3},{2,0},{3,1},{4,6},{5,7},{6,4},{7,5},{8,10},{9,11},{10,... | collective-permute-start | bytes 196616 | tf_op jit(solution)/shard_map/ppermute | solution.py:27
  30.8 5.0 %collective-permute-start.16 = (bf16[16,2048]{1,0:T(8,128)(2,1)S(1)}, bf16[16,2048]{1,0:T(8,128)(2,1)S(1)}, u32[]{:S(2)}, u32[]{:S(2)}) collective-permute-start(bf16[16,2048]{1,0:T(8,128)(2,1)S(1)} %get-tuple-element.29), channel_id=1, source_target_pairs={{0,2},{1,3},{2,0},{3,1},{4,6},{5,7},{6,4},{7,5},{8,10},{9,11},{10,... | collective-permute-start | bytes 196616 | tf_op jit(solution)/shard_map/ppermute | solution.py:27
  31.0 10.2 %collective-permute-start.6 = (bf16[16,2048]{1,0:T(8,128)(2,1)S(1)}, bf16[16,2048]{1,0:T(8,128)(2,1)S(1)}, u32[]{:S(2)}, u32[]{:S(2)}) collective-permute-start(bf16[16,2048]{1,0:T(8,128)(2,1)S(1)} %get-tuple-element.26), channel_id=1, source_target_pairs={{0,2},{1,3},{2,0},{3,1},{4,6},{5,7},{6,4},{7,5},{8,10},{9,11},{10,... | collective-permute-start | bytes 196616 | tf_op jit(solution)/shard_map/ppermute | solution.py:27
  33.0 7.4 %collective-permute-start.7 = (bf16[16,2048]{1,0:T(8,128)(2,1)S(1)}, bf16[16,2048]{1,0:T(8,128)(2,1)S(1)}, u32[]{:S(2)}, u32[]{:S(2)}) collective-permute-start(bf16[16,2048]{1,0:T(8,128)(2,1)S(1)} %get-tuple-element.27), channel_id=1, source_target_pairs={{0,2},{1,3},{2,0},{3,1},{4,6},{5,7},{6,4},{7,5},{8,10},{9,11},{10,... | collective-permute-start | bytes 196616 | tf_op jit(solution)/shard_map/ppermute | solution.py:27
  33.3 7.9 %collective-permute-start.15 = (bf16[16,2048]{1,0:T(8,128)(2,1)S(1)}, bf16[16,2048]{1,0:T(8,128)(2,1)S(1)}, u32[]{:S(2)}, u32[]{:S(2)}) collective-permute-start(bf16[16,2048]{1,0:T(8,128)(2,1)S(1)} %farsum.1), channel_id=1, source_target_pairs={{0,8},{1,9},{2,10},{3,11},{4,12},{5,13},{6,14},{7,15},{8,0},{9,1},... | collective-permute-start | bytes 196616 | tf_op jit(solution)/shard_map/ppermute | solution.py:27
  35.8 7.0 %collective-permute-start.17 = (bf16[16,2048]{1,0:T(8,128)(2,1)S(1)}, bf16[16,2048]{1,0:T(8,128)(2,1)S(1)}, u32[]{:S(2)}, u32[]{:S(2)}) collective-permute-start(bf16[16,2048]{1,0:T(8,128)(2,1)S(1)} %fusion.1), channel_id=1, source_target_pairs={{0,12},{1,13},{2,14},{3,15},{4,8},{5,9},{6,10},{7,11},{8,4},{9,5},... | collective-permute-start | bytes 196616 | tf_op jit(solution)/shard_map/ppermute | solution.py:27
  40.5 4.3 %collective-permute-start.8 = (bf16[16,2048]{1,0:T(8,128)(2,1)S(1)}, bf16[16,2048]{1,0:T(8,128)(2,1)S(1)}, u32[]{:S(2)}, u32[]{:S(2)}) collective-permute-start(bf16[16,2048]{1,0:T(8,128)(2,1)S(1)} %fusion.3), channel_id=1, source_target_pairs={{0,4},{1,5},{2,6},{3,7},{4,0},{5,1},{6,2},{7,3},{8,12},{9,13},{10,... | collective-permute-start | bytes 196616 | tf_op jit(solution)/shard_map/ppermute | solution.py:27

commit v7 on v6

--- a/solution.py
+++ b/solution.py
@@ -120,7 +120,8 @@
     packet = outs[-1]
     rows = packet.shape[0]
     here = slice(block * rows, (block + 1) * rows)
-    hidden = kept[here, :] + core[here, :].astype(jnp.float32) + chip[...].astype(jnp.float32)
+    there = slice((1 - block) * rows, (2 - block) * rows)
+    hidden = kept[here, :] + core[here, :].astype(jnp.float32) + chip[there, :].astype(jnp.float32)
     table = hidden[:, MODEL_WIDTH:]
     hidden = hidden[:, :MODEL_WIDTH]
     if block == 0:
@@ -192,10 +193,9 @@
     sent, w_gate, w_up, w_down = lax.optimization_barrier((sent, w_gate, w_up, w_down))
     core = exchanged(sent, 1)
     sums = (kept + core.astype(jnp.float32)).astype(jnp.bfloat16)
-    chip_own = exchanged(sums[rows:], 2)
-    chip_pair = exchanged(sums[:rows], 2)
-
-    def normed(block, chip):
+    chip = exchanged(sums, 2)
+
+    def normed(block):
         outs = (pltpu.VMEM((rows, MODEL_WIDTH), jnp.bfloat16),) * (block == 0)
         outs += (jax.ShapeDtypeStruct((rows, WIDE), jnp.bfloat16),)
         return pl.pallas_call(
@@ -235,9 +235,9 @@
         total = keep + back.astype(jnp.float32)
         return total.reshape(half // (2 * rows), 2, rows, MODEL_WIDTH)
 
-    attended, own = normed(0, chip_own)
+    attended, own = normed(0)
     far = exchanged(own, 8)
-    (pair,) = normed(1, chip_pair)
+    (pair,) = normed(1)
     packet = jnp.concatenate([own, pair], 0)
     near = exchanged(packet, 4)
     across = exchanged(packet, 12)

time: 45.6 us -> 46.4 us (1.018)
  waiting for transfers between devices: 11.6 us -> 15.2 us
  starting transfers between devices: 25.7 us -> 22.9 us
    ppermute x18 -> x17, waiting for transfers between devices: 11.6 us -> 15.2 us  [exchanged(): lax.ppermute(block, 'ep', [(index, index ^ mask) for index in range(count)])]
    ppermute x18 -> x17, starting transfers between devices: 25.7 us -> 22.9 us  [exchanged(): lax.ppermute(block, 'ep', [(index, index ^ mask) for index in range(count)])]
  transfers between devices with their start and end apart: 18 -> 17, of which waited for: 9 -> 10; matrix products, arithmetic and copies ran while one was open for 2% -> 2% of each run, Pallas kernels for 7% -> 7%
where the time goes in v7:
time: 46.4 us; the launch traced here: 46.3 us
  starting transfers between devices  22.9 us (49%)
  waiting for transfers between devices  15.2 us (33%)
  Pallas kernels  5.73 us (12%)
  other arithmetic  0.94 us (2%)
  between operations  0.78 us (2%)
  local copies, waits for them, and re-layouts  0.7 us (2%)
    ppermute x17, starting transfers between devices, exchanged(): lax.ppermute(block, 'ep', [(index, index ^ mask) for index in range(count)])  22.9 us
    ppermute x17, waiting for transfers between devices, exchanged(): lax.ppermute(block, 'ep', [(index, index ^ mask) for index in range(count)])  15.2 us
    pallas_call x2, Pallas kernels, expert(): pl.pallas_call(expert_kernel, out_shape=(jax.ShapeDtypeStruct((half, MODE...  2.96 us
    pallas_call x1, Pallas kernels, every_row(): pl.pallas_call(attend_kernel, out_shape=(jax.ShapeDtypeStruct((2 * rows,...  2.51 us
  transfers between devices with their start and end apart: 17, of which 10 were waited for; matrix products, arithmetic and copies ran while one was open for 2% of the time, Pallas kernels for 7%

profile of v7, /device:TPU:0, one launch (start us, length us, event | category | flops | bytes accessed | tf_op | source)
XLA Modules:
  0.0 46.3 jit_solution(1580553104596693681)
XLA Ops:
  0.6 2.5 %attend.1 = (bf16[32,2176]{1,0:T(8,128)(2,1)S(1)}, f32[32,2176]{1,0:T(8,128)S(1)}) custom-call(s32[8]{0:T(128)} %lens_hbm.1, bf16[1,64,512]{2,1,0:T(8,128)(2,1)} %q_hbm.1, bf16[1,2,512,128]{3,2,1,0:T(8,128)(2,1)} %kc_hbm.1, bf16[1,2,512,128]{3,2,1,0:T(8,128)(2,1)} %vc_hbm.1, bf16[1,64,128]{2,1,0:T(8,128)(2,1)} %kb_hbm.1, bf16[1,64,128]{2,1,0:T(8,128)(2,1)} %vb_hbm.1, ...), custom_call_target="tpu_custom_call" | custom-call | flops 1073741824 | bytes 8388608 | tf_op jit(solution)/shard_map/attend/pallas_call | solution.py:180
  3.2 0.6 %collective-permute-start = (bf16[32,2176]{1,0:T(8,128)(2,1)S(1)}, bf16[32,2176]{1,0:T(8,128)(2,1)S(1)}, u32[]{:S(2)}, u32[]{:S(2)}) collective-permute-start(bf16[32,2176]{1,0:T(8,128)(2,1)S(1)} %get-tuple-element.16), channel_id=1, source_target_pairs={{0,1},{1,0},{2,3},{3,2},{4,5},{5,4},{6,7},{7,6},{8,9},{9,8},{10,11... | collective-permute-start | bytes 417800 | tf_op jit(solution)/shard_map/ppermute | solution.py:27
  3.7 1.0 %collective-permute-done.core = bf16[32,2176]{1,0:T(8,128)(2,1)S(1)} collective-permute-done((bf16[32,2176]{1,0:T(8,128)(2,1)S(1)}, bf16[32,2176]{1,0:T(8,128)(2,1)S(1)}, u32[]{:S(2)}, u32[]{:S(2)}) %collective-permute-start) | collective-permute-done | bytes 139296 | tf_op jit(solution)/shard_map/ppermute | solution.py:27
  4.8 2.9 %collective-permute-start.1 = (bf16[32,2176]{1,0:T(8,128)(2,1)S(1)}, bf16[32,2176]{1,0:T(8,128)(2,1)S(1)}, u32[]{:S(2)}, u32[]{:S(2)}) collective-permute-start(bf16[32,2176]{1,0:T(8,128)(2,1)S(1)} %add_convert_fusion), channel_id=1, source_target_pairs={{0,2},{1,3},{2,0},{3,1},{4,6},{5,7},{6,4},{7,5},{8,10},{9,11},{10,... | collective-permute-start | bytes 417800 | tf_op jit(solution)/shard_map/ppermute | solution.py:27
  7.7 4.0 %collective-permute-done.1.chip = bf16[32,2176]{1,0:T(8,128)(2,1)S(1)} collective-permute-done((bf16[32,2176]{1,0:T(8,128)(2,1)S(1)}, bf16[32,2176]{1,0:T(8,128)(2,1)S(1)}, u32[]{:S(2)}, u32[]{:S(2)}) %collective-permute-start.1) | collective-permute-done | bytes 139296 | tf_op jit(solution)/shard_map/ppermute | solution.py:27
  11.6 0.1 norm.2
  11.8 2.9 %collective-permute-start.8 = (bf16[16,2176]{1,0:T(8,128)(2,1)S(1)}, bf16[16,2176]{1,0:T(8,128)(2,1)S(1)}, u32[]{:S(2)}, u32[]{:S(2)}) collective-permute-start(bf16[16,2176]{1,0:T(8,128)(2,1)S(1)} %get-tuple-element.18), channel_id=1, source_target_pairs={{0,8},{1,9},{2,10},{3,11},{4,12},{5,13},{6,14},{7,15},{8,0},{9,1},... | collective-permute-start | bytes 208904 | tf_op jit(solution)/shard_map/ppermute | solution.py:27
  14.7 0.1 norm.3
  14.8 1.4 %collective-permute-start.10 = (bf16[32,2176]{1,0:T(8,128)(2,1)S(1)}, bf16[32,2176]{1,0:T(8,128)(2,1)S(1)}, u32[]{:S(2)}, u32[]{:S(2)}) collective-permute-start(bf16[32,2176]{1,0:T(8,128)(2,1)S(1)} %pad_maximum_fusion.1), channel_id=1, source_target_pairs={{0,12},{1,13},{2,14},{3,15},{4,8},{5,9},{6,10},{7,11},{8,4},{9,5},... | collective-permute-start | bytes 417800 | tf_op jit(solution)/shard_map/ppermute | solution.py:27
  16.2 0.3 collective-permute-start.2
  16.6 0.8 %collective-permute-done.8 = bf16[16,2176]{1,0:T(8,128)(2,1)S(1)} collective-permute-done((bf16[16,2176]{1,0:T(8,128)(2,1)S(1)}, bf16[16,2176]{1,0:T(8,128)(2,1)S(1)}, u32[]{:S(2)}, u32[]{:S(2)}) %collective-permute-start.8) | collective-permute-done | bytes 69664 | tf_op jit(solution)/shard_map/ppermute | solution.py:27
  17.4 1.5 %collective-permute-start.9 = (bf16[16,2176]{1,0:T(8,128)(2,1)S(1)}, bf16[16,2176]{1,0:T(8,128)(2,1)S(1)}, u32[]{:S(2)}, u32[]{:S(2)}) collective-permute-start(bf16[16,2176]{1,0:T(8,128)(2,1)S(1)} %collective-permute-done.8), channel_id=1, source_target_pairs={{0,2},{1,3},{2,0},{3,1},{4,6},{5,7},{6,4},{7,5},{8,10},{9,11},{10,... | collective-permute-start | bytes 208904 | tf_op jit(solution)/shard_map/ppermute | solution.py:27
  18.9 2.8 %collective-permute-done.9 = bf16[16,2176]{1,0:T(8,128)(2,1)S(1)} collective-permute-done((bf16[16,2176]{1,0:T(8,128)(2,1)S(1)}, bf16[16,2176]{1,0:T(8,128)(2,1)S(1)}, u32[]{:S(2)}, u32[]{:S(2)}) %collective-permute-start.9) | collective-permute-done | bytes 69664 | tf_op jit(solution)/shard_map/ppermute | solution.py:27
  21.7 1.1 %collective-permute-done.10 = bf16[32,2176]{1,0:T(8,128)(2,1)S(1)} collective-permute-done((bf16[32,2176]{1,0:T(8,128)(2,1)S(1)}, bf16[32,2176]{1,0:T(8,128)(2,1)S(1)}, u32[]{:S(2)}, u32[]{:S(2)}) %collective-permute-start.10) | collective-permute-done | bytes 139296 | tf_op jit(solution)/shard_map/ppermute | solution.py:27
  22.9 0.6 %collective-permute-done.2 = bf16[32,2176]{1,0:T(8,128)(2,1)S(1)} collective-permute-done((bf16[32,2176]{1,0:T(8,128)(2,1)S(1)}, bf16[32,2176]{1,0:T(8,128)(2,1)S(1)}, u32[]{:S(2)}, u32[]{:S(2)}) %collective-permute-start.2) | collective-permute-done | bytes 139296 | tf_op jit(solution)/shard_map/ppermute | solution.py:27
  23.6 0.1 collective-permute-start.3
  23.6 0.8 %collective-permute-done.11.other = bf16[64,2176]{1,0:T(8,128)(2,1)S(1)} collective-permute-done((bf16[64,2176]{1,0:T(8,128)(2,1)S(1)}, bf16[64,2176]{1,0:T(8,128)(2,1)S(1)}, u32[]{:S(2)}, u32[]{:S(2)}) %collective-permute-start.11) | collective-permute-done | bytes 278560 | tf_op jit(solution)/shard_map/ppermute | solution.py:27
  24.5 1.5 %expert.3 = (f32[64,2048]{1,0:T(8,128)S(1)}, bf16[64,2048]{1,0:T(8,128)(2,1)S(1)}) custom-call(bf16[64,2176]{1,0:T(8,128)(2,1)S(1)} %constant_dynamic-update-slice_fusion.mine, bf16[64,2176]{1,0:T(8,128)(2,1)S(1)} %collective-permute-done.11.other, bf16[1,2048,768]{2,1,0:T(8,128)(2,1)S(1)} %copy-done, bf16[1,2048,768]{2,1,0:T(8,128)(2,1)S(1)} %copy-done.1, ...), custom_call_target="tpu_custom_call" | custom-call | flops 1073741824 | bytes 8388608 | tf_op jit(solution)/shard_map/expert/pallas_call | solution.py:216
  26.0 0.2 collective-permute-start.12
  26.2 1.5 %expert.2 = (f32[64,2048]{1,0:T(8,128)S(1)}, bf16[64,2048]{1,0:T(8,128)(2,1)S(1)}) custom-call(bf16[64,2176]{1,0:T(8,128)(2,1)S(1)} %pad_maximum_fusion.mine, bf16[64,2176]{1,0:T(8,128)(2,1)S(1)} %collective-permute-done.3.other, bf16[1,2048,768]{2,1,0:T(8,128)(2,1)S(1)} %copy-done, bf16[1,2048,768]{2,1,0:T(8,128)(2,1)S(1)} %copy-done.1, ...), custom_call_target="tpu_custom_call" | custom-call | flops 1073741824 | bytes 8388608 | tf_op jit(solution)/shard_map/expert/pallas_call | solution.py:216
  27.7 0.4 collective-permute-start.4
  28.2 1.5 %collective-permute-start.13 = (bf16[16,2048]{1,0:T(8,128)(2,1)S(1)}, bf16[16,2048]{1,0:T(8,128)(2,1)S(1)}, u32[]{:S(2)}, u32[]{:S(2)}) collective-permute-start(bf16[16,2048]{1,0:T(8,128)(2,1)S(1)} %get-tuple-element.28), channel_id=1, source_target_pairs={{0,2},{1,3},{2,0},{3,1},{4,6},{5,7},{6,4},{7,5},{8,10},{9,11},{10,... | collective-permute-start | bytes 196616 | tf_op jit(solution)/shard_map/ppermute | solution.py:27
  29.8 0.5 %collective-permute-start.15 = (bf16[16,2048]{1,0:T(8,128)(2,1)S(1)}, bf16[16,2048]{1,0:T(8,128)(2,1)S(1)}, u32[]{:S(2)}, u32[]{:S(2)}) collective-permute-start(bf16[16,2048]{1,0:T(8,128)(2,1)S(1)} %get-tuple-element.29), channel_id=1, source_target_pairs={{0,2},{1,3},{2,0},{3,1},{4,6},{5,7},{6,4},{7,5},{8,10},{9,11},{10,... | collective-permute-start | bytes 196616 | tf_op jit(solution)/shard_map/ppermute | solution.py:27
  30.4 1.5 %collective-permute-start.5 = (bf16[16,2048]{1,0:T(8,128)(2,1)S(1)}, bf16[16,2048]{1,0:T(8,128)(2,1)S(1)}, u32[]{:S(2)}, u32[]{:S(2)}) collective-permute-start(bf16[16,2048]{1,0:T(8,128)(2,1)S(1)} %get-tuple-element.26), channel_id=1, source_target_pairs={{0,2},{1,3},{2,0},{3,1},{4,6},{5,7},{6,4},{7,5},{8,10},{9,11},{10,... | collective-permute-start | bytes 196616 | tf_op jit(solution)/shard_map/ppermute | solution.py:27
  32.0 0.5 %collective-permute-start.6 = (bf16[16,2048]{1,0:T(8,128)(2,1)S(1)}, bf16[16,2048]{1,0:T(8,128)(2,1)S(1)}, u32[]{:S(2)}, u32[]{:S(2)}) collective-permute-start(bf16[16,2048]{1,0:T(8,128)(2,1)S(1)} %get-tuple-element.27), channel_id=1, source_target_pairs={{0,2},{1,3},{2,0},{3,1},{4,6},{5,7},{6,4},{7,5},{8,10},{9,11},{10,... | collective-permute-start | bytes 196616 | tf_op jit(solution)/shard_map/ppermute | solution.py:27
  32.5 0.4 collective-permute-done.13.got
  32.9 3.6 %collective-permute-start.14 = (bf16[16,2048]{1,0:T(8,128)(2,1)S(1)}, bf16[16,2048]{1,0:T(8,128)(2,1)S(1)}, u32[]{:S(2)}, u32[]{:S(2)}) collective-permute-start(bf16[16,2048]{1,0:T(8,128)(2,1)S(1)} %farsum.1), channel_id=1, source_target_pairs={{0,8},{1,9},{2,10},{3,11},{4,12},{5,13},{6,14},{7,15},{8,0},{9,1},... | collective-permute-start | bytes 196616 | tf_op jit(solution)/shard_map/ppermute | solution.py:27
  36.5 4.7 %collective-permute-start.16 = (bf16[16,2048]{1,0:T(8,128)(2,1)S(1)}, bf16[16,2048]{1,0:T(8,128)(2,1)S(1)}, u32[]{:S(2)}, u32[]{:S(2)}) collective-permute-start(bf16[16,2048]{1,0:T(8,128)(2,1)S(1)} %fusion.1), channel_id=1, source_target_pairs={{0,12},{1,13},{2,14},{3,15},{4,8},{5,9},{6,10},{7,11},{8,4},{9,5},... | collective-permute-start | bytes 196616 | tf_op jit(solution)/shard_map/ppermute | solution.py:27
  41.4 0.6 %copy.18 = bf16[16,2048]{1,0:T(8,128)(2,1)} copy(bf16[16,2048]{1,0:T(8,128)(2,1)S(1)} %get-tuple-element.30) | data formatting | bytes 131072
  42.0 1.6 %collective-permute-done.16 = bf16[16,2048]{1,0:T(8,128)(2,1)S(1)} collective-permute-done((bf16[16,2048]{1,0:T(8,128)(2,1)S(1)}, bf16[16,2048]{1,0:T(8,128)(2,1)S(1)}, u32[]{:S(2)}, u32[]{:S(2)}) %collective-permute-start.16) | collective-permute-done | bytes 65568 | tf_op jit(solution)/shard_map/ppermute | solution.py:27
  43.6 2.1 %collective-permute-done.7 = bf16[16,2048]{1,0:T(8,128)(2,1)S(1)} collective-permute-done((bf16[16,2048]{1,0:T(8,128)(2,1)S(1)}, bf16[16,2048]{1,0:T(8,128)(2,1)S(1)}, u32[]{:S(2)}, u32[]{:S(2)}) %collective-permute-start.7) | collective-permute-done | bytes 65568 | tf_op jit(solution)/shard_map/ppermute | solution.py:27
  45.6 0.7 %fusion.8 = bf16[16,2048]{1,0:T(8,128)(2,1)} fusion(f32[2,2,16,2048]{3,2,1,0:T(8,128)S(1)} %bitcast.44, bf16[16,2048]{1,0:T(8,128)(2,1)S(1)} %collective-permute-done.16, bf16[16,2048]{1,0:T(8,128)(2,1)S(1)} %collective-permute-done.14, bf16[16,2048]{1,0:T(8,128)(2,1)S(1)} %collective-permute-done.7, bf16[16,2048]{1,0:T(8,128)(2,1)S(1)} %collective-permute-done.5), kind=kLoop, calls=%fused_computation.16 | loop fusion | flops 294912 | bytes 458752 | tf_op jit(solution)/shard_map/convert_element_type | solution.py:267
  (32 shorter events, 0.5 us)
Async XLA Ops:
  0.6 11.0 %copy-start.3 = (f32[2048]{0:T(1024)S(1)}, f32[2048]{0:T(1024)}, u32[]{:S(2)}) copy-start(f32[2048]{0:T(1024)} %param.22) | copy-start | bytes 24580
  3.2 1.6 %collective-permute-start = (bf16[32,2176]{1,0:T(8,128)(2,1)S(1)}, bf16[32,2176]{1,0:T(8,128)(2,1)S(1)}, u32[]{:S(2)}, u32[]{:S(2)}) collective-permute-start(bf16[32,2176]{1,0:T(8,128)(2,1)S(1)} %get-tuple-element.16), channel_id=1, source_target_pairs={{0,1},{1,0},{2,3},{3,2},{4,5},{5,4},{6,7},{7,6},{8,9},{9,8},{10,11... | collective-permute-start | bytes 417800 | tf_op jit(solution)/shard_map/ppermute | solution.py:27
  4.8 6.9 %collective-permute-start.1 = (bf16[32,2176]{1,0:T(8,128)(2,1)S(1)}, bf16[32,2176]{1,0:T(8,128)(2,1)S(1)}, u32[]{:S(2)}, u32[]{:S(2)}) collective-permute-start(bf16[32,2176]{1,0:T(8,128)(2,1)S(1)} %add_convert_fusion), channel_id=1, source_target_pairs={{0,2},{1,3},{2,0},{3,1},{4,6},{5,7},{6,4},{7,5},{8,10},{9,11},{10,... | collective-permute-start | bytes 417800 | tf_op jit(solution)/shard_map/ppermute | solution.py:27
  11.8 5.6 %collective-permute-start.8 = (bf16[16,2176]{1,0:T(8,128)(2,1)S(1)}, bf16[16,2176]{1,0:T(8,128)(2,1)S(1)}, u32[]{:S(2)}, u32[]{:S(2)}) collective-permute-start(bf16[16,2176]{1,0:T(8,128)(2,1)S(1)} %get-tuple-element.18), channel_id=1, source_target_pairs={{0,8},{1,9},{2,10},{3,11},{4,12},{5,13},{6,14},{7,15},{8,0},{9,1},... | collective-permute-start | bytes 208904 | tf_op jit(solution)/shard_map/ppermute | solution.py:27
  14.7 9.8 %copy-start = (bf16[1,2048,768]{2,1,0:T(8,128)(2,1)S(1)}, bf16[1,2048,768]{2,1,0:T(8,128)(2,1)}, u32[]{:S(2)}) copy-start(bf16[1,2048,768]{2,1,0:T(8,128)(2,1)} %w_gate.1) | copy-start | bytes 9437188
  14.7 9.8 %copy-start.1 = (bf16[1,2048,768]{2,1,0:T(8,128)(2,1)S(1)}, bf16[1,2048,768]{2,1,0:T(8,128)(2,1)}, u32[]{:S(2)}) copy-start(bf16[1,2048,768]{2,1,0:T(8,128)(2,1)} %w_up.1) | copy-start | bytes 9437188
  14.7 9.8 %copy-start.2 = (bf16[1,768,2048]{2,1,0:T(8,128)(2,1)S(1)}, bf16[1,768,2048]{2,1,0:T(8,128)(2,1)}, u32[]{:S(2)}) copy-start(bf16[1,768,2048]{2,1,0:T(8,128)(2,1)} %w_down.1) | copy-start | bytes 9437188
  14.8 8.0 %collective-permute-start.10 = (bf16[32,2176]{1,0:T(8,128)(2,1)S(1)}, bf16[32,2176]{1,0:T(8,128)(2,1)S(1)}, u32[]{:S(2)}, u32[]{:S(2)}) collective-permute-start(bf16[32,2176]{1,0:T(8,128)(2,1)S(1)} %pad_maximum_fusion.1), channel_id=1, source_target_pairs={{0,12},{1,13},{2,14},{3,15},{4,8},{5,9},{6,10},{7,11},{8,4},{9,5},... | collective-permute-start | bytes 417800 | tf_op jit(solution)/shard_map/ppermute | solution.py:27
  16.2 7.3 %collective-permute-start.2 = (bf16[32,2176]{1,0:T(8,128)(2,1)S(1)}, bf16[32,2176]{1,0:T(8,128)(2,1)S(1)}, u32[]{:S(2)}, u32[]{:S(2)}) collective-permute-start(bf16[32,2176]{1,0:T(8,128)(2,1)S(1)} %pad_maximum_fusion.1), channel_id=1, source_target_pairs={{0,4},{1,5},{2,6},{3,7},{4,0},{5,1},{6,2},{7,3},{8,12},{9,13},{10,... | collective-permute-start | bytes 417800 | tf_op jit(solution)/shard_map/ppermute | solution.py:27
  17.4 4.3 %collective-permute-start.9 = (bf16[16,2176]{1,0:T(8,128)(2,1)S(1)}, bf16[16,2176]{1,0:T(8,128)(2,1)S(1)}, u32[]{:S(2)}, u32[]{:S(2)}) collective-permute-start(bf16[16,2176]{1,0:T(8,128)(2,1)S(1)} %collective-permute-done.8), channel_id=1, source_target_pairs={{0,2},{1,3},{2,0},{3,1},{4,6},{5,7},{6,4},{7,5},{8,10},{9,11},{10,... | collective-permute-start | bytes 208904 | tf_op jit(solution)/shard_map/ppermute | solution.py:27
  22.9 1.6 %collective-permute-start.11 = (bf16[64,2176]{1,0:T(8,128)(2,1)S(1)}, bf16[64,2176]{1,0:T(8,128)(2,1)S(1)}, u32[]{:S(2)}, u32[]{:S(2)}) collective-permute-start(bf16[64,2176]{1,0:T(8,128)(2,1)S(1)} %constant_dynamic-update-slice_fusion.mine), channel_id=1, source_target_pairs={{0,1},{1,0},{2,3},{3,2},{4,5},{5,4},{6,7},{7,6},{8,9},{9,8},{10,11... | collective-permute-start | bytes 835592 | tf_op jit(solution)/shard_map/ppermute | solution.py:27
  23.6 2.6 %collective-permute-start.3 = (bf16[64,2176]{1,0:T(8,128)(2,1)S(1)}, bf16[64,2176]{1,0:T(8,128)(2,1)S(1)}, u32[]{:S(2)}, u32[]{:S(2)}) collective-permute-start(bf16[64,2176]{1,0:T(8,128)(2,1)S(1)} %pad_maximum_fusion.mine), channel_id=1, source_target_pairs={{0,1},{1,0},{2,3},{3,2},{4,5},{5,4},{6,7},{7,6},{8,9},{9,8},{10,11... | collective-permute-start | bytes 835592 | tf_op jit(solution)/shard_map/ppermute | solution.py:27
  26.0 2.1 %collective-permute-start.12 = (bf16[64,2048]{1,0:T(8,128)(2,1)S(1)}, bf16[64,2048]{1,0:T(8,128)(2,1)S(1)}, u32[]{:S(2)}, u32[]{:S(2)}) collective-permute-start(bf16[64,2048]{1,0:T(8,128)(2,1)S(1)} %get-tuple-element.25), channel_id=1, source_target_pairs={{0,1},{1,0},{2,3},{3,2},{4,5},{5,4},{6,7},{7,6},{8,9},{9,8},{10,11... | collective-permute-start | bytes 786440 | tf_op jit(solution)/shard_map/ppermute | solution.py:27
  27.7 2.7 %collective-permute-start.4 = (bf16[64,2048]{1,0:T(8,128)(2,1)S(1)}, bf16[64,2048]{1,0:T(8,128)(2,1)S(1)}, u32[]{:S(2)}, u32[]{:S(2)}) collective-permute-start(bf16[64,2048]{1,0:T(8,128)(2,1)S(1)} %get-tuple-element.23), channel_id=1, source_target_pairs={{0,1},{1,0},{2,3},{3,2},{4,5},{5,4},{6,7},{7,6},{8,9},{9,8},{10,11... | collective-permute-start | bytes 786440 | tf_op jit(solution)/shard_map/ppermute | solution.py:27
  28.2 4.7 %collective-permute-start.13 = (bf16[16,2048]{1,0:T(8,128)(2,1)S(1)}, bf16[16,2048]{1,0:T(8,128)(2,1)S(1)}, u32[]{:S(2)}, u32[]{:S(2)}) collective-permute-start(bf16[16,2048]{1,0:T(8,128)(2,1)S(1)} %get-tuple-element.28), channel_id=1, source_target_pairs={{0,2},{1,3},{2,0},{3,1},{4,6},{5,7},{6,4},{7,5},{8,10},{9,11},{10,... | collective-permute-start | bytes 196616 | tf_op jit(solution)/shard_map/ppermute | solution.py:27
  29.8 6.7 %collective-permute-start.15 = (bf16[16,2048]{1,0:T(8,128)(2,1)S(1)}, bf16[16,2048]{1,0:T(8,128)(2,1)S(1)}, u32[]{:S(2)}, u32[]{:S(2)}) collective-permute-start(bf16[16,2048]{1,0:T(8,128)(2,1)S(1)} %get-tuple-element.29), channel_id=1, source_target_pairs={{0,2},{1,3},{2,0},{3,1},{4,6},{5,7},{6,4},{7,5},{8,10},{9,11},{10,... | collective-permute-start | bytes 196616 | tf_op jit(solution)/shard_map/ppermute | solution.py:27
  30.4 11.6 %collective-permute-start.5 = (bf16[16,2048]{1,0:T(8,128)(2,1)S(1)}, bf16[16,2048]{1,0:T(8,128)(2,1)S(1)}, u32[]{:S(2)}, u32[]{:S(2)}) collective-permute-start(bf16[16,2048]{1,0:T(8,128)(2,1)S(1)} %get-tuple-element.26), channel_id=1, source_target_pairs={{0,2},{1,3},{2,0},{3,1},{4,6},{5,7},{6,4},{7,5},{8,10},{9,11},{10,... | collective-permute-start | bytes 196616 | tf_op jit(solution)/shard_map/ppermute | solution.py:27
  32.0 9.3 %collective-permute-start.6 = (bf16[16,2048]{1,0:T(8,128)(2,1)S(1)}, bf16[16,2048]{1,0:T(8,128)(2,1)S(1)}, u32[]{:S(2)}, u32[]{:S(2)}) collective-permute-start(bf16[16,2048]{1,0:T(8,128)(2,1)S(1)} %get-tuple-element.27), channel_id=1, source_target_pairs={{0,2},{1,3},{2,0},{3,1},{4,6},{5,7},{6,4},{7,5},{8,10},{9,11},{10,... | collective-permute-start | bytes 196616 | tf_op jit(solution)/shard_map/ppermute | solution.py:27
  32.9 9.1 %collective-permute-start.14 = (bf16[16,2048]{1,0:T(8,128)(2,1)S(1)}, bf16[16,2048]{1,0:T(8,128)(2,1)S(1)}, u32[]{:S(2)}, u32[]{:S(2)}) collective-permute-start(bf16[16,2048]{1,0:T(8,128)(2,1)S(1)} %farsum.1), channel_id=1, source_target_pairs={{0,8},{1,9},{2,10},{3,11},{4,12},{5,13},{6,14},{7,15},{8,0},{9,1},... | collective-permute-start | bytes 196616 | tf_op jit(solution)/shard_map/ppermute | solution.py:27
  36.5 7.0 %collective-permute-start.16 = (bf16[16,2048]{1,0:T(8,128)(2,1)S(1)}, bf16[16,2048]{1,0:T(8,128)(2,1)S(1)}, u32[]{:S(2)}, u32[]{:S(2)}) collective-permute-start(bf16[16,2048]{1,0:T(8,128)(2,1)S(1)} %fusion.1), channel_id=1, source_target_pairs={{0,12},{1,13},{2,14},{3,15},{4,8},{5,9},{6,10},{7,11},{8,4},{9,5},... | collective-permute-start | bytes 196616 | tf_op jit(solution)/shard_map/ppermute | solution.py:27
  41.3 4.3 %collective-permute-start.7 = (bf16[16,2048]{1,0:T(8,128)(2,1)S(1)}, bf16[16,2048]{1,0:T(8,128)(2,1)S(1)}, u32[]{:S(2)}, u32[]{:S(2)}) collective-permute-start(bf16[16,2048]{1,0:T(8,128)(2,1)S(1)} %fusion.3), channel_id=1, source_target_pairs={{0,4},{1,5},{2,6},{3,7},{4,0},{5,1},{6,2},{7,3},{8,12},{9,13},{10,... | collective-permute-start | bytes 196616 | tf_op jit(solution)/shard_map/ppermute | solution.py:27
